TPU v7x, 32 devices: a whole 2x2x4 slice. The times are simulated.
32 devices in a mesh: dp: 8 (over y, x, core), mp: 4 (over z).
Axes of the slice: x: 2, y: 2, z: 4, core: 2. Of those that a mesh axis runs over, the one named last changes fastest.
Arguments:
- layer_in: bfloat16 [8192, 2048], P(('dp', 'mp')), may hold values from -6 to 6
- first_gain: bfloat16 [2048], replicated, may hold values from 0.5 to 1.5
- first_bias: bfloat16 [2048], replicated, may hold values from -1.75 to 1.75
- w_qkv: bfloat16 [2048, 3, 2048], P(None, None, 'mp'), may hold values from -0.125 to 0.125
- a_qkv: bfloat16 [2048, 8, 16], replicated, may hold values from -0.125 to 0.125
- b_qkv: bfloat16 [8, 16, 3, 2048], P(None, None, None, 'mp'), may hold values from -1.5 to 1.5
- w_dense: bfloat16 [2048, 2048], P('mp'), may hold values from -0.375 to 0.375
- a_dense: bfloat16 [2048, 8, 16], P('mp'), may hold values from -0.375 to 0.375
- b_dense: bfloat16 [8, 16, 2048], replicated, may hold values from -1.5 to 1.5
- second_gain: bfloat16 [2048], replicated, may hold values from 0.5 to 1.5
- second_bias: bfloat16 [2048], replicated, may hold values from -1.75 to 1.75
- w_up: bfloat16 [2048, 8192], P(None, 'mp'), may hold values from -0.125 to 0.125
- a_up: bfloat16 [2048, 8, 16], replicated, may hold values from -0.125 to 0.125
- b_up: bfloat16 [8, 16, 8192], P(None, None, 'mp'), may hold values from -1.5 to 1.5
- w_down: bfloat16 [8192, 2048], P('mp'), may hold values from -0.0625 to 0.0625
- a_down: bfloat16 [8192, 8, 16], P('mp'), may hold values from -0.0625 to 0.0625
- b_down: bfloat16 [8, 16, 2048], replicated, may hold values from -1.5 to 1.5
- segment_ids: int32 [8, 1024], P('dp'), may hold values from 0 to 7, never falling along the last dimension, each value on 1 to 512 neighbouring positions
- adapter_ids: int32 [8], P('dp'), may hold values from 0 to 7, as said below
- cotangent: bfloat16 [8192, 2048], P(('dp', 'mp')), may hold values from -6 to 6
Outputs:
- layer_out: bfloat16 [8192, 2048], P(('dp', 'mp'))
- input_grad: bfloat16 [8192, 2048], P(('dp', 'mp'))
- grad_a_qkv: float32 [2048, 8, 16], replicated
- grad_b_qkv: float32 [8, 16, 3, 2048], P(None, None, None, 'mp')
- grad_a_dense: float32 [2048, 8, 16], P('mp')
- grad_b_dense: float32 [8, 16, 2048], replicated
- grad_a_up: float32 [2048, 8, 16], replicated
- grad_b_up: float32 [8, 16, 8192], P(None, None, 'mp')
- grad_a_down: float32 [8192, 8, 16], P('mp')
- grad_b_down: float32 [8, 16, 2048], replicated
Inputs may be any that keep to these rules, and one draw needn't show every extreme that they name: `adapter_ids`: every one of the 8 adapters is used by at least one sequence.
All inputs are finite; a program needn't handle non-finite values.
Results may differ from a plain program's by a relative error of at most 0.023.
Values may be sent and summed in bfloat16 or wider, within the bound.
No kernel may reach another device: no remote copies, remote signals or barrier semaphores. Data moves between devices by JAX's collectives and lax.ppermute only.
A program may use at most 256 MiB of HBM per device.

v0:
```python
import jax
import jax.numpy as jnp
from jax import lax
from jax.sharding import PartitionSpec as P

HEADS = 32
HD = 64


EPSILON = 1e-05


def layer_norm(values, gain, bias):
    center = jnp.mean(values, -1, keepdims=True)
    centred = values - center
    variance = jnp.mean(centred * centred, -1, keepdims=True)
    scaler = lax.rsqrt(variance + EPSILON)
    normal = centred * scaler
    return (normal * gain.astype(jnp.float32) + bias.astype(jnp.float32), normal, scaler)


def norm_back(grad, normal, scaler, gain):
    scaled = grad * gain.astype(jnp.float32)
    first_mean = jnp.mean(scaled, -1, keepdims=True)
    second_mean = jnp.mean(scaled * normal, -1, keepdims=True)
    return (scaled - first_mean - normal * second_mean) * scaler


def exact_gelu(values):
    return jax.nn.gelu(values, approximate=False)


def adapter_table(adapter_ids, first_row, count, seq_len, kinds):
    rows = first_row + lax.iota(jnp.int32, count)
    seq_of = rows // seq_len
    picks = seq_of[:, None] == lax.iota(jnp.int32, adapter_ids.shape[0])[None, :]
    chosen = jnp.sum(jnp.where(picks, adapter_ids[None, :], 0), 1)
    return (chosen[:, None] == lax.iota(jnp.int32, kinds)[None, :]).astype(jnp.bfloat16)


def select_rows(full, table):
    count, kinds = table.shape
    shaped = full.reshape(count, kinds, full.shape[1] // kinds)
    return jnp.sum(shaped * table.astype(jnp.float32)[:, :, None], 1)


def expand_rows(inner, table):
    count, kinds = table.shape
    return (table[:, :, None] * inner[:, None, :]).reshape(count, kinds * inner.shape[1])


def plain_dot(left, right):
    return jnp.dot(left, right, preferred_element_type=jnp.float32)


def transpose_dot(left, right):
    return lax.dot_general(
        left, right, (((1,), (1,)), ((), ())), preferred_element_type=jnp.float32
    )


def weight_grad(left, right):
    return lax.dot_general(
        left, right, (((0,), (0,)), ((), ())), preferred_element_type=jnp.float32
    )


def masked_scores(query_block, key_part, seg_row, start, stop, slopes):
    block = query_block.shape[0]
    raw = jnp.einsum(
        "qhd,khd->hqk", query_block, key_part, preferred_element_type=jnp.float32
    ) * query_block.shape[2] ** (-0.5)
    query_pos = start + lax.iota(jnp.int32, block)
    key_pos = lax.iota(jnp.int32, stop)
    offsets = (key_pos[None, :] - query_pos[:, None]).astype(jnp.float32)
    raw = raw + slopes[:, None, None] * offsets[None]
    allowed = (key_pos[None, :] <= query_pos[:, None]) & (
        seg_row[:stop][None, :] == seg_row[start:stop][:, None]
    )
    return jnp.where(allowed[None], raw, -1e30)


def attention_forward(query_rows, key_rows, val_rows, segment_ids, slopes):
    seq_count, seq_len = segment_ids.shape
    block = min(512, seq_len)
    outputs = []
    log_sums = []
    seg_row = segment_ids[0]
    for block_idx in range(seq_len // block):
        start = block_idx * block
        stop = start + block
        scores = masked_scores(
            query_rows[start:stop], key_rows[0:stop], seg_row, start, stop, slopes
        )
        top = jnp.max(scores, -1, keepdims=True)
        expo = jnp.exp(scores - top)
        total = jnp.sum(expo, -1, keepdims=True)
        weights = (expo / total).astype(jnp.bfloat16)
        result = jnp.einsum(
            "hqk,khd->qhd", weights, val_rows[0:stop], preferred_element_type=jnp.float32
        )
        outputs.append(result.reshape(block, -1).astype(jnp.bfloat16))
        log_sums.append(top + jnp.log(total))
    return (jnp.concatenate(outputs, 0), log_sums)


def attention_backward(query_rows, key_rows, val_rows, d_mixed, log_sums, segment_ids, slopes):
    seq_count, seq_len = segment_ids.shape
    all_rows, local_heads, head_dim = query_rows.shape
    block = min(512, seq_len)
    scale = head_dim ** (-0.5)
    d_out = d_mixed.reshape(all_rows, local_heads, head_dim)
    query_grads = []
    counter = 0
    seg_row = segment_ids[0]
    key_grad = jnp.zeros((seq_len, local_heads, head_dim), jnp.float32)
    val_grad = jnp.zeros((seq_len, local_heads, head_dim), jnp.float32)
    for block_idx in range(seq_len // block):
        start = block_idx * block
        stop = start + block
        query_block = query_rows[start:stop]
        key_part = key_rows[0:stop]
        val_part = val_rows[0:stop]
        grad_block = d_out[start:stop]
        scores = masked_scores(query_block, key_part, seg_row, start, stop, slopes)
        weights = jnp.exp(scores - log_sums[counter])
        counter += 1
        val_grad = val_grad.at[:stop].add(
            jnp.einsum(
                "hqk,qhd->khd",
                weights.astype(jnp.bfloat16),
                grad_block,
                preferred_element_type=jnp.float32,
            )
        )
        d_prob = jnp.einsum(
            "qhd,khd->hqk", grad_block, val_part, preferred_element_type=jnp.float32
        )
        center = jnp.sum(weights * d_prob, -1, keepdims=True)
        d_scores = (weights * (d_prob - center)).astype(jnp.bfloat16)
        query_grad = (
            jnp.einsum("hqk,khd->qhd", d_scores, key_part, preferred_element_type=jnp.float32)
            * scale
        )
        query_grads.append(query_grad.astype(jnp.bfloat16))
        key_grad = key_grad.at[:stop].add(
            jnp.einsum("hqk,qhd->khd", d_scores, query_block, preferred_element_type=jnp.float32)
            * scale
        )
    key_grads = key_grad.astype(jnp.bfloat16)
    val_grads = val_grad.astype(jnp.bfloat16)
    local_width = local_heads * head_dim
    query_all = jnp.concatenate(query_grads, 0).reshape(all_rows, local_width)
    key_all = key_grads.reshape(all_rows, local_width)
    val_all = val_grads.reshape(all_rows, local_width)
    return jnp.concatenate([query_all, key_all, val_all], 1)


def local(
    layer_in,
    first_gain,
    first_bias,
    w_qkv,
    a_qkv,
    b_qkv,
    w_dense,
    a_dense,
    b_dense,
    second_gain,
    second_bias,
    w_up,
    a_up,
    b_up,
    w_down,
    a_down,
    b_down,
    segment_ids,
    adapter_ids,
    cotangent,
):
    local_rows, width = layer_in.shape
    all_rows = local_rows * lax.axis_size("mp")
    seq_len = segment_ids.shape[1]
    first_row = lax.axis_index("mp") * local_rows
    kinds = a_qkv.shape[1]
    inner_width = kinds * a_qkv.shape[2]
    local_width = w_dense.shape[0]
    local_ff = w_up.shape[1]
    local_heads = local_width // HD
    table_all = adapter_table(adapter_ids, 0, all_rows, seq_len, kinds)
    table_own = adapter_table(adapter_ids, first_row, local_rows, seq_len, kinds)
    head_ids = (lax.axis_index("mp") * local_heads + lax.iota(jnp.int32, local_heads)).astype(
        jnp.float32
    )
    slopes = jnp.exp2(-8.0 * (head_ids + 1.0) / HEADS)
    normed_own, normal_one, scaler_one = layer_norm(
        layer_in.astype(jnp.float32), first_gain, first_bias
    )
    normed_low = normed_own.astype(jnp.bfloat16)
    normed_all = lax.all_gather(normed_low, "mp", axis=0, tiled=True)
    z_qkv = select_rows(plain_dot(normed_all, a_qkv.reshape(width, inner_width)), table_all).astype(
        jnp.bfloat16
    )
    merged = plain_dot(normed_all, w_qkv.reshape(width, 3 * local_width))
    merged = merged + plain_dot(
        expand_rows(z_qkv, table_all), b_qkv.reshape(inner_width, 3 * local_width)
    )
    merged = merged.astype(jnp.bfloat16)
    query_rows = merged[:, :local_width].reshape(all_rows, local_heads, HD)
    key_rows = merged[:, local_width : 2 * local_width].reshape(all_rows, local_heads, HD)
    val_rows = merged[:, 2 * local_width :].reshape(all_rows, local_heads, HD)
    mixed, log_sums = attention_forward(query_rows, key_rows, val_rows, segment_ids, slopes)
    dense_part = plain_dot(mixed, w_dense)
    z_dense_part = select_rows(
        plain_dot(mixed, a_dense.reshape(local_width, inner_width)), table_all
    )
    branch_own, z_dense_own = (
        lax.psum_scatter(
            dense_part.astype(jnp.bfloat16), "mp", scatter_dimension=0, tiled=True
        ).astype(jnp.float32),
        lax.psum_scatter(
            z_dense_part.astype(jnp.bfloat16), "mp", scatter_dimension=0, tiled=True
        ).astype(jnp.float32),
    )
    z_dense = z_dense_own.astype(jnp.bfloat16)
    branch_own = branch_own + plain_dot(
        expand_rows(z_dense, table_own), b_dense.reshape(inner_width, width)
    )
    middle = layer_in.astype(jnp.float32) + branch_own
    normed_two, normal_two, scaler_two = layer_norm(middle, second_gain, second_bias)
    second_low = normed_two.astype(jnp.bfloat16)
    second_all = lax.all_gather(second_low, "mp", axis=0, tiled=True)
    z_up = select_rows(plain_dot(second_all, a_up.reshape(width, inner_width)), table_all).astype(
        jnp.bfloat16
    )
    hidden = plain_dot(second_all, w_up) + plain_dot(
        expand_rows(z_up, table_all), b_up.reshape(inner_width, local_ff)
    )
    active = exact_gelu(hidden).astype(jnp.bfloat16)
    down_part = plain_dot(active, w_down)
    z_down_part = select_rows(plain_dot(active, a_down.reshape(local_ff, inner_width)), table_all)
    mlp_own, z_down_own = (
        lax.psum_scatter(
            down_part.astype(jnp.bfloat16), "mp", scatter_dimension=0, tiled=True
        ).astype(jnp.float32),
        lax.psum_scatter(
            z_down_part.astype(jnp.bfloat16), "mp", scatter_dimension=0, tiled=True
        ).astype(jnp.float32),
    )
    z_down = z_down_own.astype(jnp.bfloat16)
    layer_out = (
        middle
        + mlp_own
        + plain_dot(expand_rows(z_down, table_own), b_down.reshape(inner_width, width))
    ).astype(jnp.bfloat16)
    cot_all = lax.all_gather(cotangent, "mp", axis=0, tiled=True)
    dz_down = select_rows(
        transpose_dot(cot_all, b_down.reshape(inner_width, width)), table_all
    ).astype(jnp.bfloat16)
    grad_a_down = weight_grad(active, expand_rows(dz_down, table_all)).reshape(local_ff, kinds, -1)
    grad_b_down = weight_grad(expand_rows(z_down, table_own), cotangent).reshape(kinds, -1, width)
    d_active = transpose_dot(cot_all, w_down) + transpose_dot(
        expand_rows(dz_down, table_all), a_down.reshape(local_ff, inner_width)
    )
    unused, gelu_back = jax.vjp(exact_gelu, hidden)
    d_hidden = gelu_back(d_active)[0].astype(jnp.bfloat16)
    grad_b_up = weight_grad(expand_rows(z_up, table_all), d_hidden).reshape(kinds, -1, local_ff)
    dz_up_part = select_rows(
        transpose_dot(d_hidden, b_up.reshape(inner_width, local_ff)), table_all
    )
    d_second_part = transpose_dot(d_hidden, w_up)
    d_second, dz_up_own = (
        lax.psum_scatter(
            d_second_part.astype(jnp.bfloat16), "mp", scatter_dimension=0, tiled=True
        ).astype(jnp.float32),
        lax.psum_scatter(
            dz_up_part.astype(jnp.bfloat16), "mp", scatter_dimension=0, tiled=True
        ).astype(jnp.float32),
    )
    dz_up = dz_up_own.astype(jnp.bfloat16)
    d_second = d_second + transpose_dot(
        expand_rows(dz_up, table_own), a_up.reshape(width, inner_width)
    )
    grad_a_up = weight_grad(second_low, expand_rows(dz_up, table_own)).reshape(width, kinds, -1)
    d_middle = cotangent.astype(jnp.float32) + norm_back(
        d_second, normal_two, scaler_two, second_gain
    )
    middle_low = d_middle.astype(jnp.bfloat16)
    grad_b_dense = weight_grad(expand_rows(z_dense, table_own), middle_low).reshape(
        kinds, -1, width
    )
    middle_all = lax.all_gather(middle_low, "mp", axis=0, tiled=True)
    dz_dense = select_rows(
        transpose_dot(middle_all, b_dense.reshape(inner_width, width)), table_all
    ).astype(jnp.bfloat16)
    grad_a_dense = weight_grad(mixed, expand_rows(dz_dense, table_all)).reshape(
        local_width, kinds, -1
    )
    d_mixed = transpose_dot(middle_all, w_dense) + transpose_dot(
        expand_rows(dz_dense, table_all), a_dense.reshape(local_width, inner_width)
    )
    d_mixed = d_mixed.astype(jnp.bfloat16)
    d_merged = attention_backward(
        query_rows, key_rows, val_rows, d_mixed, log_sums, segment_ids, slopes
    )
    grad_b_qkv = weight_grad(expand_rows(z_qkv, table_all), d_merged).reshape(
        kinds, -1, 3, local_width
    )
    dz_qkv_part = select_rows(
        transpose_dot(d_merged, b_qkv.reshape(inner_width, 3 * local_width)), table_all
    )
    d_first_part = transpose_dot(d_merged, w_qkv.reshape(width, 3 * local_width))
    d_first, dz_qkv_own = (
        lax.psum_scatter(
            d_first_part.astype(jnp.bfloat16), "mp", scatter_dimension=0, tiled=True
        ).astype(jnp.float32),
        lax.psum_scatter(
            dz_qkv_part.astype(jnp.bfloat16), "mp", scatter_dimension=0, tiled=True
        ).astype(jnp.float32),
    )
    dz_qkv = dz_qkv_own.astype(jnp.bfloat16)
    d_first = d_first + transpose_dot(
        expand_rows(dz_qkv, table_own), a_qkv.reshape(width, inner_width)
    )
    grad_a_qkv = weight_grad(normed_low, expand_rows(dz_qkv, table_own)).reshape(width, kinds, -1)
    input_grad = (d_middle + norm_back(d_first, normal_one, scaler_one, first_gain)).astype(
        jnp.bfloat16
    )
    grad_a_qkv, grad_b_dense, grad_a_up, grad_b_down = lax.psum(
        (grad_a_qkv, grad_b_dense, grad_a_up, grad_b_down), ("dp", "mp")
    )
    grad_b_qkv, grad_a_dense, grad_b_up, grad_a_down = (
        lax.psum(grad_b_qkv.astype(jnp.bfloat16), "dp").astype(jnp.float32),
        lax.psum(grad_a_dense.astype(jnp.bfloat16), "dp").astype(jnp.float32),
        lax.psum(grad_b_up.astype(jnp.bfloat16), "dp").astype(jnp.float32),
        lax.psum(grad_a_down.astype(jnp.bfloat16), "dp").astype(jnp.float32),
    )
    return (
        layer_out,
        input_grad,
        grad_a_qkv,
        grad_b_qkv,
        grad_a_dense,
        grad_b_dense,
        grad_a_up,
        grad_b_up,
        grad_a_down,
        grad_b_down,
    )


def solution(mesh):
    return jax.shard_map(
        local,
        mesh=mesh,
        in_specs=(
            P(("dp", "mp"), None),
            P(),
            P(),
            P(None, None, "mp"),
            P(),
            P(None, None, None, "mp"),
            P("mp", None),
            P("mp", None, None),
            P(),
            P(),
            P(),
            P(None, "mp"),
            P(),
            P(None, None, "mp"),
            P("mp", None),
            P("mp", None, None),
            P(),
            P("dp", None),
            P("dp"),
            P(("dp", "mp"), None),
        ),
        out_specs=(
            P(("dp", "mp"), None),
            P(("dp", "mp"), None),
            P(),
            P(None, None, None, "mp"),
            P("mp", None, None),
            P(),
            P(),
            P(None, None, "mp"),
            P("mp", None, None),
            P(),
        ),
        check_vma=False,
    )
```

profile of v0, /device:TPU:0, one launch (start us, length us, event | category | flops | bytes accessed | tf_op | source)
XLA Modules:
  0.0 1125.3 jit_solution(3981982386379361301)
XLA Ops:
  16.8 9.0 copy.52
  30.0 68.2 %all-gather.5.cloned.1.call-done = bf16[1024,2048]{1,0:T(8,128)(2,1)} async-done(((bf16[256,2048]{1,0:T(8,128)(2,1)}), bf16[1024,2048]{1,0:T(8,128)(2,1)}) %all-gather.5.cloned.1.call-update) | async-done | bytes 4194320 | tf_op jit(solution)/shard_map/all_gather | solution.py:200
  102.1 8.8 fusion.195
  136.9 6.5 fusion.192
  156.3 5.6 convolution_convert_fusion.3
  162.6 11.2 reduce-scatter.11.cloned.1.call-done
  173.8 77.3 %reduce-scatter.9.cloned.1.call-done = bf16[256,2048]{1,0:T(8,128)(2,1)} async-done(((bf16[1024,2048]{1,0:T(8,128)(2,1)}), bf16[256,2048]{1,0:T(8,128)(2,1)}) %reduce-scatter.9.cloned.1.call-update) | async-done | bytes 1048592 | tf_op jit(solution)/shard_map/reduce_scatter | solution.py:218
  256.1 77.8 %all-gather.9.cloned.1.call-done = bf16[1024,2048]{1,0:T(8,128)(2,1)} async-done(((bf16[256,2048]{1,0:T(8,128)(2,1)}), bf16[1024,2048]{1,0:T(8,128)(2,1)}) %all-gather.9.cloned.1.call-update) | async-done | bytes 4194320 | tf_op jit(solution)/shard_map/all_gather | solution.py:256
  337.8 13.8 %fusion.197 = f32[1024,2048]{1,0:T(8,128)} fusion(bf16[1024,2048]{1,0:T(8,128)(2,1)S(1)} %copy-done.63, bf16[2048,2048]{1,0:T(8,128)(2,1)} %param.46), kind=kOutput, calls=%fused_computation.247 | convolution fusion | flops 8589934592 | bytes 20971520 | tf_op jit(solution)/shard_map/dot_general | solution.py:57
  351.5 63.6 %all-gather.7.cloned.1.call-done = bf16[1024,2048]{1,0:T(8,128)(2,1)} async-done(((bf16[256,2048]{1,0:T(8,128)(2,1)}), bf16[1024,2048]{1,0:T(8,128)(2,1)}) %all-gather.7.cloned.1.call-update) | async-done | bytes 4194320 | tf_op jit(solution)/shard_map/all_gather | solution.py:232
  419.1 11.4 %fusion.196 = f32[1024,2048]{1,0:T(8,128)S(1)} fusion(bf16[1024,2048]{1,0:T(8,128)(2,1)S(1)} %copy-done.66, bf16[2048,2048]{1,0:T(8,128)(2,1)} %param.43), kind=kOutput, calls=%fused_computation.246 | convolution fusion | flops 8589934592 | bytes 20971520 | tf_op jit(solution)/shard_map/dot_general | solution.py:53
  430.5 21.1 %multiply_convert_fusion.2 = (bf16[1024,2048]{1,0:T(8,128)(2,1)}, f32[1024,2048]{1,0:T(8,128)}, f32[1024,2048]{1,0:T(8,128)}) fusion(f32[1024,2048]{1,0:T(8,128)S(1)} %fusion.196, bf16[8,16,2048]{2,1,0:T(8,128)(2,1)S(1)} %copy-done.67, bf16[1024,16]{0,1:T(8,128)(2,1)S(1)} %fusion.114, bf16[1024,8]{0,1:T(8,128)(2,1)S(1)} %get-tuple-element.100), kind=kOutput, calls=%fused_computation.18 | convolution fusion | flops 675414016 | bytes 29933568 | tf_op jit(solution)/shard_map/dot_general | solution.py:53
  451.7 8.2 add_convert_fusion
  464.3 13.9 %convolution_convert_fusion.1 = bf16[1024,2048]{1,0:T(8,128)(2,1)} fusion(bf16[1024,2048]{1,0:T(8,128)(2,1)} %copy-done.10, bf16[2048,2048]{1,0:T(8,128)(2,1)} %param.43), kind=kOutput, calls=%fused_computation.59 | convolution fusion | flops 8592031744 | bytes 16777216 | tf_op jit(solution)/shard_map/dot_general | solution.py:57
  481.8 77.3 %reduce-scatter.17.cloned.1.call-done = bf16[256,2048]{1,0:T(8,128)(2,1)} async-done(((bf16[1024,2048]{1,0:T(8,128)(2,1)}), bf16[256,2048]{1,0:T(8,128)(2,1)}) %reduce-scatter.17.cloned.1.call-update) | async-done | bytes 1048592 | tf_op jit(solution)/shard_map/reduce_scatter | solution.py:273
  568.5 4.5 fusion.111
  573.3 73.6 %all-gather.11.cloned.1.call-done = bf16[1024,2048]{1,0:T(8,128)(2,1)} async-done(((bf16[256,2048]{1,0:T(8,128)(2,1)}), bf16[1024,2048]{1,0:T(8,128)(2,1)}) %all-gather.11.cloned.1.call-update) | async-done | bytes 4194320 | tf_op jit(solution)/shard_map/all_gather | solution.py:292
  653.8 6.1 fusion.68
  660.0 5.1 multiply_reduce_fusion.1
  665.1 6.2 multiply_convert_fusion.1
  671.4 4.6 fusion.76
  676.0 4.5 fusion.71
  680.5 10.0 multiply_reduce_fusion
  690.5 4.9 fusion.62
  697.7 11.8 %multiply_convert_fusion = bf16[8,512,1024]{2,1,0:T(8,128)(2,1)S(1)} fusion(f32[8,512,1024]{2,1,0:T(8,128)} %get-tuple-element.113, f32[8,512,1024]{2,1,0:T(8,128)} %copy-done.1, f32[8,512]{1,0:T(8,128)} %get-tuple-element.112, f32[8,512]{1,0:T(8,128)} %log_add_fusion), kind=kLoop, calls=%fused_computation | loop fusion | flops 16777216 | bytes 41975808 | tf_op jit(solution)/shard_map/convert_element_type | solution.py:140
  722.3 14.3 %convolution_convert_fusion.2 = bf16[1024,2048]{1,0:T(8,128)(2,1)} fusion(bf16[1024,2048]{1,0:T(8,128)(2,1)} %get-tuple-element.88, bf16[2048,2048]{1,0:T(8,128)(2,1)} %param.46), kind=kOutput, calls=%fused_computation.60 | convolution fusion | flops 8592031744 | bytes 16777216 | tf_op jit(solution)/shard_map/dot_general | solution.py:53
  746.1 4.9 copy.70
  757.1 11.4 %convolution_convert_fusion = bf16[1024,2048]{1,0:T(8,128)(2,1)} fusion(bf16[2048,1536]{0,1:T(8,128)(2,1)} %bitcast.299, bf16[1024,512]{1,0:T(8,128)(2,1)S(1)} %copy-done.15, bf16[1024,512]{1,0:T(8,128)(2,1)} %copy.67, bf16[1024,512]{1,0:T(8,128)(2,1)} %copy.66), kind=kOutput, calls=%fused_computation.58 | convolution fusion | flops 6453985280 | bytes 13631488 | tf_op jit(solution)/shard_map/dot_general | solution.py:57
  778.5 38.6 %reduce-scatter.13.cloned.1.call-done = bf16[256,2048]{1,0:T(8,128)(2,1)} async-done(((bf16[1024,2048]{1,0:T(8,128)(2,1)}), bf16[256,2048]{1,0:T(8,128)(2,1)}) %reduce-scatter.13.cloned.1.call-update) | async-done | bytes 1048592 | tf_op jit(solution)/shard_map/reduce_scatter | solution.py:243
  820.6 60.9 %all-reduce.9.cloned.1.call-done = (bf16[8,16,3,512]{3,1,2,0:T(8,128)(2,1)}, bf16[512,8,16]{0,2,1:T(8,128)(2,1)}, bf16[8,16,2048]{2,1,0:T(8,128)(2,1)}, bf16[2048,8,16]{0,2,1:T(8,128)(2,1)}) async-done(((bf16[8,16,3,512]{3,1,2,0:T(8,128)(2,1)}, bf16[512,8,16]{0,2,1:T(8,128)(2,1)}, bf16[8,16,2048]{2,1,0:T(8,128)(2,1)}, bf16[2048,8,16]{0,2,1:T(8,128)(2,1)}), (bf16[8,16,3,512]{3,1,2,0:T(8,128)(2,1)}, ...) | async-done | bytes 1572880 | tf_op jit(solution)/shard_map/psum | solution.py:333
  889.3 70.6 %reduce-scatter.21.cloned.1.call-done = bf16[256,2048]{1,0:T(8,128)(2,1)} async-done(((bf16[1024,2048]{1,0:T(8,128)(2,1)}), bf16[256,2048]{1,0:T(8,128)(2,1)}) %reduce-scatter.21.cloned.1.call-update) | async-done | bytes 1048592 | tf_op jit(solution)/shard_map/reduce_scatter | solution.py:314
  964.2 146.5 %all-reduce.7.cloned.1.call-done = (f32[2048,8,16]{0,2,1:T(8,128)}, f32[8,16,2048]{2,1,0:T(8,128)}, f32[2048,8,16]{0,2,1:T(8,128)}, f32[8,16,2048]{2,1,0:T(8,128)}) async-done(((f32[2048,8,16]{0,2,1:T(8,128)}, f32[8,16,2048]{2,1,0:T(8,128)}, f32[2048,8,16]{0,2,1:T(8,128)}, f32[8,16,2048]{2,1,0:T(8,128)}), (f32[2048,8,16]{0,2,1:T(8,128)}, f32[8,16,2048]{2,1,0:T(8,128)}, f32[2048,8,16]{0,2,1:T(8,128)}, ...) | async-done | bytes 4194320 | tf_op jit(solution)/shard_map/psum | solution.py:329
  (292 shorter events, 156.9 us)
Async XLA Ops:
  7.2 149.1 %copy-start = (bf16[512,2048]{1,0:T(8,128)(2,1)S(1)}, bf16[512,2048]{1,0:T(8,128)(2,1)}, u32[]{:S(2)}) copy-start(bf16[512,2048]{1,0:T(8,128)(2,1)} %param.38) | copy-start | bytes 6291460
  7.2 91.0 %all-gather.5.cloned.1.call-start = ((), (), s32[]{:S(2)}) async-start(), calls=%async_computation.8 | async-start | bytes 5242880 | tf_op jit(solution)/shard_map/all_gather | solution.py:200
  14.6 159.2 %reduce-scatter.11.cloned.1.call-start = ((), (), s32[]{:S(2)}) async-start(), calls=%async_computation.10 | async-start | bytes 40960 | tf_op jit(solution)/shard_map/reduce_scatter | solution.py:221
  26.9 433.0 %copy-start.48 = (f32[1024,8]{0,1:T(8,128)}, f32[1024,8]{0,1:T(8,128)S(1)}, u32[]{:S(2)}) copy-start(f32[1024,8]{0,1:T(8,128)S(1)} %get-tuple-element.101) | copy-start | bytes 98308
  156.2 94.9 %copy-start.5 = (bf16[256,2048]{1,0:T(8,128)(2,1)S(1)}, bf16[256,2048]{1,0:T(8,128)(2,1)}, u32[]{:S(2)}) copy-start(bf16[256,2048]{1,0:T(8,128)(2,1)} %param.32) | copy-start | bytes 3145732
  156.3 94.9 %reduce-scatter.9.cloned.1.call-start = ((), (), s32[]{:S(2)}) async-start(), calls=%async_computation.9 | async-start | bytes 5242880 | tf_op jit(solution)/shard_map/reduce_scatter | solution.py:218
  161.9 172.0 %all-gather.9.cloned.1.call-start = ((), (), s32[]{:S(2)}) async-start(), calls=%async_computation.14 | async-start | bytes 5242880 | tf_op jit(solution)/shard_map/all_gather | solution.py:256
  162.5 252.7 %all-gather.7.cloned.1.call-start = ((), (), s32[]{:S(2)}) async-start(), calls=%async_computation.11 | async-start | bytes 5242880 | tf_op jit(solution)/shard_map/all_gather | solution.py:232
  162.6 93.4 %copy-start.44 = (f32[2048]{0:T(1024)}, f32[2048]{0:T(1024)S(1)}, u32[]{:S(2)}) copy-start(f32[2048]{0:T(1024)S(1)} %convert_element_type.275) | copy-start | bytes 24580
  162.6 93.4 %copy-start.37 = (bf16[256,8]{0,1:T(8,128)(2,1)}, bf16[256,8]{0,1:T(8,128)(2,1)S(1)}, u32[]{:S(2)}) copy-start(bf16[256,8]{0,1:T(8,128)(2,1)S(1)} %fusion.173) | copy-start | bytes 12292
  253.2 84.5 %copy-start.53 = (f32[256]{0:T(256)}, f32[256]{0:T(256)S(1)}, u32[]{:S(2)}) copy-start(f32[256]{0:T(256)S(1)} %broadcast_multiply_fusion.6) | copy-start | bytes 3076
  254.5 83.2 %copy-start.57 = (f32[256]{0:T(256)}, f32[256]{0:T(256)S(1)}, u32[]{:S(2)}) copy-start(f32[256]{0:T(256)S(1)} %add_rsqrt_fusion) | copy-start | bytes 3076
  256.0 225.8 %reduce-scatter.19.cloned.1.call-start = ((), (), s32[]{:S(2)}) async-start(), calls=%async_computation.16 | async-start | bytes 40960 | tf_op jit(solution)/shard_map/reduce_scatter | solution.py:276
  337.8 113.9 %copy-start.75 = (bf16[1024,16]{0,1:T(8,128)(2,1)}, bf16[1024,16]{0,1:T(8,128)(2,1)S(1)}, u32[]{:S(2)}) copy-start(bf16[1024,16]{0,1:T(8,128)(2,1)S(1)} %fusion.108) | copy-start | bytes 98308
  464.2 95.0 %copy-start.38 = (bf16[256,8]{0,1:T(8,128)(2,1)S(1)}, bf16[256,8]{0,1:T(8,128)(2,1)}, u32[]{:S(2)}) copy-start(bf16[256,8]{0,1:T(8,128)(2,1)} %copy-done.37) | copy-start | bytes 12292
  464.2 94.9 %copy-start.45 = (f32[2048]{0:T(1024)S(1)}, f32[2048]{0:T(1024)}, u32[]{:S(2)}) copy-start(f32[2048]{0:T(1024)} %copy-done.44) | copy-start | bytes 24580
  464.2 94.9 %copy-start.54 = (f32[256]{0:T(256)S(1)}, f32[256]{0:T(256)}, u32[]{:S(2)}) copy-start(f32[256]{0:T(256)} %copy-done.53) | copy-start | bytes 3076
  464.2 94.9 %copy-start.58 = (f32[256]{0:T(256)S(1)}, f32[256]{0:T(256)}, u32[]{:S(2)}) copy-start(f32[256]{0:T(256)} %copy-done.57) | copy-start | bytes 3076
  464.2 94.9 %reduce-scatter.17.cloned.1.call-start = ((), (), s32[]{:S(2)}) async-start(), calls=%async_computation.15 | async-start | bytes 5242880 | tf_op jit(solution)/shard_map/reduce_scatter | solution.py:273
  478.2 84.0 %copy-start.7 = (bf16[256,2048]{1,0:T(8,128)(2,1)S(1)}, bf16[256,2048]{1,0:T(8,128)(2,1)}, u32[]{:S(2)}) copy-start(bf16[256,2048]{1,0:T(8,128)(2,1)} %param.51) | copy-start | bytes 3145732
  478.2 168.7 %all-gather.11.cloned.1.call-start = ((), (), s32[]{:S(2)}) async-start(), calls=%async_computation.17 | async-start | bytes 5242880 | tf_op jit(solution)/shard_map/all_gather | solution.py:292
  565.5 205.8 %reduce-scatter.15.cloned.1.call-start = ((), (), s32[]{:S(2)}) async-start(), calls=%async_computation.13 | async-start | bytes 40960 | tf_op jit(solution)/shard_map/reduce_scatter | solution.py:246
  573.0 202.9 %reduce-scatter.23.cloned.1.call-start = ((), (), s32[]{:S(2)}) async-start(), calls=%async_computation.19 | async-start | bytes 40960 | tf_op jit(solution)/shard_map/reduce_scatter | solution.py:317
  722.2 94.9 %reduce-scatter.13.cloned.1.call-start = ((), (), s32[]{:S(2)}) async-start(), calls=%async_computation.12 | async-start | bytes 5242880 | tf_op jit(solution)/shard_map/reduce_scatter | solution.py:243
  736.6 144.8 %all-reduce.9.cloned.1.call-start = ((), (), s32[]{:S(2)}) async-start(), calls=%async_computation.21 | async-start | bytes 3145728 | tf_op jit(solution)/shard_map/psum | solution.py:333
  757.0 202.9 %reduce-scatter.21.cloned.1.call-start = ((), (), s32[]{:S(2)}) async-start(), calls=%async_computation.18 | async-start | bytes 5242880 | tf_op jit(solution)/shard_map/reduce_scatter | solution.py:314
  768.5 342.2 %all-reduce.7.cloned.1.call-start = ((), (), s32[]{:S(2)}) async-start(), calls=%async_computation.20 | async-start | bytes 8388608 | tf_op jit(solution)/shard_map/psum | solution.py:329
  778.4 181.5 %copy-start.6 = (bf16[256,2048]{1,0:T(8,128)(2,1)S(1)}, bf16[256,2048]{1,0:T(8,128)(2,1)}, u32[]{:S(2)}) copy-start(bf16[256,2048]{1,0:T(8,128)(2,1)} %param.32) | copy-start | bytes 3145732
  778.4 181.5 %copy-start.43 = (f32[2048]{0:T(1024)S(1)}, f32[2048]{0:T(1024)}, u32[]{:S(2)}) copy-start(f32[2048]{0:T(1024)} %copy-done.42) | copy-start | bytes 24580
  778.4 181.5 %copy-start.52 = (f32[256]{0:T(256)S(1)}, f32[256]{0:T(256)}, u32[]{:S(2)}) copy-start(f32[256]{0:T(256)} %copy-done.51) | copy-start | bytes 3076
  778.4 181.5 %copy-start.56 = (f32[256]{0:T(256)S(1)}, f32[256]{0:T(256)}, u32[]{:S(2)}) copy-start(f32[256]{0:T(256)} %copy-done.55) | copy-start | bytes 3076
  778.5 181.5 %copy-start.74 = (bf16[256,16]{0,1:T(8,128)(2,1)S(1)}, bf16[256,16]{0,1:T(8,128)(2,1)}, u32[]{:S(2)}) copy-start(bf16[256,16]{0,1:T(8,128)(2,1)} %reduce-scatter.23.cloned.1.call-done) | copy-start | bytes 24580
  (67 other events, 876.1 us)
Sparse Core Ops, SparseCore 0:
  14.7 83.4 all-gather.4
  156.3 17.4 reduce-scatter.10
  176.2 74.8 reduce-scatter.8
  252.6 81.2 all-gather.8
  335.9 79.2 all-gather.6
  464.3 17.4 reduce-scatter.18
  484.2 74.8 reduce-scatter.16
  565.6 81.2 all-gather.10
  649.2 17.4 reduce-scatter.14
  722.3 17.4 reduce-scatter.22
  742.1 74.9 reduce-scatter.12
  821.5 59.8 all-reduce.8
  883.7 76.1 reduce-scatter.20
  967.2 143.3 all-reduce.6
where the time goes:
time: 1140 us; the launch traced here: 1130 us
  waiting for transfers between devices  770 us (68%)
  matrix products  230 us (20%)
  local copies, waits for them, and re-layouts  54.5 us (5%)
  other arithmetic  53.9 us (5%)
  between operations  15.9 us (1%)
    psum x1, waiting for transfers between devices, local(): lax.psum((grad_a_qkv, grad_b_dense, grad_a_up, grad_b_down), ('dp', 'mp'))  146 us
    dot_general x12, matrix products, plain_dot(): return jnp.dot(left, right, preferred_element_type=jnp.float32)  81 us
    all_gather x1, waiting for transfers between devices, local(): cot_all = lax.all_gather(cotangent, 'mp', axis=0, tiled=True)  77.8 us
    reduce_scatter x1, waiting for transfers between devices, local(): lax.psum_scatter(d_second_part.astype(jnp.bfloat16), 'mp', scatter_dimens...  77.3 us
    reduce_scatter x1, waiting for transfers between devices, local(): lax.psum_scatter(dense_part.astype(jnp.bfloat16), 'mp', scatter_dimension...  77.3 us
    all_gather x1, waiting for transfers between devices, local(): middle_all = lax.all_gather(middle_low, 'mp', axis=0, tiled=True)  73.6 us
    reduce_scatter x1, waiting for transfers between devices, local(): lax.psum_scatter(d_first_part.astype(jnp.bfloat16), 'mp', scatter_dimensi...  70.6 us
    dot_general x12, matrix products, transpose_dot(): lax.dot_general(left, right, (((1,), (1,)), ((), ())), preferred_element_...  69.1 us
  transfers between devices with their start and end apart: 14, of which 12 were waited for; matrix products, arithmetic and copies ran while one was open for 19% of the time, Pallas kernels for 0%

commit v1 on v0

v1 whole, which is shorter than its diff:
```python
import functools

import jax
import jax.numpy as jnp
from jax import lax
from jax.experimental import pallas as pl
from jax.experimental.pallas import tpu as pltpu
from jax.sharding import PartitionSpec as P

HEADS = 32
HD = 64
LONGEST = 512
EPSILON = 1e-05
F32 = jnp.float32
BF16 = jnp.bfloat16
MASKED = -1e30


def layer_norm(values, gain, bias):
    center = jnp.mean(values, -1, keepdims=True)
    centred = values - center
    variance = jnp.mean(centred * centred, -1, keepdims=True)
    scaler = lax.rsqrt(variance + EPSILON)
    normal = centred * scaler
    return (normal * gain.astype(F32) + bias.astype(F32), normal, scaler)


def norm_back(grad, normal, scaler, gain):
    scaled = grad * gain.astype(F32)
    first_mean = jnp.mean(scaled, -1, keepdims=True)
    second_mean = jnp.mean(scaled * normal, -1, keepdims=True)
    return (scaled - first_mean - normal * second_mean) * scaler


def dot_nn(left, right):
    return jnp.dot(left, right, preferred_element_type=F32)


def dot_nt(left, right):
    return lax.dot_general(left, right, (((1,), (1,)), ((), ())), preferred_element_type=F32)


def dot_tn(left, right):
    return lax.dot_general(left, right, (((0,), (0,)), ((), ())), preferred_element_type=F32)


def swap(value, axis, bit):
    pairs = [(i, i ^ bit) for i in range(lax.axis_size(axis))]
    return lax.ppermute(value, axis, pairs)


def gather_four(value):
    one = swap(value, "mp", 1)
    two = swap(value, "mp", 2)
    three = swap(two, "mp", 1)
    return [value, one, two, three]


def scatter_four(parts):
    relay = swap(parts[3].astype(BF16), "mp", 1)
    pair = (parts[2].astype(F32) + relay.astype(F32)).astype(BF16)
    far = swap(pair, "mp", 2)
    near = swap(parts[1].astype(BF16), "mp", 1)
    return parts[0].astype(F32) + near.astype(F32) + far.astype(F32)


def place(blocks, index):
    rows = blocks[0].shape[0]
    whole = jnp.zeros((rows * len(blocks),) + blocks[0].shape[1:], blocks[0].dtype)
    for offset, block in enumerate(blocks):
        whole = lax.dynamic_update_slice_in_dim(whole, block, (index ^ offset) * rows, 0)
    return whole


def lane_mask(half):
    return (lax.broadcasted_iota(jnp.int32, (1, 2 * HD), 1) // HD) == half


def pair_scores(keys, query, seg_col, seg_row, slope, apart):
    rows, cols = keys.shape[0], query.shape[0]
    raw = dot_nt(keys, query)
    delta = (
        lax.broadcasted_iota(jnp.int32, (rows, cols), 0)
        - lax.broadcasted_iota(jnp.int32, (rows, cols), 1)
        - apart
    )
    allowed = seg_col == seg_row
    if apart == 0:
        allowed = allowed & (delta <= 0)
    return jnp.where(allowed, raw + slope * delta.astype(F32), MASKED)


def reach_of(block):
    return -(-LONGEST // block)


def forward_kernel(block, seg_ref, slope_ref, col_ref, row_ref, q_ref, k_ref, v_ref, o_ref, stat_ref,
                   turned_ref, top_ref, total_ref, sum_ref):
    head = pl.program_id(0)
    half = lax.rem(head, 2)
    slope = slope_ref[head]
    count = q_ref.shape[0] // block
    mask = lane_mask(half)
    base = half * HD

    @pl.when(half == 0)
    def _():
        turned_ref[...] = v_ref[...].T

    for i in range(count):
        queries = pl.ds(i * block, block)
        scaled = jnp.where(mask, q_ref[queries, :] * HD ** -0.5, 0).astype(BF16)
        row = row_ref[:, queries]

        def one(j, first):
            keys = pl.ds(j * block, block)
            scores = pair_scores(k_ref[keys, :], scaled, col_ref[keys, :1], row, slope, (i - j) * block)
            best = jnp.max(scores, 0, keepdims=True)
            if not first:
                best = jnp.maximum(best, top_ref[...])
            weights = jnp.exp(scores - best)
            total = jnp.sum(weights, 0, keepdims=True)
            rows = pl.ds(pl.multiple_of(base, HD), HD)
            result = dot_nn(turned_ref[rows, keys], weights.astype(BF16))
            if not first:
                fade = jnp.exp(top_ref[...] - best)
                total = total + fade * total_ref[...]
                result = result + fade * sum_ref[...]
            top_ref[...] = best
            total_ref[...] = total
            sum_ref[...] = result

        one(i, True)
        for back in range(1, min(i, reach_of(block)) + 1):
            j = i - back

            @pl.when(seg_ref[j * block + block - 1] == seg_ref[i * block])
            def _(j=j):
                one(j, False)

        stat_ref[0, :, queries] = jnp.broadcast_to(top_ref[...] + jnp.log(total_ref[...]), (8, block))
        done = (sum_ref[...] / total_ref[...]).T
        both = jnp.concatenate([done, done], 1)
        kept = o_ref[queries, :]
        o_ref[queries, :] = jnp.where(mask, both, kept.astype(F32)).astype(BF16)


def attention_forward(query, key, val, seg, slopes):
    rows, width = query.shape
    block = min(256, rows)
    wide = pl.BlockSpec((rows, 2 * HD), lambda h, *_: (0, h // 2))
    col = jnp.broadcast_to(seg[:, None], (rows, 128))
    return pl.pallas_call(
        functools.partial(forward_kernel, block),
        out_shape=(
            jax.ShapeDtypeStruct((rows, width), BF16),
            jax.ShapeDtypeStruct((width // HD, 8, rows), F32),
        ),
        grid_spec=pltpu.PrefetchScalarGridSpec(
            num_scalar_prefetch=2,
            grid=(width // HD,),
            in_specs=[
                pl.BlockSpec((rows, 128), lambda h, *_: (0, 0)),
                pl.BlockSpec((1, rows), lambda h, *_: (0, 0)),
                wide, wide, wide,
            ],
            out_specs=(wide, pl.BlockSpec((1, 8, rows), lambda h, *_: (h, 0, 0))),
            scratch_shapes=[
                pltpu.VMEM((2 * HD, rows), BF16),
                pltpu.VMEM((1, block), F32),
                pltpu.VMEM((1, block), F32),
                pltpu.VMEM((HD, block), F32),
            ],
        ),
        name="attention_forward",
    )(seg, slopes, col, seg[None, :], query, key, val)


def backward_kernel(block, seg_ref, slope_ref, col_ref, row_ref, stat_ref, center_ref, q_ref, k_ref, v_ref, g_ref,
                    dq_ref, dk_ref, dv_ref, turned_ref, qsum_ref, ksum_ref, vsum_ref):
    head = pl.program_id(0)
    half = lax.rem(head, 2)
    slope = slope_ref[head]
    count = q_ref.shape[0] // block
    mask = lane_mask(half)
    base = half * HD
    rows = pl.ds(pl.multiple_of(base, HD), HD)

    @pl.when(half == 0)
    def _():
        turned_ref[...] = k_ref[...].T
        qsum_ref[...] = jnp.zeros_like(qsum_ref)
        ksum_ref[...] = jnp.zeros_like(ksum_ref)
        vsum_ref[...] = jnp.zeros_like(vsum_ref)

    for i in range(count):
        queries = pl.ds(i * block, block)
        scaled = jnp.where(mask, q_ref[queries, :] * HD ** -0.5, 0).astype(BF16)
        grads = jnp.where(mask, g_ref[queries, :], 0).astype(BF16)
        row = row_ref[:, queries]

        def one(j):
            keys = pl.ds(j * block, block)
            scores = pair_scores(k_ref[keys, :], scaled, col_ref[keys, :1], row, slope, (i - j) * block)
            probs = jnp.exp(scores - stat_ref[0, :1, queries])
            d_probs = dot_nt(v_ref[keys, :], grads)
            d_scores = (probs * (d_probs - center_ref[0, :1, queries])).astype(BF16)
            vsum_ref[keys, :] += dot_nn(probs.astype(BF16), grads)
            ksum_ref[keys, :] += dot_nn(d_scores, scaled)
            qsum_ref[rows, queries] += dot_nn(turned_ref[rows, keys], d_scores)

        one(i)
        for back in range(1, min(i, reach_of(block)) + 1):
            j = i - back

            @pl.when(seg_ref[j * block + block - 1] == seg_ref[i * block])
            def _(j=j):
                one(j)

    @pl.when(half == 1)
    def _():
        dq_ref[...] = (qsum_ref[...] * HD ** -0.5).T.astype(BF16)
        dk_ref[...] = ksum_ref[...].astype(BF16)
        dv_ref[...] = vsum_ref[...].astype(BF16)


def attention_backward(query, key, val, grad, stat, center, seg, slopes):
    rows, width = query.shape
    block = min(256, rows)
    wide = pl.BlockSpec((rows, 2 * HD), lambda h, *_: (0, h // 2))
    thin = pl.BlockSpec((1, 8, rows), lambda h, *_: (h, 0, 0))
    col = jnp.broadcast_to(seg[:, None], (rows, 128))
    return pl.pallas_call(
        functools.partial(backward_kernel, block),
        out_shape=(jax.ShapeDtypeStruct((rows, width), BF16),) * 3,
        grid_spec=pltpu.PrefetchScalarGridSpec(
            num_scalar_prefetch=2,
            grid=(width // HD,),
            in_specs=[
                pl.BlockSpec((rows, 128), lambda h, *_: (0, 0)),
                pl.BlockSpec((1, rows), lambda h, *_: (0, 0)),
                thin, thin, wide, wide, wide, wide,
            ],
            out_specs=(wide, wide, wide),
            scratch_shapes=[
                pltpu.VMEM((2 * HD, rows), BF16),
                pltpu.VMEM((2 * HD, rows), F32),
                pltpu.VMEM((rows, 2 * HD), F32),
                pltpu.VMEM((rows, 2 * HD), F32),
            ],
        ),
        name="attention_backward",
    )(seg, slopes, col, seg[None, :], stat, center, query, key, val, grad)


def gelu_pair(values):
    below = 0.5 * (1.0 + lax.erf(values * 0.5 ** 0.5))
    density = jnp.exp(values * values * -0.5) * 0.3989422804014327
    return values * below, below + values * density


def turned(factor, which):
    return lax.dynamic_index_in_dim(factor.transpose(1, 2, 0), which, 0, False)


def local(
    layer_in, first_gain, first_bias, w_qkv, a_qkv, b_qkv, w_dense, a_dense, b_dense, second_gain, second_bias,
    w_up, a_up, b_up, w_down, a_down, b_down, segment_ids, adapter_ids, cotangent,
):
    own_rows, width = layer_in.shape
    kinds = a_qkv.shape[1]
    rank = a_qkv.shape[2]
    local_width = w_dense.shape[0]
    local_ff = w_up.shape[1]
    local_heads = local_width // HD
    index = lax.axis_index("mp")
    spot = lax.axis_index("dp")
    copies = lax.axis_size("dp")
    pair_rows = 2 * own_rows
    low, high = index & 1, index >> 1
    which = adapter_ids[0]
    seg = segment_ids[0]
    head_ids = (index * local_heads + lax.iota(jnp.int32, local_heads)).astype(F32)
    slopes = jnp.exp2(-8.0 * (head_ids + 1.0) / HEADS)

    aq, ad, au, an = (turned(a, which) for a in (a_qkv, a_dense, a_up, a_down))
    bq = lax.dynamic_index_in_dim(b_qkv.transpose(0, 2, 1, 3), which, 0, False)
    bd, bu, bn = (lax.dynamic_index_in_dim(b, which, 0, False) for b in (b_dense, b_up, b_down))

    blocks = gather_four(layer_in)
    ad_parts = gather_four(ad)
    bu_far, an_far = swap(bu, "mp", 2), swap(an, "mp", 2)

    def slice_of(weight):
        size = weight.shape[0] // copies
        return lax.dynamic_slice_in_dim(weight, spot * size, size, 0)

    wd_slices = gather_four(slice_of(w_dense))
    wd = [w_dense] + [lax.all_gather(s, "dp", axis=0, tiled=True) for s in wd_slices[1:]]
    wu_far = lax.all_gather(swap(slice_of(w_up), "mp", 2), "dp", axis=0, tiled=True)
    wn_far = lax.all_gather(swap(slice_of(w_down), "mp", 2), "dp", axis=0, tiled=True)

    rows_all = place(blocks, index)
    normed_all = layer_norm(rows_all.astype(F32), first_gain, first_bias)[0].astype(BF16)
    wq = w_qkv.transpose(1, 0, 2)
    z_qkv = dot_nt(normed_all, aq).astype(BF16)
    query, key, val = (
        (dot_nn(normed_all, wq[i]) + dot_nn(z_qkv, bq[i])).astype(BF16) for i in range(3)
    )
    mixed, stat = attention_forward(query, key, val, seg, slopes)

    mine = lax.dynamic_slice_in_dim(mixed, high * pair_rows, pair_rows, 0)
    other = lax.dynamic_slice_in_dim(mixed, (1 - high) * pair_rows, pair_rows, 0)
    m_one = swap(mine, "mp", 1)
    m_two = swap(other, "mp", 2)
    m_three = swap(m_two, "mp", 1)
    m_parts = [mine, m_one, m_two, m_three]
    z_dense = sum(dot_nt(m, a) for m, a in zip(m_parts, ad_parts)).astype(BF16)
    branch = sum(dot_nn(m, w) for m, w in zip(m_parts, wd)) + dot_nn(z_dense, bd)
    rows_pair = lax.dynamic_slice_in_dim(rows_all, high * pair_rows, pair_rows, 0)
    middle = rows_pair.astype(F32) + branch
    second, normal_two, scaler_two = layer_norm(middle, second_gain, second_bias)
    second = second.astype(BF16)

    def own(value):
        return lax.dynamic_slice_in_dim(value, low * own_rows, own_rows, 0)

    def partner(value):
        return lax.dynamic_slice_in_dim(value, (1 - low) * own_rows, own_rows, 0)

    cot_pair = place([cotangent, swap(cotangent, "mp", 1)], low)
    z_up = dot_nt(second, au).astype(BF16)
    dz_down = dot_nt(cot_pair, bn).astype(BF16)
    down_part, d_second_part, z_down, dz_up, ga_down, gb_up = 0.0, 0.0, 0.0, 0.0, [], []
    for up, bup, down, adown in ((w_up, bu, w_down, an), (wu_far, bu_far, wn_far, an_far)):
        hidden = dot_nn(second, up) + dot_nn(z_up, bup)
        active, slope = gelu_pair(hidden)
        active = active.astype(BF16)
        d_active = dot_nt(cot_pair, down) + dot_nn(dz_down, adown)
        d_hidden = (d_active * slope).astype(BF16)
        d_second_part += dot_nt(d_hidden, up)
        dz_up += dot_nt(d_hidden, bup)
        down_part += dot_nn(active, down)
        z_down += dot_nt(active, adown)
        ga_down.append(dot_tn(dz_down, active))
        gb_up.append(dot_tn(z_up, d_hidden))
    dz_up, z_down = dz_up.astype(BF16), z_down.astype(BF16)
    d_second_part = d_second_part + dot_nn(dz_up, au)
    down_part = down_part + dot_nn(z_down, bn)
    d_second = own(d_second_part) + swap(partner(d_second_part).astype(BF16), "mp", 1).astype(F32)
    mlp = own(down_part) + swap(partner(down_part).astype(BF16), "mp", 1).astype(F32)
    layer_out = (own(middle) + mlp).astype(BF16)
    ga_up = dot_tn(dz_up, second)
    gb_down = dot_tn(z_down, cot_pair)
    ga_down = ga_down[0] + swap(ga_down[1].astype(BF16), "mp", 2).astype(F32)
    gb_up = gb_up[0] + swap(gb_up[1].astype(BF16), "mp", 2).astype(F32)

    d_middle = cotangent.astype(F32) + norm_back(d_second, own(normal_two), own(scaler_two), second_gain)
    middle_low = d_middle.astype(BF16)
    gb_dense = dot_tn(own(z_dense), middle_low)
    dz_dense = dot_nt(middle_low, bd).astype(BF16)
    ga_dense = [dot_tn(dz_dense, own(m)) for m in m_parts]
    d_mixed = [
        (dot_nt(middle_low, w) + dot_nn(dz_dense, a)).astype(BF16) for w, a in zip(wd, ad_parts)
    ]
    d_mixed = place([d_mixed[0]] + [swap(d_mixed[r], "mp", r) for r in (1, 2, 3)], index)

    center = jnp.einsum(
        "thd,thd->ht",
        d_mixed.astype(F32).reshape(-1, local_heads, HD),
        mixed.astype(F32).reshape(-1, local_heads, HD),
    )
    center = jnp.broadcast_to(center[:, None, :], stat.shape)
    d_parts = attention_backward(query, key, val, d_mixed, stat, center, seg, slopes)
    gb_qkv = [dot_tn(z_qkv, d) for d in d_parts]
    dz_qkv = sum(dot_nt(d, b) for d, b in zip(d_parts, (bq[0], bq[1], bq[2]))).astype(BF16)
    ga_qkv = dot_tn(dz_qkv, normed_all)
    d_first_part = sum(dot_nt(d, wq[i]) for i, d in enumerate(d_parts)) + dot_nn(dz_qkv, aq)
    d_first = scatter_four([
        lax.dynamic_slice_in_dim(d_first_part, (index ^ r) * own_rows, own_rows, 0) for r in range(4)
    ])
    normal_one, scaler_one = layer_norm(layer_in.astype(F32), first_gain, first_bias)[1:]
    input_grad = (d_middle + norm_back(d_first, normal_one, scaler_one, first_gain)).astype(BF16)

    quarter = width // 4
    full = jnp.concatenate([ga_qkv, gb_dense, ga_up, gb_down], 0)
    full = scatter_four([
        lax.dynamic_slice_in_dim(full, (index ^ r) * quarter, quarter, 1) for r in range(4)
    ])
    full = place(gather_four(full.astype(BF16)[None]), index)
    ga_dense = scatter_four(ga_dense)
    shard = jnp.concatenate([*gb_qkv, ga_dense, gb_up, ga_down], 1)
    packed = jnp.concatenate([
        full.reshape(-1, 128), shard.astype(BF16).reshape(-1, 128),
        jnp.full((16, 128), which, BF16),
    ], 0)
    packed = lax.all_gather(packed, "dp", axis=0)
    ids = packed[:, -1, 0]
    choice = (ids[None, :] == lax.iota(jnp.int32, kinds).astype(BF16)[:, None]).astype(BF16)

    def spread(first, count, *shape):
        part = lax.slice_in_dim(packed, first // 128, (first + count) // 128, axis=1).reshape(copies, -1)
        return dot_nn(choice, part).reshape(kinds, *shape)

    size = 4 * rank * width
    full = spread(0, size, 4, 4, rank, quarter)
    ga_qkv, gb_dense, ga_up, gb_down = (
        full[:, :, i].transpose(0, 2, 1, 3).reshape(kinds, rank, width) for i in range(4)
    )
    shard = spread(size, rank * (4 * local_width + 2 * local_ff), rank, -1)
    gb_qkv = shard[:, :, : 3 * local_width].reshape(kinds, rank, 3, local_width)
    ga_dense = shard[:, :, 3 * local_width : 4 * local_width]
    gb_up = shard[:, :, 4 * local_width : 4 * local_width + local_ff]
    ga_down = shard[:, :, 4 * local_width + local_ff :]
    return (
        layer_out,
        input_grad,
        ga_qkv.transpose(2, 0, 1),
        gb_qkv,
        ga_dense.transpose(2, 0, 1),
        gb_dense,
        ga_up.transpose(2, 0, 1),
        gb_up,
        ga_down.transpose(2, 0, 1),
        gb_down,
    )


def solution(mesh):
    return jax.shard_map(
        local,
        mesh=mesh,
        in_specs=(
            P(("dp", "mp"), None), P(), P(), P(None, None, "mp"), P(), P(None, None, None, "mp"), P("mp", None),
            P("mp", None, None), P(), P(), P(), P(None, "mp"), P(), P(None, None, "mp"), P("mp", None),
            P("mp", None, None), P(), P("dp", None), P("dp"), P(("dp", "mp"), None),
        ),
        out_specs=(
            P(("dp", "mp"), None), P(("dp", "mp"), None), P(), P(None, None, None, "mp"), P("mp", None, None), P(),
            P(), P(None, None, "mp"), P("mp", None, None), P(),
        ),
        check_vma=False,
    )
```

time: 1140 us -> 706 us (0.62)
  waiting for transfers between devices: 770 us -> 275 us
  Pallas kernels: 0 us -> 59.1 us
  starting transfers between devices: 0.96 us -> 50 us
  matrix products: 230 us -> 200 us
  other arithmetic: 53.9 us -> 28.2 us
  local copies, waits for them, and re-layouts: 54.5 us -> 69.9 us
    all_gather x4 -> x6, waiting for transfers between devices: 283 us -> 0.01 us  [the longest x3 0.01 us: local(): lax.all_gather(s, 'dp', axis=0, tiled=True)]
    reduce_scatter x8 -> x0, waiting for transfers between devices: 279 us -> none  [the longest x1 77.3 us: local(): lax.psum_scatter(d_second_part.astype(jnp.bfloat16), 'mp', scatter_dimens...]
    ppermute x0 -> x36, waiting for transfers between devices: none -> 275 us  [swap(): return lax.ppermute(value, axis, pairs)]
    psum x2 -> x0, waiting for transfers between devices: 207 us -> none  [the longest x1 146 us: local(): lax.psum((grad_a_qkv, grad_b_dense, grad_a_up, grad_b_down), ('dp', 'mp'))]
    pallas_call x0 -> x2, Pallas kernels: none -> 59.1 us  [the longest x1 30.4 us: attention_forward(): pl.pallas_call(functools.partial(forward_kernel, block), out_shape=(jax.S...]
    ppermute x0 -> x36, starting transfers between devices: none -> 49.8 us  [swap(): return lax.ppermute(value, axis, pairs)]
    dot_general x44 -> x69, matrix products: 230 us -> 200 us  [the longest x28 93.3 us: dot_nn(): return jnp.dot(left, right, preferred_element_type=F32)]
    convert_element_type x17 -> x11, other arithmetic: 37.3 us -> 10.4 us  [the longest x1 3.64 us: local(): layer_norm(rows_all.astype(F32), first_gain, first_bias)[0].astype(BF16)]
  transfers between devices with their start and end apart: 14 -> 42, of which waited for: 12 -> 21; matrix products, arithmetic and copies ran while one was open for 19% -> 34% of each run, Pallas kernels for 0% -> 8%
where the time goes in v1:
time: 706 us; the launch traced here: 699 us
  waiting for transfers between devices  275 us (39%)
  matrix products  200 us (28%)
  local copies, waits for them, and re-layouts  69.9 us (10%)
  Pallas kernels  59.1 us (8%)
  starting transfers between devices  50 us (7%)
  other arithmetic  28.2 us (4%)
  between operations  16.1 us (2%)
    ppermute x36, waiting for transfers between devices, swap(): return lax.ppermute(value, axis, pairs)  275 us
    dot_general x28, matrix products, dot_nn(): return jnp.dot(left, right, preferred_element_type=F32)  93.3 us
    dot_general x26, matrix products, dot_nt(): lax.dot_general(left, right, (((1,), (1,)), ((), ())), preferred_element_...  88.7 us
    ppermute x36, starting transfers between devices, swap(): return lax.ppermute(value, axis, pairs)  49.8 us
    pallas_call x1, Pallas kernels, attention_forward(): pl.pallas_call(functools.partial(forward_kernel, block), out_shape=(jax.S...  30.4 us
    pallas_call x1, Pallas kernels, attention_backward(): pl.pallas_call(functools.partial(backward_kernel, block), out_shape=(jax....  28.8 us
    unnamed x116, local copies, waits for them, and re-layouts  20.5 us
    dot_general x15, matrix products, dot_tn(): lax.dot_general(left, right, (((0,), (0,)), ((), ())), preferred_element_...  18.4 us
  transfers between devices with their start and end apart: 42, of which 21 were waited for; matrix products, arithmetic and copies ran while one was open for 34% of the time, Pallas kernels for 8%

profile of v1, /device:TPU:0, one launch (start us, length us, event | category | flops | bytes accessed | tf_op | source)
XLA Modules:
  0.0 699.0 jit_solution(15963169130386245775)
XLA Ops:
  11.9 6.4 collective-permute-done.4
  21.2 11.4 %collective-permute-done.6 = bf16[64,2048]{1,0:T(8,128)(2,1)} collective-permute-done((bf16[64,2048]{1,0:T(8,128)(2,1)S(1)}, bf16[64,2048]{1,0:T(8,128)(2,1)}, u32[]{:S(2)}, u32[]{:S(2)}) %collective-permute-start.6) | collective-permute-done | bytes 262176 | tf_op jit(solution)/shard_map/ppermute | solution.py:49
  33.1 7.1 %collective-permute-done.8 = bf16[64,2048]{1,0:T(8,128)(2,1)S(1)} collective-permute-done((bf16[64,2048]{1,0:T(8,128)(2,1)}, bf16[64,2048]{1,0:T(8,128)(2,1)S(1)}, u32[]{:S(2)}, u32[]{:S(2)}) %collective-permute-start.8) | collective-permute-done | bytes 262176 | tf_op jit(solution)/shard_map/ppermute | solution.py:49
  45.4 45.4 %collective-permute-done.12 = bf16[256,2048]{1,0:T(8,128)(2,1)} collective-permute-done((bf16[256,2048]{1,0:T(8,128)(2,1)S(1)}, bf16[256,2048]{1,0:T(8,128)(2,1)}, u32[]{:S(2)}, u32[]{:S(2)}) %collective-permute-start.12) | collective-permute-done | bytes 1048608 | tf_op jit(solution)/shard_map/ppermute | solution.py:49
  112.8 26.6 %collective-permute-done = bf16[256,2048]{1,0:T(8,128)(2,1)} collective-permute-done((bf16[256,2048]{1,0:T(8,128)(2,1)S(1)}, bf16[256,2048]{1,0:T(8,128)(2,1)}, u32[]{:S(2)}, u32[]{:S(2)}) %collective-permute-start) | collective-permute-done | bytes 1048608 | tf_op jit(solution)/shard_map/ppermute | solution.py:49
  147.1 38.5 %collective-permute-done.14 = bf16[256,2048]{1,0:T(8,128)(2,1)} collective-permute-done((bf16[256,2048]{1,0:T(8,128)(2,1)}, bf16[256,2048]{1,0:T(8,128)(2,1)}, u32[]{:S(2)}, u32[]{:S(2)}) %collective-permute-start.14) | collective-permute-done | bytes 1048608 | tf_op jit(solution)/shard_map/ppermute | solution.py:49
  197.4 11.3 %collective-permute-done.2 = bf16[256,2048]{1,0:T(8,128)(2,1)S(1)} collective-permute-done((bf16[256,2048]{1,0:T(8,128)(2,1)}, bf16[256,2048]{1,0:T(8,128)(2,1)S(1)}, u32[]{:S(2)}, u32[]{:S(2)}) %collective-permute-start.2) | collective-permute-done | bytes 1048608 | tf_op jit(solution)/shard_map/ppermute | solution.py:49
  234.3 30.4 %attention_forward.1 = (bf16[1024,512]{1,0:T(8,128)(2,1)}, f32[8,8,1024]{2,1,0:T(8,128)}) custom-call(s32[1024]{0:T(1024)} %bitcast.270, f32[8]{0:T(128)} %multiply_exponential_fusion.slope_ref, s32[1024,128]{1,0:T(8,128)} %broadcast_in_dim.17.col_ref, s32[1,1024]{1,0:T(1,128)} %row_ref.3, bf16[1024,512]{1,0:T(8,128)(2,1)} %add_convert_fusion.5.q_ref, ...), custom_call_target="tpu_custom_call" | custom-call | tf_op jit(solution)/shard_map/attention_forward/pallas_call | solution.py:153
  274.5 4.4 fusion.95
  278.9 13.6 %collective-permute-done.5 = bf16[512,512]{1,0:T(8,128)(2,1)} collective-permute-done((bf16[512,512]{1,0:T(8,128)(2,1)S(1)}, bf16[512,512]{1,0:T(8,128)(2,1)}, u32[]{:S(2)}, u32[]{:S(2)}) %collective-permute-start.5) | collective-permute-done | bytes 524320 | tf_op jit(solution)/shard_map/ppermute | solution.py:49
  299.5 7.4 %collective-permute-done.7 = bf16[512,512]{1,0:T(8,128)(2,1)} collective-permute-done((bf16[512,512]{1,0:T(8,128)(2,1)}, bf16[512,512]{1,0:T(8,128)(2,1)}, u32[]{:S(2)}, u32[]{:S(2)}) %collective-permute-start.7) | collective-permute-done | bytes 524320 | tf_op jit(solution)/shard_map/ppermute | solution.py:49
  311.7 5.0 fusion.96
  316.7 5.1 fusion.97
  321.9 9.0 %fusion.94 = (f32[512]{0:T(512)S(1)}, f32[512,2048]{1,0:T(8,128)S(1)}) fusion(f32[512,2048]{1,0:T(8,128)} %fusion.56, bf16[512,512]{1,0:T(8,128)(2,1)} %collective-permute-done.7, bf16[512,2048]{1,0:T(8,128)(2,1)} %all-gather.12.cloned.1.call-done, f32[512,2048]{1,0:T(8,128)} %fusion.97, f32[512,2048]{1,0:T(8,128)} %fusion.95, f32[512,2048]{1,0:T(8,128)} %fusion.96, ...), kind=kOutput, calls=%fused_computation.211 | convolution fusion | flops 1081081344 | bytes 25692164 | tf_op jit(solution)/shard_map/dot_general | solution.py:36
  338.1 4.6 fusion.99
  344.9 8.9 %multiply_convert_fusion.1 = bf16[512,2048]{1,0:T(8,128)(2,1)S(1)} fusion(f32[512,2048]{1,0:T(8,128)S(1)} %get-tuple-element.76, f32[512,2048]{1,0:T(8,128)S(1)} %copy-done.23, bf16[512,2048]{1,0:T(8,128)(2,1)} %constant_dynamic-update-slice_fusion.7, bf16[2048,2048]{1,0:T(8,128)(2,1)} %param.34), kind=kOutput, calls=%fused_computation.11 | convolution fusion | flops 4306501632 | bytes 20971520 | tf_op jit(solution)/shard_map/dot_general | solution.py:40
  359.3 9.6 %fusion.104 = f32[512,2048]{1,0:T(8,128)} fusion(bf16[512,2048]{1,0:T(8,128)(2,1)S(1)} %multiply_convert_fusion.1, bf16[2048,2048]{1,0:T(8,128)(2,1)} %param.31), kind=kOutput, calls=%fused_computation.221 | convolution fusion | flops 4294967296 | bytes 14680064 | tf_op jit(solution)/shard_map/dot_general | solution.py:40
  368.9 6.0 fusion.100
  374.9 10.2 %multiply_convert_fusion.2 = (bf16[512,2048]{1,0:T(8,128)(2,1)}, f32[512,2048]{1,0:T(8,128)}) fusion(f32[512,2048]{1,0:T(8,128)} %fusion.101, bf16[512,2048]{1,0:T(8,128)(2,1)} %copy-done.9, bf16[2048,2048]{1,0:T(8,128)(2,1)} %all-gather.14.cloned.1.call-done), kind=kOutput, calls=%fused_computation.13 | convolution fusion | flops 4301258752 | bytes 20971520 | tf_op jit(solution)/shard_map/dot_general | solution.py:36
  385.2 10.5 %multiply_convert_fusion = bf16[512,2048]{1,0:T(8,128)(2,1)S(1)} fusion(f32[512,2048]{1,0:T(8,128)} %get-tuple-element.78, f32[512,2048]{1,0:T(8,128)} %fusion.105, bf16[512,2048]{1,0:T(8,128)(2,1)} %constant_dynamic-update-slice_fusion.7, bf16[2048,2048]{1,0:T(8,128)(2,1)} %all-gather.16.cloned.1.call-done), kind=kOutput, calls=%fused_computation.10 | convolution fusion | flops 4306501632 | bytes 20971520 | tf_op jit(solution)/shard_map/dot_general | solution.py:40
  399.0 9.8 %add_add_fusion.1 = f32[512,2048]{1,0:T(8,128)S(1)} fusion(f32[512,2048]{1,0:T(8,128)S(1)} %fusion.49, f32[512,2048]{1,0:T(8,128)} %fusion.104, bf16[512,2048]{1,0:T(8,128)(2,1)S(1)} %multiply_convert_fusion, bf16[2048,2048]{1,0:T(8,128)(2,1)} %all-gather.14.cloned.1.call-done), kind=kOutput, calls=%fused_computation.9 | convolution fusion | flops 4297064448 | bytes 23068672 | tf_op jit(solution)/shard_map/dot_general | solution.py:40
  420.9 14.8 %collective-permute-done.18 = bf16[256,2048]{1,0:T(8,128)(2,1)S(1)} collective-permute-done((bf16[256,2048]{1,0:T(8,128)(2,1)S(1)}, bf16[256,2048]{1,0:T(8,128)(2,1)S(1)}, u32[]{:S(2)}, u32[]{:S(2)}) %collective-permute-start.18) | collective-permute-done | bytes 1048608 | tf_op jit(solution)/shard_map/ppermute | solution.py:49
  463.2 7.8 %collective-permute-done.20 = bf16[256,512]{1,0:T(8,128)(2,1)S(1)} collective-permute-done((bf16[256,512]{1,0:T(8,128)(2,1)S(1)}, bf16[256,512]{1,0:T(8,128)(2,1)S(1)}, u32[]{:S(2)}, u32[]{:S(2)}) %collective-permute-start.20) | collective-permute-done | bytes 262176 | tf_op jit(solution)/shard_map/ppermute | solution.py:49
  475.1 28.8 %attention_backward.1 = (bf16[1024,512]{1,0:T(8,128)(2,1)}, bf16[1024,512]{1,0:T(8,128)(2,1)}, bf16[1024,512]{1,0:T(8,128)(2,1)}) custom-call(s32[1024]{0:T(1024)} %bitcast.271, f32[8]{0:T(128)} %multiply_exponential_fusion.slope_ref, s32[1024,128]{1,0:T(8,128)} %broadcast_in_dim.17.col_ref, s32[1,1024]{1,0:T(1,128)} %row_ref.3, ...), custom_call_target="tpu_custom_call" | custom-call | tf_op jit(solution)/shard_map/attention_backward/pallas_call | solution.py:233
  511.8 5.6 fusion.46
  517.4 5.7 fusion.17
  523.1 5.6 fusion.19
  558.8 11.9 %add_add_fusion = f32[1024,2048]{1,0:T(8,128)S(1)} fusion(f32[1024,2048]{1,0:T(8,128)} %fusion.46, f32[1024,2048]{1,0:T(8,128)} %fusion.17, f32[1024,2048]{1,0:T(8,128)} %fusion.19, bf16[1024,512]{1,0:T(8,128)(2,1)S(1)} %copy-done.13, bf16[3,2048,512]{2,1,0:T(8,128)(2,1)} %bitcast.256), kind=kOutput, calls=%fused_computation.8 | convolution fusion | flops 2153775104 | bytes 36700160 | tf_op jit(solution)/shard_map/dot_general | solution.py:40
  572.3 9.3 %add_add_fusion.2 = f32[512,2048]{1,0:T(8,128)S(1)} fusion(f32[512,2048]{1,0:T(8,128)S(1)} %copy-done.22, f32[512,2048]{1,0:T(8,128)} %fusion.100, bf16[512,2048]{1,0:T(8,128)(2,1)S(1)} %copy-done.17, bf16[2048,2048]{1,0:T(8,128)(2,1)} %all-gather.16.cloned.1.call-done), kind=kOutput, calls=%fused_computation.12 | convolution fusion | flops 4297064448 | bytes 23068672 | tf_op jit(solution)/shard_map/dot_general | solution.py:36
  583.8 24.6 %collective-permute-done.23 = bf16[256,2048]{1,0:T(8,128)(2,1)S(1)} collective-permute-done((bf16[256,2048]{1,0:T(8,128)(2,1)S(1)}, bf16[256,2048]{1,0:T(8,128)(2,1)S(1)}, u32[]{:S(2)}, u32[]{:S(2)}) %collective-permute-start.23) | collective-permute-done | bytes 1048608 | tf_op jit(solution)/shard_map/ppermute | solution.py:49
  609.3 32.9 %collective-permute-done.16 = bf16[256,2048]{1,0:T(8,128)(2,1)S(1)} collective-permute-done((bf16[256,2048]{1,0:T(8,128)(2,1)S(1)}, bf16[256,2048]{1,0:T(8,128)(2,1)S(1)}, u32[]{:S(2)}, u32[]{:S(2)}) %collective-permute-start.16) | collective-permute-done | bytes 1048608 | tf_op jit(solution)/shard_map/ppermute | solution.py:49
  643.6 15.5 %collective-permute-done.22 = bf16[256,2048]{1,0:T(8,128)(2,1)S(1)} collective-permute-done((bf16[256,2048]{1,0:T(8,128)(2,1)S(1)}, bf16[256,2048]{1,0:T(8,128)(2,1)S(1)}, u32[]{:S(2)}, u32[]{:S(2)}) %collective-permute-start.22) | collective-permute-done | bytes 1048608 | tf_op jit(solution)/shard_map/ppermute | solution.py:49
  (332 shorter events, 239.2 us)
Async XLA Ops:
  7.2 304.5 %all-gather.8.cloned.1.call-start = ((), (), s32[]{:S(2)}) async-start(), calls=%async_computation | async-start | bytes 2359296 | tf_op jit(solution)/shard_map/all_gather | solution.py:299
  18.3 298.4 %all-gather.10.cloned.1.call-start = ((), (), s32[]{:S(2)}) async-start(), calls=%async_computation.1 | async-start | bytes 2359296 | tf_op jit(solution)/shard_map/all_gather | solution.py:299
  18.4 14.2 %collective-permute-start.6 = (bf16[64,2048]{1,0:T(8,128)(2,1)S(1)}, bf16[64,2048]{1,0:T(8,128)(2,1)}, u32[]{:S(2)}, u32[]{:S(2)}) collective-permute-start(bf16[64,2048]{1,0:T(8,128)(2,1)S(1)} %constant_dynamic-slice_fusion.4), channel_id=1, source_target_pairs={{0,2},{1,3},{2,0},{3,1},{4,6},{5,7},{6,4},{7,5},{8,10},{9,11},{10,... | collective-permute-start | bytes 786440 | tf_op jit(solution)/shard_map/ppermute | solution.py:49
  32.6 289.3 %all-gather.12.cloned.1.call-start = ((), (), s32[]{:S(2)}) async-start(), calls=%async_computation.2 | async-start | bytes 2359296 | tf_op jit(solution)/shard_map/all_gather | solution.py:299
  40.9 334.0 %all-gather.14.cloned.1.call-start = ((), (), s32[]{:S(2)}) async-start(), calls=%async_computation.3 | async-start | bytes 9437184 | tf_op jit(solution)/shard_map/all_gather | solution.py:300
  42.3 48.5 %collective-permute-start.12 = (bf16[256,2048]{1,0:T(8,128)(2,1)S(1)}, bf16[256,2048]{1,0:T(8,128)(2,1)}, u32[]{:S(2)}, u32[]{:S(2)}) collective-permute-start(bf16[256,2048]{1,0:T(8,128)(2,1)S(1)} %constant_dynamic-slice_fusion.2), channel_id=1, source_target_pairs={{0,2},{1,3},{2,0},{3,1},{4,6},{5,7},{6,4},{7,5},{8,10},{9,11},{10,... | collective-permute-start | bytes 3145736 | tf_op jit(solution)/shard_map/ppermute | solution.py:49
  90.9 294.3 %all-gather.16.cloned.1.call-start = ((), (), s32[]{:S(2)}) async-start(), calls=%async_computation.4 | async-start | bytes 9437184 | tf_op jit(solution)/shard_map/all_gather | solution.py:301
  90.9 48.5 %collective-permute-start = (bf16[256,2048]{1,0:T(8,128)(2,1)S(1)}, bf16[256,2048]{1,0:T(8,128)(2,1)}, u32[]{:S(2)}, u32[]{:S(2)}) collective-permute-start(bf16[256,2048]{1,0:T(8,128)(2,1)S(1)} %copy-done.5), channel_id=1, source_target_pairs={{0,1},{1,0},{2,3},{3,2},{4,5},{5,4},{6,7},{7,6},{8,9},{9,8},{10,11... | collective-permute-start | bytes 3145736 | tf_op jit(solution)/shard_map/ppermute | solution.py:49
  91.6 50.2 %collective-permute-start.1 = (bf16[256,2048]{1,0:T(8,128)(2,1)S(1)}, bf16[256,2048]{1,0:T(8,128)(2,1)}, u32[]{:S(2)}, u32[]{:S(2)}) collective-permute-start(bf16[256,2048]{1,0:T(8,128)(2,1)S(1)} %copy-done.5), channel_id=1, source_target_pairs={{0,2},{1,3},{2,0},{3,1},{4,6},{5,7},{6,4},{7,5},{8,10},{9,11},{10,... | collective-permute-start | bytes 3145736 | tf_op jit(solution)/shard_map/ppermute | solution.py:49
  96.4 200.3 %collective-permute-start.9 = (bf16[16,512]{1,0:T(8,128)(2,1)S(1)}, bf16[16,512]{1,0:T(8,128)(2,1)}, u32[]{:S(2)}, u32[]{:S(2)}) collective-permute-start(bf16[16,512]{1,0:T(8,128)(2,1)S(1)} %dynamic-slice_bitcast_fusion.3), channel_id=1, source_target_pairs={{0,1},{1,0},{2,3},{3,2},{4,5},{5,4},{6,7},{7,6},{8,9},{9,8},{10,11... | collective-permute-start | bytes 49160 | tf_op jit(solution)/shard_map/ppermute | solution.py:49
  96.5 92.2 %collective-permute-start.17 = (bf16[256,2048]{1,0:T(8,128)(2,1)}, bf16[256,2048]{1,0:T(8,128)(2,1)}, u32[]{:S(2)}, u32[]{:S(2)}) collective-permute-start(bf16[256,2048]{1,0:T(8,128)(2,1)} %param.39), channel_id=1, source_target_pairs={{0,1},{1,0},{2,3},{3,2},{4,5},{5,4},{6,7},{7,6},{8,9},{9,8},{10,11... | collective-permute-start | bytes 3145736 | tf_op jit(solution)/shard_map/ppermute | solution.py:49
  100.7 84.9 %collective-permute-start.14 = (bf16[256,2048]{1,0:T(8,128)(2,1)}, bf16[256,2048]{1,0:T(8,128)(2,1)}, u32[]{:S(2)}, u32[]{:S(2)}) collective-permute-start(bf16[256,2048]{1,0:T(8,128)(2,1)} %constant_dynamic-slice_fusion.1), channel_id=1, source_target_pairs={{0,2},{1,3},{2,0},{3,1},{4,6},{5,7},{6,4},{7,5},{8,10},{9,11},{10,... | collective-permute-start | bytes 3145736 | tf_op jit(solution)/shard_map/ppermute | solution.py:49
  139.4 47.1 %collective-permute-start.10 = (bf16[16,512]{1,0:T(8,128)(2,1)S(1)}, bf16[16,512]{1,0:T(8,128)(2,1)}, u32[]{:S(2)}, u32[]{:S(2)}) collective-permute-start(bf16[16,512]{1,0:T(8,128)(2,1)S(1)} %dynamic-slice_bitcast_fusion.3), channel_id=1, source_target_pairs={{0,2},{1,3},{2,0},{3,1},{4,6},{5,7},{6,4},{7,5},{8,10},{9,11},{10,... | collective-permute-start | bytes 49160 | tf_op jit(solution)/shard_map/ppermute | solution.py:49
  141.7 67.0 %collective-permute-start.2 = (bf16[256,2048]{1,0:T(8,128)(2,1)}, bf16[256,2048]{1,0:T(8,128)(2,1)S(1)}, u32[]{:S(2)}, u32[]{:S(2)}) collective-permute-start(bf16[256,2048]{1,0:T(8,128)(2,1)} %collective-permute-done.1), channel_id=1, source_target_pairs={{0,1},{1,0},{2,3},{3,2},{4,5},{5,4},{6,7},{7,6},{8,9},{9,8},{10,11... | collective-permute-start | bytes 3145736 | tf_op jit(solution)/shard_map/ppermute | solution.py:49
  185.6 170.9 %collective-permute-start.13 = (bf16[16,2048]{1,0:T(8,128)(2,1)S(1)}, bf16[16,2048]{1,0:T(8,128)(2,1)S(1)}, u32[]{:S(2)}, u32[]{:S(2)}) collective-permute-start(bf16[16,2048]{1,0:T(8,128)(2,1)S(1)} %dynamic-slice_bitcast_fusion.1), channel_id=1, source_target_pairs={{0,2},{1,3},{2,0},{3,1},{4,6},{5,7},{6,4},{7,5},{8,10},{9,11},{10,... | collective-permute-start | bytes 196616 | tf_op jit(solution)/shard_map/ppermute | solution.py:49
  186.5 475.2 %all-gather.18.cloned.1.call-start = ((), (), s32[]{:S(2)}) async-start(), calls=%async_computation.5 | async-start | bytes 4165632 | tf_op jit(solution)/shard_map/all_gather | solution.py:397
  186.5 82.7 %collective-permute-start.15 = (bf16[16,2048]{1,0:T(8,128)(2,1)S(1)}, bf16[16,2048]{1,0:T(8,128)(2,1)S(1)}, u32[]{:S(2)}, u32[]{:S(2)}) collective-permute-start(bf16[16,2048]{1,0:T(8,128)(2,1)S(1)} %dynamic-slice_bitcast_fusion), channel_id=1, source_target_pairs={{0,2},{1,3},{2,0},{3,1},{4,6},{5,7},{6,4},{7,5},{8,10},{9,11},{10,... | collective-permute-start | bytes 196616 | tf_op jit(solution)/shard_map/ppermute | solution.py:49
  188.7 110.8 %collective-permute-start.11 = (bf16[16,512]{1,0:T(8,128)(2,1)}, bf16[16,512]{1,0:T(8,128)(2,1)}, u32[]{:S(2)}, u32[]{:S(2)}) collective-permute-start(bf16[16,512]{1,0:T(8,128)(2,1)} %collective-permute-done.10), channel_id=1, source_target_pairs={{0,1},{1,0},{2,3},{3,2},{4,5},{5,4},{6,7},{7,6},{8,9},{9,8},{10,11... | collective-permute-start | bytes 49160 | tf_op jit(solution)/shard_map/ppermute | solution.py:49
  266.7 25.9 %collective-permute-start.5 = (bf16[512,512]{1,0:T(8,128)(2,1)S(1)}, bf16[512,512]{1,0:T(8,128)(2,1)}, u32[]{:S(2)}, u32[]{:S(2)}) collective-permute-start(bf16[512,512]{1,0:T(8,128)(2,1)S(1)} %get-tuple-element.69), channel_id=1, source_target_pairs={{0,2},{1,3},{2,0},{3,1},{4,6},{5,7},{6,4},{7,5},{8,10},{9,11},{10,... | collective-permute-start | bytes 1572872 | tf_op jit(solution)/shard_map/ppermute | solution.py:49
  272.0 24.9 %collective-permute-start.3 = (bf16[512,512]{1,0:T(8,128)(2,1)}, bf16[512,512]{1,0:T(8,128)(2,1)}, u32[]{:S(2)}, u32[]{:S(2)}) collective-permute-start(bf16[512,512]{1,0:T(8,128)(2,1)} %get-tuple-element.70), channel_id=1, source_target_pairs={{0,1},{1,0},{2,3},{3,2},{4,5},{5,4},{6,7},{7,6},{8,9},{9,8},{10,11... | collective-permute-start | bytes 1572872 | tf_op jit(solution)/shard_map/ppermute | solution.py:49
  292.6 14.3 %collective-permute-start.7 = (bf16[512,512]{1,0:T(8,128)(2,1)}, bf16[512,512]{1,0:T(8,128)(2,1)}, u32[]{:S(2)}, u32[]{:S(2)}) collective-permute-start(bf16[512,512]{1,0:T(8,128)(2,1)} %collective-permute-done.5), channel_id=1, source_target_pairs={{0,1},{1,0},{2,3},{3,2},{4,5},{5,4},{6,7},{7,6},{8,9},{9,8},{10,11... | collective-permute-start | bytes 1572872 | tf_op jit(solution)/shard_map/ppermute | solution.py:49
  408.9 26.8 %collective-permute-start.18 = (bf16[256,2048]{1,0:T(8,128)(2,1)S(1)}, bf16[256,2048]{1,0:T(8,128)(2,1)S(1)}, u32[]{:S(2)}, u32[]{:S(2)}) collective-permute-start(bf16[256,2048]{1,0:T(8,128)(2,1)S(1)} %dynamic-slice_convert_fusion.2), channel_id=1, source_target_pairs={{0,1},{1,0},{2,3},{3,2},{4,5},{5,4},{6,7},{7,6},{8,9},{9,8},{10,11... | collective-permute-start | bytes 3145736 | tf_op jit(solution)/shard_map/ppermute | solution.py:49
  409.4 127.6 %collective-permute-start.34 = (bf16[16,2048]{1,0:T(8,128)(2,1)}, bf16[16,2048]{1,0:T(8,128)(2,1)}, u32[]{:S(2)}, u32[]{:S(2)}) collective-permute-start(bf16[16,2048]{1,0:T(8,128)(2,1)} %convolution_convert_fusion.1), channel_id=1, source_target_pairs={{0,2},{1,3},{2,0},{3,1},{4,6},{5,7},{6,4},{7,5},{8,10},{9,11},{10,... | collective-permute-start | bytes 196616 | tf_op jit(solution)/shard_map/ppermute | solution.py:49
  413.9 131.7 %collective-permute-start.35 = (bf16[16,2048]{1,0:T(8,128)(2,1)}, bf16[16,2048]{1,0:T(8,128)(2,1)}, u32[]{:S(2)}, u32[]{:S(2)}) collective-permute-start(bf16[16,2048]{1,0:T(8,128)(2,1)} %convolution_convert_fusion), channel_id=1, source_target_pairs={{0,2},{1,3},{2,0},{3,1},{4,6},{5,7},{6,4},{7,5},{8,10},{9,11},{10,... | collective-permute-start | bytes 196616 | tf_op jit(solution)/shard_map/ppermute | solution.py:49
  442.7 28.3 %collective-permute-start.21 = (bf16[256,512]{1,0:T(8,128)(2,1)S(1)}, bf16[256,512]{1,0:T(8,128)(2,1)S(1)}, u32[]{:S(2)}, u32[]{:S(2)}) collective-permute-start(bf16[256,512]{1,0:T(8,128)(2,1)S(1)} %fusion.26), channel_id=1, source_target_pairs={{0,3},{1,2},{2,1},{3,0},{4,7},{5,6},{6,5},{7,4},{8,11},{9,10},{10,... | collective-permute-start | bytes 786440 | tf_op jit(solution)/shard_map/ppermute | solution.py:49
  457.4 13.6 %collective-permute-start.20 = (bf16[256,512]{1,0:T(8,128)(2,1)S(1)}, bf16[256,512]{1,0:T(8,128)(2,1)S(1)}, u32[]{:S(2)}, u32[]{:S(2)}) collective-permute-start(bf16[256,512]{1,0:T(8,128)(2,1)S(1)} %fusion.25), channel_id=1, source_target_pairs={{0,2},{1,3},{2,0},{3,1},{4,6},{5,7},{6,4},{7,5},{8,10},{9,11},{10,... | collective-permute-start | bytes 786440 | tf_op jit(solution)/shard_map/ppermute | solution.py:49
  460.7 74.2 %collective-permute-start.31 = (bf16[16,512]{1,0:T(8,128)(2,1)}, bf16[16,512]{1,0:T(8,128)(2,1)}, u32[]{:S(2)}, u32[]{:S(2)}) collective-permute-start(bf16[16,512]{1,0:T(8,128)(2,1)} %convolution_convert_fusion.4), channel_id=1, source_target_pairs={{0,1},{1,0},{2,3},{3,2},{4,5},{5,4},{6,7},{7,6},{8,9},{9,8},{10,11... | collective-permute-start | bytes 49160 | tf_op jit(solution)/shard_map/ppermute | solution.py:49
  471.0 63.9 %collective-permute-start.33 = (bf16[16,512]{1,0:T(8,128)(2,1)}, bf16[16,512]{1,0:T(8,128)(2,1)}, u32[]{:S(2)}, u32[]{:S(2)}) collective-permute-start(bf16[16,512]{1,0:T(8,128)(2,1)} %fusion.32), channel_id=1, source_target_pairs={{0,2},{1,3},{2,0},{3,1},{4,6},{5,7},{6,4},{7,5},{8,10},{9,11},{10,... | collective-permute-start | bytes 49160 | tf_op jit(solution)/shard_map/ppermute | solution.py:49
  571.0 37.4 %collective-permute-start.23 = (bf16[256,2048]{1,0:T(8,128)(2,1)S(1)}, bf16[256,2048]{1,0:T(8,128)(2,1)S(1)}, u32[]{:S(2)}, u32[]{:S(2)}) collective-permute-start(bf16[256,2048]{1,0:T(8,128)(2,1)S(1)} %get-tuple-element.62), channel_id=1, source_target_pairs={{0,1},{1,0},{2,3},{3,2},{4,5},{5,4},{6,7},{7,6},{8,9},{9,8},{10,11... | collective-permute-start | bytes 3145736 | tf_op jit(solution)/shard_map/ppermute | solution.py:49
  581.7 60.4 %collective-permute-start.16 = (bf16[256,2048]{1,0:T(8,128)(2,1)S(1)}, bf16[256,2048]{1,0:T(8,128)(2,1)S(1)}, u32[]{:S(2)}, u32[]{:S(2)}) collective-permute-start(bf16[256,2048]{1,0:T(8,128)(2,1)S(1)} %dynamic-slice_convert_fusion.3), channel_id=1, source_target_pairs={{0,1},{1,0},{2,3},{3,2},{4,5},{5,4},{6,7},{7,6},{8,9},{9,8},{10,11... | collective-permute-start | bytes 3145736 | tf_op jit(solution)/shard_map/ppermute | solution.py:49
  582.6 76.4 %collective-permute-start.22 = (bf16[256,2048]{1,0:T(8,128)(2,1)S(1)}, bf16[256,2048]{1,0:T(8,128)(2,1)S(1)}, u32[]{:S(2)}, u32[]{:S(2)}) collective-permute-start(bf16[256,2048]{1,0:T(8,128)(2,1)S(1)} %get-tuple-element.61), channel_id=1, source_target_pairs={{0,1},{1,0},{2,3},{3,2},{4,5},{5,4},{6,7},{7,6},{8,9},{9,8},{10,11... | collective-permute-start | bytes 3145736 | tf_op jit(solution)/shard_map/ppermute | solution.py:49
  608.7 50.4 %collective-permute-start.24 = (bf16[256,2048]{1,0:T(8,128)(2,1)S(1)}, bf16[256,2048]{1,0:T(8,128)(2,1)S(1)}, u32[]{:S(2)}, u32[]{:S(2)}) collective-permute-start(bf16[256,2048]{1,0:T(8,128)(2,1)S(1)} %add_convert_fusion.1), channel_id=1, source_target_pairs={{0,2},{1,3},{2,0},{3,1},{4,6},{5,7},{6,4},{7,5},{8,10},{9,11},{10,... | collective-permute-start | bytes 3145736 | tf_op jit(solution)/shard_map/ppermute | solution.py:49
  (64 other events, 1208.6 us)
Sparse Core Ops, SparseCore 0:
  18.4 29.2 all-gather.7
  49.7 27.8 all-gather.9
  80.1 27.8 all-gather.11
  109.7 54.3 all-gather.13
  186.6 55.0 all-gather.15
  558.9 33.1 all-gather.17

commit v2 on v1

v2 whole, which is shorter than its diff:
```python
import functools

import jax
import jax.numpy as jnp
from jax import lax
from jax.experimental import pallas as pl
from jax.experimental.pallas import tpu as pltpu
from jax.sharding import PartitionSpec as P

HEADS = 32
HD = 64
LONGEST = 512
EPSILON = 1e-05
F32 = jnp.float32
BF16 = jnp.bfloat16
MASKED = -1e30
WHOLE = pl.BlockSpec(memory_space=pltpu.VMEM)
REMOTE = pl.BlockSpec(memory_space=pl.ANY)


def shape(dims, kind=BF16):
    return jax.ShapeDtypeStruct(dims, kind)


def statistics(values):
    center = jnp.mean(values, -1, keepdims=True)
    centred = values - center
    variance = jnp.mean(centred * centred, -1, keepdims=True)
    scaler = lax.rsqrt(variance + EPSILON)
    return centred * scaler, scaler


def layer_norm(values, gain, bias):
    return statistics(values)[0] * gain.astype(F32) + bias.astype(F32)


def norm_back(grad, values, gain):
    normal, scaler = statistics(values)
    scaled = grad * gain.astype(F32)
    first_mean = jnp.mean(scaled, -1, keepdims=True)
    second_mean = jnp.mean(scaled * normal, -1, keepdims=True)
    return (scaled - first_mean - normal * second_mean) * scaler


def by_rows(count, body, chunk=32):
    for i in range(count // chunk):
        body(slice(i * chunk, (i + 1) * chunk))


def dot_nn(left, right):
    return jnp.dot(left, right, preferred_element_type=F32)


def dot_nt(left, right):
    return lax.dot_general(left, right, (((1,), (1,)), ((), ())), preferred_element_type=F32)


def dot_tn(left, right):
    return lax.dot_general(left, right, (((0,), (0,)), ((), ())), preferred_element_type=F32)


def swap(value, axis, bit):
    pairs = [(i, i ^ bit) for i in range(lax.axis_size(axis))]
    return lax.ppermute(value, axis, pairs)


def after(value, *others):
    return lax.optimization_barrier((value, *others))[0]


def gelu_pair(values):
    below = 0.5 * (1.0 + lax.erf(values * 0.5 ** 0.5))
    density = jnp.exp(values * values * -0.5) * 0.3989422804014327
    return values * below, below + values * density


def project_kernel(kept, at_ref, x_ref, gain_ref, bias_ref, aq_ref, bq_ref, wq_ref, *refs):
    merged_ref, normed_ref, z_ref, w_ref, out_ref, low_ref, thin_ref, sems, loads = refs[kept:]
    count = x_ref.shape[0]
    weights = [pltpu.make_async_copy(wq_ref.at[i], w_ref.at[i], loads.at[i]) for i in range(wq_ref.shape[0])]
    for copy in weights:
        copy.start()
    rows = pl.ds(pl.multiple_of(at_ref[0] * count, count), count)

    def norm(part):
        low_ref[part, :] = layer_norm(x_ref[part, :].astype(F32), gain_ref[...], bias_ref[...]).astype(BF16)

    by_rows(count, norm)
    normed = low_ref[...]
    copies = [pltpu.make_async_copy(low_ref, normed_ref.at[rows, :], sems.at[0])]
    copies[0].start()
    inner = dot_nt(normed, aq_ref[...]).astype(BF16)
    thin_ref[...] = inner
    copies.append(pltpu.make_async_copy(thin_ref, z_ref.at[rows, :], sems.at[1]))
    copies[1].start()
    for i in range(wq_ref.shape[0]):
        weights[i].wait()
        out_ref[i] = (dot_nn(normed, w_ref[i]) + dot_nn(inner, bq_ref[i])).astype(BF16)
        copies.append(pltpu.make_async_copy(out_ref.at[i], merged_ref.at[i, rows, :], sems.at[2 + i]))
        copies[-1].start()
    for copy in copies:
        copy.wait()


def project(at, rows, gain, bias, aq, bq, wq, total, earlier):
    count, width = rows.shape
    parts, _, local_width = wq.shape
    rank = aq.shape[0]
    kept = len(earlier)
    return pl.pallas_call(
        functools.partial(project_kernel, kept),
        out_shape=(shape((parts, total, local_width)), shape((total, width)), shape((total, rank))),
        grid_spec=pltpu.PrefetchScalarGridSpec(
            num_scalar_prefetch=1,
            grid=(),
            in_specs=[WHOLE] * 5 + [REMOTE] * (1 + kept),
            out_specs=(REMOTE,) * 3,
            scratch_shapes=[
                pltpu.VMEM(wq.shape, BF16),
                pltpu.VMEM((parts, count, local_width), BF16),
                pltpu.VMEM((count, width), BF16),
                pltpu.VMEM((count, rank), BF16),
                pltpu.SemaphoreType.DMA((2 + parts,)),
                pltpu.SemaphoreType.DMA((parts,)),
            ],
        ),
        input_output_aliases={7 + i: i for i in range(kept)},
        name="project",
    )(at.reshape(1), rows, gain, bias, aq, bq, wq, *earlier)


def lane_mask(half):
    return (lax.broadcasted_iota(jnp.int32, (1, 2 * HD), 1) // HD) == half


def pair_scores(keys, query, seg_col, seg_row, slope, apart):
    rows, cols = keys.shape[0], query.shape[0]
    raw = dot_nt(keys, query)
    delta = (
        lax.broadcasted_iota(jnp.int32, (rows, cols), 0)
        - lax.broadcasted_iota(jnp.int32, (rows, cols), 1)
        - apart
    )
    allowed = seg_col == seg_row
    if apart == 0:
        allowed = allowed & (delta <= 0)
    return jnp.where(allowed, raw + slope * delta.astype(F32), MASKED)


def reach_of(block):
    return -(-LONGEST // block)


def attend_kernel(block, count, first_ref, seg_ref, slope_ref, col_ref, row_ref, q_ref, k_ref, v_ref,
                  o_ref, stat_ref, turned_ref, top_ref, total_ref, sum_ref):
    head = pl.program_id(0)
    half = lax.rem(head, 2)
    slope = slope_ref[head]
    mask = lane_mask(half)
    heads_rows = pl.ds(pl.multiple_of(half * HD, HD), HD)

    @pl.when(half == 0)
    def _():
        turned_ref[...] = v_ref[0].T

    for own in range(count):
        i = first_ref[0] + own
        start = pl.multiple_of(i * block, block)
        here = pl.ds(own * block, block)
        scaled = jnp.where(mask, q_ref[0, pl.ds(start, block), :] * HD ** -0.5, 0).astype(BF16)
        row = row_ref[:, pl.ds(start, block)]

        def one(back):
            at = pl.multiple_of(start - back * block, block)
            keys = pl.ds(at, block)
            scores = pair_scores(k_ref[0, keys, :], scaled, col_ref[keys, :1], row, slope, back * block)
            best = jnp.max(scores, 0, keepdims=True)
            if back:
                best = jnp.maximum(best, top_ref[...])
            weights = jnp.exp(scores - best)
            total = jnp.sum(weights, 0, keepdims=True)
            result = dot_nn(turned_ref[heads_rows, keys], weights.astype(BF16))
            if back:
                fade = jnp.exp(top_ref[...] - best)
                total = total + fade * total_ref[...]
                result = result + fade * sum_ref[...]
            top_ref[...] = best
            total_ref[...] = total
            sum_ref[...] = result

        one(0)
        for back in range(1, reach_of(block) + 1):
            last = jnp.maximum(start - (back - 1) * block - 1, 0)

            @pl.when((i >= back) & (seg_ref[last] == seg_ref[start]))
            def _(back=back):
                one(back)

        stat_ref[0, :, here] = top_ref[...] + jnp.log(total_ref[...])
        done = (sum_ref[...] / total_ref[...]).T
        both = jnp.concatenate([done, done], 1)
        o_ref[here, :] = jnp.where(mask, both, o_ref[here, :].astype(F32)).astype(BF16)


def attend(first, merged, seg, slopes, count):
    _, rows, width = merged.shape
    block = min(256, rows)
    heads = width // HD
    col = jnp.broadcast_to(seg[:, None], (rows, 128))

    def part(i):
        return pl.BlockSpec((1, rows, 2 * HD), lambda h, *_: (i, 0, h // 2))

    return pl.pallas_call(
        functools.partial(attend_kernel, block, count),
        out_shape=(shape((count * block, width)), shape((heads, 1, count * block), F32)),
        grid_spec=pltpu.PrefetchScalarGridSpec(
            num_scalar_prefetch=3,
            grid=(heads,),
            in_specs=[
                pl.BlockSpec((rows, 128), lambda h, *_: (0, 0)),
                pl.BlockSpec((1, rows), lambda h, *_: (0, 0)),
                part(0), part(1), part(2),
            ],
            out_specs=(
                pl.BlockSpec((count * block, 2 * HD), lambda h, *_: (0, h // 2)),
                pl.BlockSpec((1, 1, count * block), lambda h, *_: (h, 0, 0)),
            ),
            scratch_shapes=[
                pltpu.VMEM((2 * HD, rows), BF16),
                pltpu.VMEM((1, block), F32),
                pltpu.VMEM((1, block), F32),
                pltpu.VMEM((HD, block), F32),
            ],
        ),
        name="attend",
    )(first.reshape(1), seg, slopes, col, seg[None, :], merged, merged, merged)


def attend_back_kernel(block, seg_ref, slope_ref, col_ref, row_ref, stat_ref, m_ref, g_ref, q_ref, k_ref, v_ref,
                       d_ref, turned_ref, center_ref, qsum_ref, ksum_ref, vsum_ref):
    head = pl.program_id(0)
    half = lax.rem(head, 2)
    slope = slope_ref[head]
    count = g_ref.shape[0] // block
    mask = lane_mask(half)
    rows = pl.ds(pl.multiple_of(half * HD, HD), HD)

    @pl.when(half == 0)
    def _():
        turned_ref[...] = k_ref[0].T
        product = (g_ref[...].astype(F32) * m_ref[...].astype(F32)).T
        center_ref[0:1] = jnp.sum(product[:HD], 0, keepdims=True)
        center_ref[1:2] = jnp.sum(product[HD:], 0, keepdims=True)
        qsum_ref[...] = jnp.zeros_like(qsum_ref)
        ksum_ref[...] = jnp.zeros_like(ksum_ref)
        vsum_ref[...] = jnp.zeros_like(vsum_ref)

    for i in range(count):
        queries = pl.ds(i * block, block)
        scaled = jnp.where(mask, q_ref[0, queries, :] * HD ** -0.5, 0).astype(BF16)
        grads = jnp.where(mask, g_ref[queries, :], 0).astype(BF16)
        row = row_ref[:, queries]

        def one(j):
            keys = pl.ds(j * block, block)
            scores = pair_scores(k_ref[0, keys, :], scaled, col_ref[keys, :1], row, slope, (i - j) * block)
            probs = jnp.exp(scores - stat_ref[0, :, queries])
            d_probs = dot_nt(v_ref[0, keys, :], grads)
            d_scores = (probs * (d_probs - center_ref[pl.ds(half, 1), queries])).astype(BF16)
            vsum_ref[keys, :] += dot_nn(probs.astype(BF16), grads)
            ksum_ref[keys, :] += dot_nn(d_scores, scaled)
            qsum_ref[rows, queries] += dot_nn(turned_ref[rows, keys], d_scores)

        one(i)
        for back in range(1, min(i, reach_of(block)) + 1):
            j = i - back

            @pl.when(seg_ref[j * block + block - 1] == seg_ref[i * block])
            def _(j=j):
                one(j)

    @pl.when(half == 1)
    def _():
        d_ref[0] = (qsum_ref[...] * HD ** -0.5).T.astype(BF16)
        d_ref[1] = ksum_ref[...].astype(BF16)
        d_ref[2] = vsum_ref[...].astype(BF16)


def attend_back(merged, mixed, grad, stat, seg, slopes):
    parts, rows, width = merged.shape
    block = min(256, rows)
    wide = pl.BlockSpec((rows, 2 * HD), lambda h, *_: (0, h // 2))
    col = jnp.broadcast_to(seg[:, None], (rows, 128))

    def part(i):
        return pl.BlockSpec((1, rows, 2 * HD), lambda h, *_: (i, 0, h // 2))

    return pl.pallas_call(
        functools.partial(attend_back_kernel, block),
        out_shape=shape(merged.shape),
        grid_spec=pltpu.PrefetchScalarGridSpec(
            num_scalar_prefetch=2,
            grid=(width // HD,),
            in_specs=[
                pl.BlockSpec((rows, 128), lambda h, *_: (0, 0)),
                pl.BlockSpec((1, rows), lambda h, *_: (0, 0)),
                pl.BlockSpec((1, 1, rows), lambda h, *_: (h, 0, 0)),
                wide, wide, part(0), part(1), part(2),
            ],
            out_specs=pl.BlockSpec((parts, rows, 2 * HD), lambda h, *_: (0, 0, h // 2)),
            scratch_shapes=[
                pltpu.VMEM((2 * HD, rows), BF16),
                pltpu.VMEM((2, rows), F32),
                pltpu.VMEM((2 * HD, rows), F32),
                pltpu.VMEM((rows, 2 * HD), F32),
                pltpu.VMEM((rows, 2 * HD), F32),
            ],
        ),
        name="attend_back",
    )(seg, slopes, col, seg[None, :], stat, mixed, grad, merged, merged, merged)


def dense_kernel(at_ref, x0_ref, x1_ref, m0_ref, m1_ref, m2_ref, m3_ref, a_ref, bd_ref, gain_ref, bias_ref, au_ref,
                 own_ref, far_ref, middle_ref, second_ref, zd_ref, zu_ref, w_ref, m_ref, loads):
    size = m0_ref.shape[1]
    count = x0_ref.shape[0]
    width = x0_ref.shape[1]
    pieces, _, thick, _ = far_ref.shape
    copies = [pltpu.make_async_copy(own_ref.reshape(pieces, thick, width), w_ref.at[0], loads.at[0])]
    copies += [pltpu.make_async_copy(far_ref.at[:, r], w_ref.at[1 + r], loads.at[1 + r]) for r in range(3)]
    for copy in copies:
        copy.start()
    for r, m in enumerate((m0_ref, m1_ref, m2_ref, m3_ref)):
        m_ref[:, r * size:(r + 1) * size] = m[...]
    inner = dot_nt(m_ref[...], a_ref[...]).astype(BF16)
    zd_ref[...] = inner
    for copy in copies:
        copy.wait()
    weights = w_ref[...].reshape(4 * size, width)
    swapped = at_ref[0] == 1
    tile = min(512, width)
    for i in range(2):
        rows = slice(i * count, (i + 1) * count)
        near, away = (x0_ref, x1_ref) if i == 0 else (x1_ref, x0_ref)
        for j in range(width // tile):
            cols = slice(j * tile, (j + 1) * tile)
            x = jnp.where(swapped, away[:, cols], near[:, cols]).astype(F32)
            middle_ref[rows, cols] = x + dot_nn(m_ref[rows, :], weights[:, cols]) + dot_nn(inner[rows], bd_ref[:, cols])

    def norm(part):
        second_ref[part, :] = layer_norm(middle_ref[part, :], gain_ref[...], bias_ref[...]).astype(BF16)

    by_rows(2 * count, norm)
    zu_ref[...] = dot_nt(second_ref[...], au_ref[...]).astype(BF16)


def dense(low, x_own, x_far, m_parts, ad, bd, gain, bias, au, w_own, w_far):
    count, width = x_own.shape
    rank = ad.shape[0]
    return pl.pallas_call(
        dense_kernel,
        out_shape=(
            shape((2 * count, width), F32), shape((2 * count, width)), shape((2 * count, rank)),
            shape((2 * count, rank)),
        ),
        in_specs=[pl.BlockSpec(memory_space=pltpu.SMEM)] + [WHOLE] * 11 + [REMOTE] * 2,
        out_specs=(WHOLE,) * 4,
        scratch_shapes=[
            pltpu.VMEM((4, w_far.shape[0]) + w_far.shape[2:], BF16), pltpu.VMEM((2 * count, width), BF16),
            pltpu.SemaphoreType.DMA((4,)),
        ],
        name="dense",
    )(low.reshape(1), x_own, x_far, *m_parts, ad, bd, gain, bias, au, w_own, w_far)


def feed_kernel(earlier, at_ref, x_ref, g_ref, up_ref, down_ref, zu_ref, dz_ref, bu_ref, an_ref, au_ref, *refs):
    step = pl.program_id(0)
    total_ref, inner_ref = refs[-2:]
    if earlier:
        before_ref, active_ref, hidden_ref, dz_out_ref, out_ref = refs[:-2]
    else:
        active_ref, hidden_ref, dz_out_ref, out_ref = refs[:-2]

    @pl.when(step == 0)
    def _():
        total_ref[...] = before_ref[...] if earlier else jnp.zeros_like(total_ref)
        inner_ref[...] = jnp.zeros_like(inner_ref)

    hidden = dot_nn(x_ref[...], up_ref[...]) + dot_nn(zu_ref[...], bu_ref[...])
    d_active = dot_nt(g_ref[...], down_ref[...]) + dot_nn(dz_ref[...], an_ref[...])
    active, slope = gelu_pair(hidden)
    active_ref[...] = active.astype(BF16)
    d_hidden = (d_active * slope).astype(BF16)
    hidden_ref[...] = d_hidden
    total_ref[...] += dot_nt(d_hidden, up_ref[...])
    inner_ref[...] += dot_nt(d_hidden, bu_ref[...])

    @pl.when(step == pl.num_programs(0) - 1)
    def _():
        inner = inner_ref[...].astype(BF16)
        dz_out_ref[...] = inner
        out_ref[...] = (total_ref[...] + dot_nn(inner, au_ref[...])).astype(out_ref.dtype)


def feed(at, count, x, g, up, down, zu, dz, bu, an, au, before, kind):
    width = x.shape[1]
    ff = up.shape[1]
    tile = min(512, ff)
    rank = bu.shape[0]
    earlier = before is not None
    once = pl.Buffered(1)
    rows = pl.BlockSpec((count, width), lambda t, at: (at[0], 0), pipeline_mode=once)
    thin = pl.BlockSpec((count, rank), lambda t, at: (at[0], 0))
    cols = pl.BlockSpec((count, tile), lambda t, at: (0, t))
    row = pl.BlockSpec((rank, tile), lambda t, at: (0, t))
    return pl.pallas_call(
        functools.partial(feed_kernel, earlier),
        out_shape=(shape((count, ff)), shape((count, ff)), shape((count, rank)), shape((count, width), kind)),
        grid_spec=pltpu.PrefetchScalarGridSpec(
            num_scalar_prefetch=1,
            grid=(ff // tile,),
            in_specs=[
                rows, rows, pl.BlockSpec((width, tile), lambda t, at: (0, t)),
                pl.BlockSpec((tile, width), lambda t, at: (t, 0)), thin, thin, row, row,
                pl.BlockSpec((rank, width), lambda t, at: (0, 0)),
            ] + [rows] * earlier,
            out_specs=(
                cols, cols, pl.BlockSpec((count, rank), lambda t, at: (0, 0)),
                pl.BlockSpec((count, width), lambda t, at: (0, 0), pipeline_mode=once),
            ),
            scratch_shapes=[pltpu.VMEM((count, width), F32), pltpu.VMEM((count, rank), F32)],
        ),
        name="feed",
    )(at.reshape(1), x, g, up, down, zu, dz, bu, an, au, *((before,) if earlier else ()))


def emit_kernel(earlier, at_ref, *refs):
    parts = 2 if earlier else 1
    step = pl.program_id(0)
    total_ref, inner_ref = refs[-2:]
    actives, hiddens, zs, ds = (refs[i * parts:(i + 1) * parts] for i in range(4))
    down_ref, an_ref, bn_ref = refs[4 * parts:4 * parts + 3]
    outs = refs[4 * parts + 3:-2]
    if earlier:
        befores, outs = outs[:2], outs[2:]
    gn_ref, gu_ref, z_ref = outs[:3]
    count = actives[0].shape[0]
    gn, gu = 0.0, 0.0
    for i in range(parts):
        rows = slice(i * count, (i + 1) * count)

        @pl.when(step == 0)
        def _():
            total_ref[rows] = befores[i][...] if earlier else jnp.zeros((count, total_ref.shape[1]), F32)
            inner_ref[rows] = jnp.zeros((count, inner_ref.shape[1]), F32)

        active = actives[i][...]
        total_ref[rows] += dot_nn(active, down_ref[...])
        inner_ref[rows] += dot_nt(active, an_ref[...])
        gn = gn + dot_tn(ds[i][...], active)
        gu = gu + dot_tn(zs[i][...], hiddens[i][...])
    gn_ref[...] = gn.astype(BF16)
    gu_ref[...] = gu.astype(BF16)

    @pl.when(step == pl.num_programs(0) - 1)
    def _():
        inner = inner_ref[...].astype(BF16)
        z_ref[...] = inner
        for i in range(parts):
            rows = slice(i * count, (i + 1) * count)
            out = outs[3 + i]
            out[...] = (total_ref[rows] + dot_nn(inner[rows], bn_ref[...])).astype(out.dtype)


def emit(low, actives, hiddens, down, an, bn, zu, dz, before):
    parts = len(actives)
    count, ff = actives[0].shape
    width = down.shape[1]
    tile = min(512, ff)
    rank = an.shape[0]
    earlier = before is not None
    once = pl.Buffered(1)
    places = (lambda at: 1 - at[0], lambda at: at[0]) if earlier else (lambda at: 0,)
    cols = pl.BlockSpec((count, tile), lambda t, at: (0, t))
    row = pl.BlockSpec((rank, tile), lambda t, at: (0, t))
    thin = [pl.BlockSpec((count, rank), lambda t, at, p=p: (p(at), 0)) for p in places]
    wide = [pl.BlockSpec((count, width), lambda t, at, p=p: (p(at), 0), pipeline_mode=once) for p in places]
    kinds = (BF16, F32) if earlier else (F32,)
    return pl.pallas_call(
        functools.partial(emit_kernel, earlier),
        out_shape=(
            shape((rank, ff)), shape((rank, ff)), shape((parts * count, rank)),
        ) + tuple(shape((count, width), k) for k in kinds),
        grid_spec=pltpu.PrefetchScalarGridSpec(
            num_scalar_prefetch=1,
            grid=(ff // tile,),
            in_specs=[cols] * (2 * parts) + thin * 2 + [
                pl.BlockSpec((tile, width), lambda t, at: (t, 0)), row,
                pl.BlockSpec((rank, width), lambda t, at: (0, 0)),
            ] + wide * earlier,
            out_specs=(
                row, row, pl.BlockSpec((parts * count, rank), lambda t, at: (0, 0)),
            ) + (pl.BlockSpec((count, width), lambda t, at: (0, 0), pipeline_mode=once),) * parts,
            scratch_shapes=[pltpu.VMEM((parts * count, width), F32), pltpu.VMEM((parts * count, rank), F32)],
        ),
        name="emit",
    )(low.reshape(1), *actives, *hiddens, *([zu] * parts), *([dz] * parts), down, an, bn, *([before] * parts * earlier))


def dense_back_kernel(low_ref, own_ref, far_ref, cot_ref, gain_ref, bd_ref, ad_ref, middle_ref, w0_ref, w1_ref,
                      d_ref, low_out_ref, dz_ref, mixed_ref, mid_ref, w_ref, loads):
    count, width = own_ref.shape
    size = mixed_ref.shape[2]
    pieces, _, thick, _ = w1_ref.shape
    rows = pl.ds(pl.multiple_of(low_ref[0] * count, count), count)
    first = pltpu.make_async_copy(middle_ref.at[rows, :], mid_ref, loads.at[4])
    first.start()
    copies = [pltpu.make_async_copy(w0_ref.reshape(pieces, thick, width), w_ref.at[0], loads.at[0])]
    copies += [pltpu.make_async_copy(w1_ref.at[:, r], w_ref.at[1 + r], loads.at[1 + r]) for r in range(3)]
    order = (3, 2, 1, 0)
    for r in order:
        copies[r].start()
    first.wait()

    def norm(part):
        grad = own_ref[part, :] + far_ref[part, :].astype(F32)
        d_middle = cot_ref[part, :].astype(F32) + norm_back(grad, mid_ref[part, :], gain_ref[...])
        d_ref[part, :] = d_middle
        low_out_ref[part, :] = d_middle.astype(BF16)

    by_rows(count, norm)
    low = low_out_ref[...]
    inner = dot_nt(low, bd_ref[...]).astype(BF16)
    dz_ref[...] = inner
    for r in order:
        copies[r].wait()
        cols = slice(r * size, (r + 1) * size)
        weights = w_ref[r].reshape(size, width)
        mixed_ref[r] = (dot_nt(low, weights) + dot_nn(inner, ad_ref[:, cols])).astype(BF16)


def dense_back(low, own, far, middle, cot, gain, bd, ad, w_own, w_far):
    count, width = own.shape
    rank = bd.shape[0]
    return pl.pallas_call(
        dense_back_kernel,
        out_shape=(shape((count, width), F32), shape((count, width)), shape((count, rank)), shape((4, count, width // 4))),
        in_specs=[pl.BlockSpec(memory_space=pltpu.SMEM)] + [WHOLE] * 6 + [REMOTE] * 3,
        out_specs=(WHOLE,) * 4,
        scratch_shapes=[
            pltpu.VMEM((count, width), F32), pltpu.VMEM((4, w_far.shape[0]) + w_far.shape[2:], BF16),
            pltpu.SemaphoreType.DMA((5,)),
        ],
        name="dense_back",
    )(low.reshape(1), own, far, cot, gain, bd, ad, middle, w_own, w_far)


def project_back_kernel(order, at_ref, aq_ref, bq_ref, d_ref, wq_ref, *refs):
    outs, part_ref, w_ref, sems, loads = refs[:-4], *refs[-4:]
    count = outs[0].shape[0]

    def fetch(place):
        rows = pl.ds(pl.multiple_of((at_ref[0] ^ order[place]) * count, count), count)
        return pltpu.make_async_copy(d_ref.at[:, rows, :], part_ref.at[place], sems.at[place])

    blocks = [fetch(place) for place in range(len(order))]
    weights = [pltpu.make_async_copy(wq_ref.at[i], w_ref.at[i], loads.at[i]) for i in range(3)]
    blocks[0].start()
    for copy in weights + blocks[1:]:
        copy.start()
    for place, out in enumerate(outs):
        blocks[place].wait()
        parts = [part_ref[place, i] for i in range(3)]
        inner = sum(dot_nt(d, bq_ref[i]) for i, d in enumerate(parts)).astype(BF16)
        total = dot_nn(inner, aq_ref[...])
        for i in range(3):
            if place == 0:
                weights[i].wait()
            total = total + dot_nt(parts[i], w_ref[i])
        out[...] = total.astype(out.dtype)


def project_back(at, d_merged, wq, aq, bq, order, kinds):
    parts, total, local_width = d_merged.shape
    width = wq.shape[1]
    count = total // 4
    return pl.pallas_call(
        functools.partial(project_back_kernel, order),
        out_shape=tuple(shape((count, width), k) for k in kinds),
        in_specs=[pl.BlockSpec(memory_space=pltpu.SMEM)] + [WHOLE] * 2 + [REMOTE] * 2,
        out_specs=(WHOLE,) * len(order),
        scratch_shapes=[
            pltpu.VMEM((len(order), parts, count, local_width), BF16), pltpu.VMEM(wq.shape, BF16),
            pltpu.SemaphoreType.DMA((len(order),)), pltpu.SemaphoreType.DMA((3,)),
        ],
        name="project_back",
    )(at.reshape(1), aq, bq, d_merged, wq)


def inner_kernel(d_ref, z_ref, n_ref, bq_ref, ga_ref, gb_ref):
    step = pl.program_id(0)

    @pl.when(step == 0)
    def _():
        ga_ref[...] = jnp.zeros_like(ga_ref)
        gb_ref[...] = jnp.zeros_like(gb_ref)

    inner = sum(dot_nt(d_ref[i], bq_ref[i]) for i in range(3)).astype(BF16)
    ga_ref[...] += dot_tn(inner, n_ref[...])
    width = d_ref.shape[2]
    for i in range(3):
        gb_ref[:, i * width:(i + 1) * width] += dot_tn(z_ref[...], d_ref[i])


def inner_grads(d_merged, z_qkv, normed, bq):
    parts, total, local_width = d_merged.shape
    width = normed.shape[1]
    rank = z_qkv.shape[1]
    count = total // 2
    return pl.pallas_call(
        inner_kernel,
        out_shape=(shape((rank, width), F32), shape((rank, parts * local_width), F32)),
        grid=(2,),
        in_specs=[
            pl.BlockSpec((parts, count, local_width), lambda i: (0, i, 0)),
            pl.BlockSpec((count, rank), lambda i: (i, 0)),
            pl.BlockSpec((count, width), lambda i: (i, 0)),
            pl.BlockSpec(bq.shape, lambda i: (0, 0, 0)),
        ],
        out_specs=(
            pl.BlockSpec((rank, width), lambda i: (0, 0)),
            pl.BlockSpec((rank, parts * local_width), lambda i: (0, 0)),
        ),
        name="inner_grads",
    )(d_merged, z_qkv, normed, bq)


def spread_kernel(ids_ref, first_ref, second_ref, *outs):
    step = pl.program_id(0)

    @pl.when(step == 0)
    def _():
        for out in outs:
            out[...] = jnp.zeros_like(out)

    which = ids_ref[step]
    ga_up, gb_down, gb_dense, gb_up, ga_down, ga_dense, ga_qkv, gb_qkv = outs
    at = 0
    for out in (ga_up, gb_down, gb_dense, gb_up, ga_down, ga_dense):
        size = out.shape[2]
        out[which] += first_ref[0, :, at:at + size].astype(F32)
        at += size
    size = ga_qkv.shape[2]
    ga_qkv[which] += second_ref[0, :, :size].astype(F32)
    local_width = gb_qkv.shape[3]
    for i in range(3):
        gb_qkv[which, i] += second_ref[0, :, size + i * local_width:size + (i + 1) * local_width].astype(F32)


def spread(ids, first, second, kinds, width, local_width, local_ff):
    copies, rank, _ = first.shape
    dims = [(kinds, rank, n) for n in (width, width, width, local_ff, local_ff, local_width, width)]
    dims.append((kinds, 3, rank, local_width))
    return pl.pallas_call(
        spread_kernel,
        out_shape=tuple(shape(d, F32) for d in dims),
        grid_spec=pltpu.PrefetchScalarGridSpec(
            num_scalar_prefetch=1,
            grid=(copies,),
            in_specs=[
                pl.BlockSpec((1,) + first.shape[1:], lambda s, _: (s, 0, 0)),
                pl.BlockSpec((1,) + second.shape[1:], lambda s, _: (s, 0, 0)),
            ],
            out_specs=tuple(
                pl.BlockSpec(d, lambda s, _, n=len(d): (0,) * n, pipeline_mode=pl.Buffered(1)) for d in dims
            ),
        ),
        name="spread",
    )(ids, first, second)


def turned(factor, which):
    return lax.dynamic_index_in_dim(factor.transpose(1, 2, 0), which, 0, False)


def local(
    layer_in, first_gain, first_bias, w_qkv, a_qkv, b_qkv, w_dense, a_dense, b_dense, second_gain, second_bias,
    w_up, a_up, b_up, w_down, a_down, b_down, segment_ids, adapter_ids, cotangent,
):
    own_rows, width = layer_in.shape
    kinds = a_qkv.shape[1]
    rank = a_qkv.shape[2]
    local_width = w_dense.shape[0]
    local_ff = w_up.shape[1]
    local_heads = local_width // HD
    index = lax.axis_index("mp")
    spot = lax.axis_index("dp")
    copies = lax.axis_size("dp")
    total_rows = 4 * own_rows
    low, high = index & 1, index >> 1
    which = adapter_ids[0]
    seg = segment_ids[0]
    head_ids = (index * local_heads + lax.iota(jnp.int32, local_heads)).astype(F32)
    slopes = jnp.exp2(-8.0 * (head_ids + 1.0) / HEADS)
    first_gain, first_bias, second_gain, second_bias = (
        v[None, :] for v in (first_gain, first_bias, second_gain, second_bias)
    )

    aq, ad, au, an = (turned(a, which) for a in (a_qkv, a_dense, a_up, a_down))
    bq = lax.dynamic_index_in_dim(b_qkv.transpose(0, 2, 1, 3), which, 0, False)
    bd, bu, bn = (lax.dynamic_index_in_dim(b, which, 0, False) for b in (b_dense, b_up, b_down))
    wq = w_qkv.transpose(1, 0, 2)

    def slice_of(weight):
        size = weight.shape[0] // copies
        return lax.dynamic_slice_in_dim(weight, spot * size, size, 0)

    x_one = swap(layer_in, "mp", 1)
    x_two = swap(layer_in, "mp", 2)
    wd_slice = slice_of(w_dense)
    size = wd_slice.shape[0]
    ad_flat = ad.reshape(-1, width)
    last = size + ad_flat.shape[0]
    tail = jnp.concatenate([wd_slice, ad_flat], 0)

    def step_in(r, block, held):
        return project(index ^ r, block, first_gain, first_bias, aq, bq, wq, total_rows, held)

    held = step_in(0, layer_in, ())
    wu_halves = jnp.split(slice_of(w_up), 2, axis=0)
    x_one, x_two, *held = lax.optimization_barrier((x_one, x_two, *held))

    x_three = swap(x_two, "mp", 1)
    pack_two = swap(after(jnp.concatenate([tail, bu, an], 0), x_one), "mp", 2)
    wu_first = swap(after(wu_halves[0], x_one), "mp", 2)
    held = step_in(1, x_one, held)
    held = step_in(2, x_two, held)
    x_three, pack_two, wu_first, *held = lax.optimization_barrier((x_three, pack_two, wu_first, *held))

    pack_one = swap(jnp.concatenate([tail, pack_two[:last]], 0), "mp", 1)
    wu_second = swap(after(wu_halves[1], x_three), "mp", 2)
    held = step_in(3, x_three, held)
    merged, normed, z_qkv = held
    other, stat_other = attend(2 * (1 - high), merged, seg, slopes, 2)
    other, pack_one, pack_two, wu_first, wu_second, merged = lax.optimization_barrier(
        (other, pack_one, pack_two, wu_first, wu_second, merged)
    )

    m_two = swap(other, "mp", 2)
    bu_far, an_far = pack_two[last:last + rank], pack_two[last + rank:]
    packs = (pack_one[:last], pack_two, pack_one[last:])
    wd_slices = jnp.concatenate([p[:size] for p in packs], 0)
    wd_far = lax.all_gather(wd_slices, "dp", axis=0).reshape(copies, 3, size, width)
    ad = jnp.concatenate([ad] + [p[size:last].reshape(rank, local_width) for p in packs], 1)
    wu_slice = after(jnp.concatenate([wu_first, wu_second], 0), wd_slices)
    wu_far = lax.all_gather(wu_slice, "dp", axis=0, tiled=True)
    mine, stat_mine = attend(2 * high, merged, seg, slopes, 2)
    m_two, mine = lax.optimization_barrier((m_two, mine))

    m_one = swap(mine, "mp", 1)
    m_three = swap(m_two, "mp", 1)
    wn_halves = jnp.split(after(slice_of(w_down), m_two), 2, axis=0)
    wn_first = swap(wn_halves[0], "mp", 2)
    m_one, m_three, wn_first = lax.optimization_barrier((m_one, m_three, wn_first))

    m_parts = [mine, m_one, m_two, m_three]
    cot_far = swap(after(cotangent, m_one), "mp", 1)
    wn_second = swap(after(wn_halves[1], m_one), "mp", 2)

    def pair(own, far):
        return jnp.where(low == 0, jnp.concatenate([own, far], 0), jnp.concatenate([far, own], 0))

    middle, second, z_dense, z_up = dense(
        low, layer_in, x_one, m_parts, ad, bd, second_gain, second_bias, au, w_dense, wd_far
    )
    wn_second, second, cot_far = lax.optimization_barrier((wn_second, second, cot_far))
    wn_far = lax.all_gather(jnp.concatenate([wn_first, wn_second], 0), "dp", axis=0, tiled=True)

    cot_pair = pair(cotangent, cot_far)
    dz_down = dot_nt(cot_pair, bn).astype(BF16)
    zero = jnp.zeros((), jnp.int32)
    act, dh, dzu, so_far = feed(
        zero, 2 * own_rows, second, cot_pair, w_up, w_down, z_up, dz_down, bu, an, au, None, F32
    )
    gn_own, gu_own, zn, out_so_far = emit(zero, (act,), (dh,), w_down, an, bn, z_up, dz_down, None)
    out_so_far, so_far = lax.optimization_barrier((out_so_far, so_far))
    far_args = (second, cot_pair, wu_far, wn_far, z_up, dz_down, bu_far, an_far, au, so_far)
    act_a, dh_a, dzu_a, d_send = feed(1 - low, own_rows, *far_args, BF16)
    low_late, d_send = lax.optimization_barrier((low, d_send))

    d_near = swap(d_send, "mp", 1)
    act_b, dh_b, dzu_b, d_own = feed(low_late, own_rows, *far_args, F32)
    gn_far, gu_far, zn_far, out_send, out_own = emit(
        low, (act_a, act_b), (dh_a, dh_b), wn_far, an_far, bn, z_up, dz_down, out_so_far
    )

    def halves(own, far, axis):
        return jnp.where(high == 0, jnp.concatenate([own, far], axis), jnp.concatenate([far, own], axis))

    def own(value):
        return lax.dynamic_slice_in_dim(value, low * own_rows, own_rows, 0)

    def join(value, first, second):
        return (value.astype(F32) + pair(second, first).astype(F32)).astype(BF16)

    mixed = halves(mine, other, 0)
    stat = halves(stat_mine, stat_other, 2)
    d_near, out_send, mixed, stat = lax.optimization_barrier((d_near, out_send, mixed, stat))

    d_middle, d_low, dz_dense, d_mixed = dense_back(
        low, d_own, d_near, middle, cotangent, second_gain, bd, ad, w_dense, wd_far
    )
    d_mixed, d_low, dz_dense = lax.optimization_barrier((d_mixed, d_low, dz_dense))
    g_blocks = [d_mixed[0]] + [swap(d_mixed[r], "mp", r) for r in (1, 2, 3)]
    ga_up = dot_tn(join(dzu, dzu_a, dzu_b), second)
    gb_down = dot_tn(join(zn, zn_far[:own_rows], zn_far[own_rows:]), cot_pair)
    gb_dense = dot_tn(own(z_dense), d_low)
    gd = [dot_tn(dz_dense, own(m)) for m in m_parts]
    sums = jnp.concatenate([ga_up, gb_down, gb_dense], 1)
    near_in = jnp.concatenate([sums, gd[1], gd[3]], 1).astype(BF16)
    *g_blocks, near_in = lax.optimization_barrier((*g_blocks, near_in))

    near = swap(near_in, "mp", 1)
    out_near = swap(after(out_send, near_in), "mp", 1)
    grad = jnp.zeros((total_rows, local_width), BF16)
    for r, block in enumerate(g_blocks):
        grad = lax.dynamic_update_slice_in_dim(grad, block, (index ^ r) * own_rows, 0)
    d_merged = attend_back(merged, mixed, grad, stat, seg, slopes)
    (send,) = project_back(index, d_merged, wq, aq, bq, (3,), (BF16,))
    send, d_merged, near, out_near = lax.optimization_barrier((send, d_merged, near, out_near))

    relay = swap(send, "mp", 1)
    ga_qkv, gb_qkv = inner_grads(d_merged, z_qkv, normed, bq)
    ga_low = ga_qkv.astype(BF16)
    near = near.astype(F32)
    sums = sums + near[:, :3 * width]
    gd_own = gd[0] + near[:, 3 * width:3 * width + local_width]
    gd_far = gd[2] + near[:, 3 * width + local_width:]
    mate_in = jnp.concatenate([sums.astype(BF16), gu_far, gn_far, gd_far.astype(BF16)], 1)
    ga_low, mate_in, d_merged = lax.optimization_barrier((ga_low, mate_in, d_merged))
    ga_others = [swap(ga_low, "mp", r) for r in (1, 2, 3)]
    mate = swap(mate_in, "mp", 2)
    send_two, send_one, kept = project_back(index, d_merged, wq, aq, bq, (2, 1, 0), (F32, BF16, F32))
    relay, kept, send_one, send_two, mate, *ga_others = lax.optimization_barrier(
        (relay, kept, send_one, send_two, mate, *ga_others)
    )

    d_two = swap((send_two + relay.astype(F32)).astype(BF16), "mp", 2)
    d_one = swap(send_one, "mp", 1)
    layer_out = (own(middle) + out_own + out_near.astype(F32)).astype(BF16)
    first_pack = jnp.concatenate([sums, gu_own, gn_own, gd_own], 1) + mate.astype(F32)
    first_pack = jnp.concatenate([first_pack.astype(BF16), jnp.full((rank, 128), which, BF16)], 1)
    first_pack = lax.all_gather(first_pack, "dp", axis=0)
    ga_qkv = ga_qkv + sum(g.astype(F32) for g in ga_others)
    second_pack = jnp.concatenate([ga_qkv, gb_qkv], 1).astype(BF16)
    second_pack = lax.all_gather(second_pack, "dp", axis=0)
    ids = first_pack[:, 0, -1].astype(jnp.int32)
    ga_up, gb_down, gb_dense, gb_up, ga_down, ga_dense, ga_qkv, gb_qkv = spread(
        ids, first_pack, second_pack, kinds, width, local_width, local_ff
    )
    d_one, d_two = lax.optimization_barrier((d_one, d_two, gb_qkv))[:2]
    d_first = kept + d_one.astype(F32) + d_two.astype(F32)
    input_grad = (d_middle + norm_back(d_first, layer_in.astype(F32), first_gain)).astype(BF16)
    return (
        layer_out,
        input_grad,
        ga_qkv.transpose(2, 0, 1),
        gb_qkv.transpose(0, 2, 1, 3),
        ga_dense.transpose(2, 0, 1),
        gb_dense,
        ga_up.transpose(2, 0, 1),
        gb_up,
        ga_down.transpose(2, 0, 1),
        gb_down,
    )


def solution(mesh):
    return jax.shard_map(
        local,
        mesh=mesh,
        in_specs=(
            P(("dp", "mp"), None), P(), P(), P(None, None, "mp"), P(), P(None, None, None, "mp"), P("mp", None),
            P("mp", None, None), P(), P(), P(), P(None, "mp"), P(), P(None, None, "mp"), P("mp", None),
            P("mp", None, None), P(), P("dp", None), P("dp"), P(("dp", "mp"), None),
        ),
        out_specs=(
            P(("dp", "mp"), None), P(("dp", "mp"), None), P(), P(None, None, None, "mp"), P("mp", None, None), P(),
            P(), P(None, None, "mp"), P("mp", None, None), P(),
        ),
        check_vma=False,
    )
```

time: 706 us -> 545 us (0.77)
  matrix products: 200 us -> 7.27 us
  Pallas kernels: 59.1 us -> 237 us
  waiting for transfers between devices: 275 us -> 161 us
  local copies, waits for them, and re-layouts: 69.9 us -> 28.5 us
  blocking collectives: 0 us -> 11.4 us
  starting transfers between devices: 50 us -> 41.1 us
    pallas_call x2 -> x18, Pallas kernels: 59.1 us -> 237 us  [the longest x3 53 us: feed(): pl.pallas_call(functools.partial(feed_kernel, earlier), out_shape=(shape(...]
    ppermute x36 -> x26, waiting for transfers between devices: 275 us -> 135 us  [swap(): return lax.ppermute(value, axis, pairs)]
    dot_general x28 -> x0, matrix products: 93.3 us -> none  [dot_nn(): return jnp.dot(left, right, preferred_element_type=F32)]
    dot_general x26 -> x1, matrix products: 88.7 us -> 1.41 us  [dot_nt(): lax.dot_general(left, right, (((1,), (1,)), ((), ())), preferred_element_...]
    all_gather x6 -> x4, waiting for transfers between devices: 0.01 us -> 26.7 us  [the longest x1 18.7 us: local(): lax.all_gather(jnp.concatenate([wn_first, wn_second], 0), 'dp', axis=0, t...]
    unnamed x116 -> x96, local copies, waits for them, and re-layouts: 20.5 us -> 2.56 us
    dot_general x15 -> x7, matrix products: 18.4 us -> 5.86 us  [dot_tn(): lax.dot_general(left, right, (((0,), (0,)), ((), ())), preferred_element_...]
    dynamic_update_slice x12 -> x4, local copies, waits for them, and re-layouts: 13.3 us -> 1.08 us  [local(): lax.dynamic_update_slice_in_dim(grad, block, (index ^ r) * own_rows, 0)]
  transfers between devices with their start and end apart: 42 -> 30, of which waited for: 21 -> 15; matrix products, arithmetic and copies ran while one was open for 34% -> 11% of each run, Pallas kernels for 8% -> 39%
where the time goes in v2:
time: 545 us; the launch traced here: 534 us
  Pallas kernels  237 us (43%)
  waiting for transfers between devices  161 us (30%)
  starting transfers between devices  41.1 us (8%)
  other arithmetic  32.4 us (6%)
  local copies, waits for them, and re-layouts  28.5 us (5%)
  between operations  15.6 us (3%)
  blocking collectives  11.4 us (2%)
  matrix products  7.27 us (1%)
    ppermute x26, waiting for transfers between devices, swap(): return lax.ppermute(value, axis, pairs)  135 us
    pallas_call x3, Pallas kernels, feed(): pl.pallas_call(functools.partial(feed_kernel, earlier), out_shape=(shape(...  53 us
    ppermute x26, starting transfers between devices, swap(): return lax.ppermute(value, axis, pairs)  40.6 us
    pallas_call x2, Pallas kernels, attend(): pl.pallas_call(functools.partial(attend_kernel, block, count), out_shape=...  36.8 us
    pallas_call x4, Pallas kernels, project(): pl.pallas_call(functools.partial(project_kernel, kept), out_shape=(shape(...  29.6 us
    pallas_call x1, Pallas kernels, attend_back(): pl.pallas_call(functools.partial(attend_back_kernel, block), out_shape=sh...  29.5 us
    pallas_call x2, Pallas kernels, emit(): pl.pallas_call(functools.partial(emit_kernel, earlier), out_shape=(shape(...  26 us
    pallas_call x2, Pallas kernels, project_back(): pl.pallas_call(functools.partial(project_back_kernel, order), out_shape=t...  20.1 us
  transfers between devices with their start and end apart: 30, of which 15 were waited for; matrix products, arithmetic and copies ran while one was open for 11% of the time, Pallas kernels for 39%

profile of v2, /device:TPU:0, one launch (start us, length us, event | category | flops | bytes accessed | tf_op | source)
XLA Modules:
  0.0 534.2 jit_solution(7582580601297859106)
XLA Ops:
  19.0 7.3 %project.4 = (bf16[3,1024,512]{2,1,0:T(8,128)(2,1)}, bf16[1024,2048]{1,0:T(8,128)(2,1)}, bf16[1024,16]{1,0:T(8,128)(2,1)}) custom-call(s32[1]{0:T(128)} %bitcast.1.at_ref, bf16[256,2048]{1,0:T(8,128)(2,1)} %x0_ref.1, bf16[1,2048]{1,0:T(2,128)(2,1)} %broadcast_in_dim.12.gain_ref, bf16[1,2048]{1,0:T(2,128)(2,1)} %broadcast_in_dim.13.bias_ref, ...), custom_call_target="tpu_custom_call" | custom-call | tf_op jit(solution)/shard_map/project/pallas_call | solution.py:110
  28.1 27.9 %collective-permute-done.x_ref.x1_ref = bf16[256,2048]{1,0:T(8,128)(2,1)S(1)} collective-permute-done((bf16[256,2048]{1,0:T(8,128)(2,1)}, bf16[256,2048]{1,0:T(8,128)(2,1)S(1)}, u32[]{:S(2)}, u32[]{:S(2)}) %collective-permute-start) | collective-permute-done | bytes 1048608 | tf_op jit(solution)/shard_map/ppermute | solution.py:64
  65.9 7.4 %project.5 = (bf16[3,1024,512]{2,1,0:T(8,128)(2,1)}, bf16[1024,2048]{1,0:T(8,128)(2,1)}, bf16[1024,16]{1,0:T(8,128)(2,1)}) custom-call(s32[1]{0:T(128)} %bitcast.18.at_ref, bf16[256,2048]{1,0:T(8,128)(2,1)} %copy-done.7, bf16[1,2048]{1,0:T(2,128)(2,1)} %broadcast_in_dim.12.gain_ref, ...), custom_call_target="tpu_custom_call", output_to_operand_aliasing={{0}: (7, {}), {1}: (8, {}), {2}: (9, {})} | custom-call | tf_op jit(solution)/shard_map/project/pallas_call | solution.py:110
  73.3 7.4 %project.6 = (bf16[3,1024,512]{2,1,0:T(8,128)(2,1)}, bf16[1024,2048]{1,0:T(8,128)(2,1)}, bf16[1024,16]{1,0:T(8,128)(2,1)}) custom-call(s32[1]{0:T(128)} %bitcast.15.at_ref, bf16[256,2048]{1,0:T(8,128)(2,1)} %copy-done.20, bf16[1,2048]{1,0:T(2,128)(2,1)} %broadcast_in_dim.12.gain_ref, ...), custom_call_target="tpu_custom_call", output_to_operand_aliasing={{0}: (7, {}), {1}: (8, {}), {2}: (9, {})} | custom-call | tf_op jit(solution)/shard_map/project/pallas_call | solution.py:110
  80.7 24.6 %collective-permute-done.3 = bf16[100,2048]{1,0:T(8,128)(2,1)S(1)} collective-permute-done((bf16[100,2048]{1,0:T(8,128)(2,1)}, bf16[100,2048]{1,0:T(8,128)(2,1)S(1)}, u32[]{:S(2)}, u32[]{:S(2)}) %collective-permute-start.3) | collective-permute-done | bytes 409632 | tf_op jit(solution)/shard_map/ppermute | solution.py:64
  108.0 7.6 %project.7 = (bf16[3,1024,512]{2,1,0:T(8,128)(2,1)}, bf16[1024,2048]{1,0:T(8,128)(2,1)}, bf16[1024,16]{1,0:T(8,128)(2,1)}) custom-call(s32[1]{0:T(128)} %bitcast.10.at_ref, bf16[256,2048]{1,0:T(8,128)(2,1)} %collective-permute-done.2.x_ref, bf16[1,2048]{1,0:T(2,128)(2,1)} %broadcast_in_dim.12.gain_ref, ...), custom_call_target="tpu_custom_call", output_to_operand_aliasing={{0}: (7, {}), {1}: (8, {}), {2}: (9, {})} | custom-call | tf_op jit(solution)/shard_map/project/pallas_call | solution.py:110
  116.6 21.6 %attend.2 = (bf16[512,512]{1,0:T(8,128)(2,1)}, f32[8,1,512]{2,1,0:T(1,128)}) custom-call(s32[1]{0:T(128)} %bitcast.8.first_ref, s32[1024]{0:T(1024)} %bitcast.81, f32[8]{0:T(128)} %multiply_exponential_fusion.slope_ref, s32[1024,128]{1,0:T(8,128)} %broadcast_in_dim.14.col_ref, s32[1,1024]{1,0:T(1,128)} %row_ref.5, ...), custom_call_target="tpu_custom_call" | custom-call | tf_op jit(solution)/shard_map/attend/pallas_call | solution.py:214
  142.9 15.1 %attend.3 = (bf16[512,512]{1,0:T(8,128)(2,1)}, f32[8,1,512]{2,1,0:T(1,128)}) custom-call(s32[1]{0:T(128)} %bitcast.19.first_ref, s32[1024]{0:T(1024)} %bitcast.82, f32[8]{0:T(128)} %multiply_exponential_fusion.slope_ref, s32[1024,128]{1,0:T(8,128)} %broadcast_in_dim.14.col_ref, s32[1,1024]{1,0:T(1,128)} %row_ref.5, ...), custom_call_target="tpu_custom_call" | custom-call | tf_op jit(solution)/shard_map/attend/pallas_call | solution.py:214
  158.1 5.5 %collective-permute-done.7.m2_ref = bf16[512,512]{1,0:T(8,128)(2,1)S(1)} collective-permute-done((bf16[512,512]{1,0:T(8,128)(2,1)}, bf16[512,512]{1,0:T(8,128)(2,1)S(1)}, u32[]{:S(2)}, u32[]{:S(2)}) %collective-permute-start.7) | collective-permute-done | bytes 524320 | tf_op jit(solution)/shard_map/ppermute | solution.py:64
  172.0 26.7 %collective-permute-done.8.m1_ref = bf16[512,512]{1,0:T(8,128)(2,1)S(1)} collective-permute-done((bf16[512,512]{1,0:T(8,128)(2,1)S(1)}, bf16[512,512]{1,0:T(8,128)(2,1)S(1)}, u32[]{:S(2)}, u32[]{:S(2)}) %collective-permute-start.8) | collective-permute-done | bytes 524320 | tf_op jit(solution)/shard_map/ppermute | solution.py:64
  206.8 14.2 %dense.1 = (f32[512,2048]{1,0:T(8,128)}, bf16[512,2048]{1,0:T(8,128)(2,1)}, bf16[512,16]{1,0:T(8,128)(2,1)}, bf16[512,16]{1,0:T(8,128)(2,1)}) custom-call(s32[1]{0:T(128)} %bitcast.at_ref.low_ref, bf16[256,2048]{1,0:T(8,128)(2,1)} %x0_ref.1, bf16[256,2048]{1,0:T(8,128)(2,1)} %copy-done.7, bf16[512,512]{1,0:T(8,128)(2,1)} %get-tuple-element.162.m0_ref, ...), custom_call_target="tpu_custom_call" | custom-call | tf_op jit(solution)/shard_map/dense/pallas_call | solution.py:361
  221.0 9.9 %collective-permute-done.11 = bf16[128,2048]{1,0:T(8,128)(2,1)} collective-permute-done((bf16[128,2048]{1,0:T(8,128)(2,1)}, bf16[128,2048]{1,0:T(8,128)(2,1)}, u32[]{:S(2)}, u32[]{:S(2)}) %collective-permute-start.11) | collective-permute-done | bytes 524320 | tf_op jit(solution)/shard_map/ppermute | solution.py:64
  242.7 23.1 %feed.3 = (bf16[512,2048]{1,0:T(8,128)(2,1)}, bf16[512,2048]{1,0:T(8,128)(2,1)}, bf16[512,16]{1,0:T(8,128)(2,1)}, f32[512,2048]{1,0:T(8,128)}) custom-call(s32[1]{0:T(128)} %constant.68.clone.1.at_ref, bf16[512,2048]{1,0:T(8,128)(2,1)} %get-tuple-element.173.x_ref, bf16[512,2048]{1,0:T(8,128)(2,1)} %copy-done.2, bf16[2048,2048]{1,0:T(8,128)(2,1)} %up_ref.1, ...), custom_call_target="tpu_custom_call" | custom-call | tf_op jit(solution)/shard_map/feed/pallas_call | solution.py:417
  265.8 12.5 %emit.2 = (bf16[16,2048]{1,0:T(8,128)(2,1)}, bf16[16,2048]{1,0:T(8,128)(2,1)}, bf16[512,16]{1,0:T(8,128)(2,1)}, f32[512,2048]{1,0:T(8,128)}) custom-call(s32[1]{0:T(128)} %constant.68.clone.1.at_ref, bf16[512,2048]{1,0:T(8,128)(2,1)} %get-tuple-element.181.refs_0_, bf16[512,2048]{1,0:T(8,128)(2,1)} %get-tuple-element.182.refs_1_, ...), custom_call_target="tpu_custom_call" | custom-call | tf_op jit(solution)/shard_map/emit/pallas_call | solution.py:490
  278.4 18.7 %all-gather.9.cloned.1.call-done.down_ref.refs_8_ = bf16[2048,2048]{1,0:T(8,128)(2,1)} async-done(((bf16[256,2048]{1,0:T(8,128)(2,1)}), bf16[2048,2048]{1,0:T(8,128)(2,1)}) %all-gather.9.cloned.1.call-update) | async-done | bytes 8388624 | tf_op jit(solution)/shard_map/all_gather | solution.py:778
  297.1 14.7 %feed.4 = (bf16[256,2048]{1,0:T(8,128)(2,1)}, bf16[256,2048]{1,0:T(8,128)(2,1)}, bf16[256,16]{1,0:T(8,128)(2,1)}, bf16[256,2048]{1,0:T(8,128)(2,1)}) custom-call(s32[1]{0:T(128)} %bitcast.25.at_ref, bf16[512,2048]{1,0:T(8,128)(2,1)} %get-tuple-element.173.x_ref, bf16[512,2048]{1,0:T(8,128)(2,1)} %copy-done.2, ...), custom_call_target="tpu_custom_call" | custom-call | tf_op jit(solution)/shard_map/feed/pallas_call | solution.py:417
  316.0 15.1 %feed.5 = (bf16[256,2048]{1,0:T(8,128)(2,1)}, bf16[256,2048]{1,0:T(8,128)(2,1)}, bf16[256,16]{1,0:T(8,128)(2,1)}, f32[256,2048]{1,0:T(8,128)}) custom-call(s32[1]{0:T(128)} %bitcast.29.at_ref, bf16[512,2048]{1,0:T(8,128)(2,1)} %get-tuple-element.173.x_ref, bf16[512,2048]{1,0:T(8,128)(2,1)} %copy-done.2, ...), custom_call_target="tpu_custom_call" | custom-call | tf_op jit(solution)/shard_map/feed/pallas_call | solution.py:417
  332.4 13.5 %emit.3 = (bf16[16,2048]{1,0:T(8,128)(2,1)}, bf16[16,2048]{1,0:T(8,128)(2,1)}, bf16[512,16]{1,0:T(8,128)(2,1)}, bf16[256,2048]{1,0:T(8,128)(2,1)}, f32[256,2048]{1,0:T(8,128)}) custom-call(s32[1]{0:T(128)} %bitcast.at_ref.low_ref, bf16[256,2048]{1,0:T(8,128)(2,1)} %get-tuple-element.186.refs_0_, bf16[256,2048]{1,0:T(8,128)(2,1)} %get-tuple-element.189.refs_1_, ...), custom_call_target="tpu_custom_call" | custom-call | tf_op jit(solution)/shard_map/emit/pallas_call | solution.py:490
  349.1 11.9 %dense_back.1 = (f32[256,2048]{1,0:T(8,128)}, bf16[256,2048]{1,0:T(8,128)(2,1)}, bf16[256,16]{1,0:T(8,128)(2,1)}, bf16[4,256,512]{2,1,0:T(8,128)(2,1)}) custom-call(s32[1]{0:T(128)} %bitcast.at_ref.low_ref, f32[256,2048]{1,0:T(8,128)} %get-tuple-element.200.own_ref, bf16[256,2048]{1,0:T(8,128)(2,1)} %collective-permute-done.13.far_ref, ...), custom_call_target="tpu_custom_call" | custom-call | tf_op jit(solution)/shard_map/dense_back/pallas_call | solution.py:546
  370.3 5.7 %collective-permute-done.14 = bf16[256,512]{1,0:T(8,128)(2,1)S(1)} collective-permute-done((bf16[256,512]{1,0:T(8,128)(2,1)S(1)}, bf16[256,512]{1,0:T(8,128)(2,1)S(1)}, u32[]{:S(2)}, u32[]{:S(2)}) %collective-permute-start.14) | collective-permute-done | bytes 262176 | tf_op jit(solution)/shard_map/ppermute | solution.py:64
  376.0 8.3 %collective-permute-done.15 = bf16[256,512]{1,0:T(8,128)(2,1)S(1)} collective-permute-done((bf16[256,512]{1,0:T(8,128)(2,1)S(1)}, bf16[256,512]{1,0:T(8,128)(2,1)S(1)}, u32[]{:S(2)}, u32[]{:S(2)}) %collective-permute-start.15) | collective-permute-done | bytes 262176 | tf_op jit(solution)/shard_map/ppermute | solution.py:64
  385.8 4.2 collective-permute-start.18
  392.2 29.5 %attend_back.1.d_ref = bf16[3,1024,512]{2,1,0:T(8,128)(2,1)} custom-call(s32[1024]{0:T(1024)} %bitcast.83, f32[8]{0:T(128)} %multiply_exponential_fusion.slope_ref, s32[1024,128]{1,0:T(8,128)} %broadcast_in_dim.14.col_ref, s32[1,1024]{1,0:T(1,128)} %row_ref.5, f32[8,1,1024]{2,1,0:T(1,128)} %broadcast_select_fusion.stat_ref, ...), custom_call_target="tpu_custom_call" | custom-call | tf_op jit(solution)/shard_map/attend_back/pallas_call | solution.py:299
  421.7 7.5 %project_back.2 = bf16[256,2048]{1,0:T(8,128)(2,1)} custom-call(s32[1]{0:T(128)} %bitcast.1.at_ref, bf16[16,2048]{1,0:T(8,128)(2,1)} %dynamic-slice_bitcast_fusion.5.aq_ref, bf16[3,16,512]{2,1,0:T(8,128)(2,1)} %dynamic-slice_bitcast_fusion.6.bq_ref, bf16[3,1024,512]{2,1,0:T(8,128)(2,1)} %attend_back.1.d_ref, bf16[3,2048,512]{2,1,0:T(8,128)(2,1)} %bitcast.75), custom_call_target="tpu_custom_call" | custom-call | tf_op jit(solution)/shard_map/project_back/pallas_call | solution.py:588
  431.2 6.6 %inner_grads.1 = (f32[16,2048]{1,0:T(8,128)}, f32[16,1536]{1,0:T(8,128)}) custom-call(bf16[3,1024,512]{2,1,0:T(8,128)(2,1)} %attend_back.1.d_ref, bf16[1024,16]{1,0:T(8,128)(2,1)} %get-tuple-element.225.z_ref, bf16[1024,2048]{1,0:T(8,128)(2,1)} %get-tuple-element.226.n_ref, bf16[3,16,512]{2,1,0:T(8,128)(2,1)} %dynamic-slice_bitcast_fusion.6.bq_ref), custom_call_target="tpu_custom_call" | custom-call | tf_op jit(solution)/shard_map/inner_grads/pallas_call | solution.py:621
  448.1 12.6 %project_back.3 = (f32[256,2048]{1,0:T(8,128)}, bf16[256,2048]{1,0:T(8,128)(2,1)}, f32[256,2048]{1,0:T(8,128)}) custom-call(s32[1]{0:T(128)} %bitcast.1.at_ref, bf16[16,2048]{1,0:T(8,128)(2,1)} %dynamic-slice_bitcast_fusion.5.aq_ref, bf16[3,16,512]{2,1,0:T(8,128)(2,1)} %dynamic-slice_bitcast_fusion.6.bq_ref, bf16[3,1024,512]{2,1,0:T(8,128)(2,1)} %attend_back.1.d_ref, ...), custom_call_target="tpu_custom_call" | custom-call | tf_op jit(solution)/shard_map/project_back/pallas_call | solution.py:588
  463.3 4.4 collective-permute-done.23
  478.8 11.4 %all_gather.28.second_ref = bf16[8,16,3584]{2,1,0:T(8,128)(2,1)} all-gather(bf16[1,16,3584]{2,1,0:T(8,128)(2,1)S(1)} %pad_maximum_fusion.6), channel_id=1, replica_groups=mesh['dp'=8,'mp'=4] {'dp'}, dimensions={0}, use_global_device_ids=true | all-gather | bytes 1032192 | tf_op jit(solution)/shard_map/all_gather | solution.py:857
  490.2 8.0 %all-gather.13.cloned.1.call-done = bf16[128,10880]{1,0:T(8,128)(2,1)} async-done(((bf16[16,10880]{1,0:T(8,128)(2,1)}), bf16[128,10880]{1,0:T(8,128)(2,1)}) %all-gather.13.cloned.1.call-update) | async-done | bytes 2785296 | tf_op jit(solution)/shard_map/all_gather | solution.py:854
  499.7 8.9 %spread.1 = (f32[8,16,2048]{2,1,0:T(8,128)}, f32[8,16,2048]{2,1,0:T(8,128)}, f32[8,16,2048]{2,1,0:T(8,128)}, f32[8,16,2048]{2,1,0:T(8,128)}, f32[8,16,2048]{2,1,...) custom-call(s32[8]{0:T(128)} %fusion.33.ids_ref, ...), custom_call_target="tpu_custom_call" | custom-call | tf_op jit(solution)/shard_map/spread/pallas_call | solution.py:665
  508.6 5.8 %collective-permute-done.24 = bf16[256,2048]{1,0:T(8,128)(2,1)S(1)} collective-permute-done((bf16[256,2048]{1,0:T(8,128)(2,1)}, bf16[256,2048]{1,0:T(8,128)(2,1)S(1)}, u32[]{:S(2)}, u32[]{:S(2)}) %collective-permute-start.24) | collective-permute-done | bytes 1048608 | tf_op jit(solution)/shard_map/ppermute | solution.py:64
  514.4 8.2 %collective-permute-done.25 = bf16[256,2048]{1,0:T(8,128)(2,1)} collective-permute-done((bf16[256,2048]{1,0:T(8,128)(2,1)}, bf16[256,2048]{1,0:T(8,128)(2,1)}, u32[]{:S(2)}, u32[]{:S(2)}) %collective-permute-start.25) | collective-permute-done | bytes 1048608 | tf_op jit(solution)/shard_map/ppermute | solution.py:64
  (227 shorter events, 112.6 us)
Async XLA Ops:
  7.2 199.6 %all-gather.11.cloned.1.call-start = ((), (), s32[]{:S(2)}) async-start(), calls=%async_computation.2 | async-start | bytes 7077888 | tf_op jit(solution)/shard_map/all_gather | solution.py:754
  7.2 48.8 %collective-permute-start = (bf16[256,2048]{1,0:T(8,128)(2,1)}, bf16[256,2048]{1,0:T(8,128)(2,1)S(1)}, u32[]{:S(2)}, u32[]{:S(2)}) collective-permute-start(bf16[256,2048]{1,0:T(8,128)(2,1)} %x0_ref.1), channel_id=1, source_target_pairs={{0,1},{1,0},{2,3},{3,2},{4,5},{5,4},{6,7},{7,6},{8,9},{9,8},{10,11... | collective-permute-start | bytes 3145736 | tf_op jit(solution)/shard_map/ppermute | solution.py:64
  10.3 48.3 %collective-permute-start.1 = (bf16[256,2048]{1,0:T(8,128)(2,1)}, bf16[256,2048]{1,0:T(8,128)(2,1)S(1)}, u32[]{:S(2)}, u32[]{:S(2)}) collective-permute-start(bf16[256,2048]{1,0:T(8,128)(2,1)} %x0_ref.1), channel_id=1, source_target_pairs={{0,2},{1,3},{2,0},{3,1},{4,6},{5,7},{6,4},{7,5},{8,10},{9,11},{10,... | collective-permute-start | bytes 3145736 | tf_op jit(solution)/shard_map/ppermute | solution.py:64
  27.2 46.1 %copy-start.19 = (bf16[16,2048]{1,0:T(8,128)(2,1)}, bf16[16,2048]{1,0:T(8,128)(2,1)S(1)}, u32[]{:S(2)}) copy-start(bf16[16,2048]{1,0:T(8,128)(2,1)S(1)} %dynamic-slice_bitcast_fusion.3.an_ref.refs_5_) | copy-start | bytes 196612
  58.6 46.7 %collective-permute-start.2 = (bf16[256,2048]{1,0:T(8,128)(2,1)S(1)}, bf16[256,2048]{1,0:T(8,128)(2,1)}, u32[]{:S(2)}, u32[]{:S(2)}) collective-permute-start(bf16[256,2048]{1,0:T(8,128)(2,1)S(1)} %collective-permute-done.1.x_ref), channel_id=1, source_target_pairs={{0,1},{1,0},{2,3},{3,2},{4,5},{5,4},{6,7},{7,6},{8,9},{9,8},{10,11... | collective-permute-start | bytes 3145736 | tf_op jit(solution)/shard_map/ppermute | solution.py:64
  62.2 43.1 %collective-permute-start.4 = (bf16[128,2048]{1,0:T(8,128)(2,1)}, bf16[128,2048]{1,0:T(8,128)(2,1)}, u32[]{:S(2)}, u32[]{:S(2)}) collective-permute-start(bf16[128,2048]{1,0:T(8,128)(2,1)} %get-tuple-element.140), channel_id=1, source_target_pairs={{0,2},{1,3},{2,0},{3,1},{4,6},{5,7},{6,4},{7,5},{8,10},{9,11},{10,... | collective-permute-start | bytes 1572872 | tf_op jit(solution)/shard_map/ppermute | solution.py:64
  65.6 39.6 %collective-permute-start.3 = (bf16[100,2048]{1,0:T(8,128)(2,1)}, bf16[100,2048]{1,0:T(8,128)(2,1)S(1)}, u32[]{:S(2)}, u32[]{:S(2)}) collective-permute-start(bf16[100,2048]{1,0:T(8,128)(2,1)} %pad_maximum_fusion.4), channel_id=1, source_target_pairs={{0,2},{1,3},{2,0},{3,1},{4,6},{5,7},{6,4},{7,5},{8,10},{9,11},{10,... | collective-permute-start | bytes 1228808 | tf_op jit(solution)/shard_map/ppermute | solution.py:64
  105.4 32.8 %collective-permute-start.5 = (bf16[136,2048]{1,0:T(8,128)(2,1)S(1)}, bf16[136,2048]{1,0:T(8,128)(2,1)S(1)}, u32[]{:S(2)}, u32[]{:S(2)}) collective-permute-start(bf16[136,2048]{1,0:T(8,128)(2,1)S(1)} %pad_maximum_fusion.3), channel_id=1, source_target_pairs={{0,1},{1,0},{2,3},{3,2},{4,5},{5,4},{6,7},{7,6},{8,9},{9,8},{10,11... | collective-permute-start | bytes 1671176 | tf_op jit(solution)/shard_map/ppermute | solution.py:64
  105.5 32.7 %collective-permute-start.6 = (bf16[128,2048]{1,0:T(8,128)(2,1)}, bf16[128,2048]{1,0:T(8,128)(2,1)S(1)}, u32[]{:S(2)}, u32[]{:S(2)}) collective-permute-start(bf16[128,2048]{1,0:T(8,128)(2,1)} %get-tuple-element.158), channel_id=1, source_target_pairs={{0,2},{1,3},{2,0},{3,1},{4,6},{5,7},{6,4},{7,5},{8,10},{9,11},{10,... | collective-permute-start | bytes 1572872 | tf_op jit(solution)/shard_map/ppermute | solution.py:64
  139.3 139.0 %all-gather.7.cloned.1.call-start = ((), (), s32[]{:S(2)}) async-start(), calls=%async_computation | async-start | bytes 9437184 | tf_op jit(solution)/shard_map/all_gather | solution.py:757
  141.5 155.6 %all-gather.9.cloned.1.call-start = ((), (), s32[]{:S(2)}) async-start(), calls=%async_computation.1 | async-start | bytes 9437184 | tf_op jit(solution)/shard_map/all_gather | solution.py:778
  141.5 22.1 %collective-permute-start.7 = (bf16[512,512]{1,0:T(8,128)(2,1)}, bf16[512,512]{1,0:T(8,128)(2,1)S(1)}, u32[]{:S(2)}, u32[]{:S(2)}) collective-permute-start(bf16[512,512]{1,0:T(8,128)(2,1)} %get-tuple-element.159), channel_id=1, source_target_pairs={{0,2},{1,3},{2,0},{3,1},{4,6},{5,7},{6,4},{7,5},{8,10},{9,11},{10,... | collective-permute-start | bytes 1572872 | tf_op jit(solution)/shard_map/ppermute | solution.py:64
  158.1 48.0 %slice-start = ((bf16[100,2048]{1,0:T(8,128)(2,1)}), bf16[4,2048]{1,0:T(4,128)(2,1)S(1)}, s32[]{:S(2)}) async-start(bf16[100,2048]{1,0:T(8,128)(2,1)} %copy-done.17), calls=%async_computation.4 | async-start | bytes 32768 | tf_op jit(solution)/shard_map/slice | solution.py:755
  163.6 35.1 %collective-permute-start.9 = (bf16[512,512]{1,0:T(8,128)(2,1)S(1)}, bf16[512,512]{1,0:T(8,128)(2,1)}, u32[]{:S(2)}, u32[]{:S(2)}) collective-permute-start(bf16[512,512]{1,0:T(8,128)(2,1)S(1)} %collective-permute-done.7.m2_ref), channel_id=1, source_target_pairs={{0,1},{1,0},{2,3},{3,2},{4,5},{5,4},{6,7},{7,6},{8,9},{9,8},{10,11... | collective-permute-start | bytes 1572872 | tf_op jit(solution)/shard_map/ppermute | solution.py:64
  164.7 34.0 %collective-permute-start.8 = (bf16[512,512]{1,0:T(8,128)(2,1)S(1)}, bf16[512,512]{1,0:T(8,128)(2,1)S(1)}, u32[]{:S(2)}, u32[]{:S(2)}) collective-permute-start(bf16[512,512]{1,0:T(8,128)(2,1)S(1)} %copy-done.9), channel_id=1, source_target_pairs={{0,1},{1,0},{2,3},{3,2},{4,5},{5,4},{6,7},{7,6},{8,9},{9,8},{10,11... | collective-permute-start | bytes 1572872 | tf_op jit(solution)/shard_map/ppermute | solution.py:64
  166.7 32.1 %collective-permute-start.10 = (bf16[128,2048]{1,0:T(8,128)(2,1)}, bf16[128,2048]{1,0:T(8,128)(2,1)S(1)}, u32[]{:S(2)}, u32[]{:S(2)}) collective-permute-start(bf16[128,2048]{1,0:T(8,128)(2,1)} %get-tuple-element.269), channel_id=1, source_target_pairs={{0,2},{1,3},{2,0},{3,1},{4,6},{5,7},{6,4},{7,5},{8,10},{9,11},{10,... | collective-permute-start | bytes 1572872 | tf_op jit(solution)/shard_map/ppermute | solution.py:64
  198.8 34.4 %collective-permute-start.12 = (bf16[256,2048]{1,0:T(8,128)(2,1)S(1)}, bf16[256,2048]{1,0:T(8,128)(2,1)}, u32[]{:S(2)}, u32[]{:S(2)}) collective-permute-start(bf16[256,2048]{1,0:T(8,128)(2,1)S(1)} %copy-done.6), channel_id=1, source_target_pairs={{0,1},{1,0},{2,3},{3,2},{4,5},{5,4},{6,7},{7,6},{8,9},{9,8},{10,11... | collective-permute-start | bytes 3145736 | tf_op jit(solution)/shard_map/ppermute | solution.py:64
  202.9 28.1 %collective-permute-start.11 = (bf16[128,2048]{1,0:T(8,128)(2,1)}, bf16[128,2048]{1,0:T(8,128)(2,1)}, u32[]{:S(2)}, u32[]{:S(2)}) collective-permute-start(bf16[128,2048]{1,0:T(8,128)(2,1)} %get-tuple-element.170), channel_id=1, source_target_pairs={{0,2},{1,3},{2,0},{3,1},{4,6},{5,7},{6,4},{7,5},{8,10},{9,11},{10,... | collective-permute-start | bytes 1572872 | tf_op jit(solution)/shard_map/ppermute | solution.py:64
  235.4 262.7 %all-gather.13.cloned.1.call-start = ((), (), s32[]{:S(2)}) async-start(), calls=%async_computation.3 | async-start | bytes 3133440 | tf_op jit(solution)/shard_map/all_gather | solution.py:854
  311.8 37.3 %collective-permute-start.13 = (bf16[256,2048]{1,0:T(8,128)(2,1)}, bf16[256,2048]{1,0:T(8,128)(2,1)}, u32[]{:S(2)}, u32[]{:S(2)}) collective-permute-start(bf16[256,2048]{1,0:T(8,128)(2,1)} %get-tuple-element.194), channel_id=1, source_target_pairs={{0,1},{1,0},{2,3},{3,2},{4,5},{5,4},{6,7},{7,6},{8,9},{9,8},{10,11... | collective-permute-start | bytes 3145736 | tf_op jit(solution)/shard_map/ppermute | solution.py:64
  362.4 13.6 %collective-permute-start.14 = (bf16[256,512]{1,0:T(8,128)(2,1)S(1)}, bf16[256,512]{1,0:T(8,128)(2,1)S(1)}, u32[]{:S(2)}, u32[]{:S(2)}) collective-permute-start(bf16[256,512]{1,0:T(8,128)(2,1)S(1)} %get-tuple-element.267), channel_id=1, source_target_pairs={{0,1},{1,0},{2,3},{3,2},{4,5},{5,4},{6,7},{7,6},{8,9},{9,8},{10,11... | collective-permute-start | bytes 786440 | tf_op jit(solution)/shard_map/ppermute | solution.py:64
  363.0 21.3 %collective-permute-start.15 = (bf16[256,512]{1,0:T(8,128)(2,1)S(1)}, bf16[256,512]{1,0:T(8,128)(2,1)S(1)}, u32[]{:S(2)}, u32[]{:S(2)}) collective-permute-start(bf16[256,512]{1,0:T(8,128)(2,1)S(1)} %get-tuple-element.266), channel_id=1, source_target_pairs={{0,2},{1,3},{2,0},{3,1},{4,6},{5,7},{6,4},{7,5},{8,10},{9,11},{10,... | collective-permute-start | bytes 786440 | tf_op jit(solution)/shard_map/ppermute | solution.py:64
  365.4 18.9 %collective-permute-start.16 = (bf16[256,512]{1,0:T(8,128)(2,1)S(1)}, bf16[256,512]{1,0:T(8,128)(2,1)S(1)}, u32[]{:S(2)}, u32[]{:S(2)}) collective-permute-start(bf16[256,512]{1,0:T(8,128)(2,1)S(1)} %get-tuple-element.265), channel_id=1, source_target_pairs={{0,3},{1,2},{2,1},{3,0},{4,7},{5,6},{6,5},{7,4},{8,11},{9,10},{10,... | collective-permute-start | bytes 786440 | tf_op jit(solution)/shard_map/ppermute | solution.py:64
  385.8 43.4 %collective-permute-start.18 = (bf16[256,2048]{1,0:T(8,128)(2,1)}, bf16[256,2048]{1,0:T(8,128)(2,1)S(1)}, u32[]{:S(2)}, u32[]{:S(2)}) collective-permute-start(bf16[256,2048]{1,0:T(8,128)(2,1)} %get-tuple-element.220), channel_id=1, source_target_pairs={{0,1},{1,0},{2,3},{3,2},{4,5},{5,4},{6,7},{7,6},{8,9},{9,8},{10,11... | collective-permute-start | bytes 3145736 | tf_op jit(solution)/shard_map/ppermute | solution.py:64
  390.0 39.2 %collective-permute-start.17 = (bf16[16,7168]{1,0:T(8,128)(2,1)}, bf16[16,7168]{1,0:T(8,128)(2,1)}, u32[]{:S(2)}, u32[]{:S(2)}) collective-permute-start(bf16[16,7168]{1,0:T(8,128)(2,1)} %fusion.11), channel_id=1, source_target_pairs={{0,1},{1,0},{2,3},{3,2},{4,5},{5,4},{6,7},{7,6},{8,9},{9,8},{10,11... | collective-permute-start | bytes 688136 | tf_op jit(solution)/shard_map/ppermute | solution.py:64
  429.2 38.6 %collective-permute-start.19 = (bf16[256,2048]{1,0:T(8,128)(2,1)}, bf16[256,2048]{1,0:T(8,128)(2,1)}, u32[]{:S(2)}, u32[]{:S(2)}) collective-permute-start(bf16[256,2048]{1,0:T(8,128)(2,1)} %project_back.2), channel_id=1, source_target_pairs={{0,1},{1,0},{2,3},{3,2},{4,5},{5,4},{6,7},{7,6},{8,9},{9,8},{10,11... | collective-permute-start | bytes 3145736 | tf_op jit(solution)/shard_map/ppermute | solution.py:64
  441.4 26.3 %collective-permute-start.20 = (bf16[16,10752]{1,0:T(8,128)(2,1)}, bf16[16,10752]{1,0:T(8,128)(2,1)}, u32[]{:S(2)}, u32[]{:S(2)}) collective-permute-start(bf16[16,10752]{1,0:T(8,128)(2,1)} %pad_maximum_fusion.5), channel_id=1, source_target_pairs={{0,2},{1,3},{2,0},{3,1},{4,6},{5,7},{6,4},{7,5},{8,10},{9,11},{10,... | collective-permute-start | bytes 1032200 | tf_op jit(solution)/shard_map/ppermute | solution.py:64
  443.4 19.9 %collective-permute-start.21 = (bf16[16,2048]{1,0:T(8,128)(2,1)}, bf16[16,2048]{1,0:T(8,128)(2,1)S(1)}, u32[]{:S(2)}, u32[]{:S(2)}) collective-permute-start(bf16[16,2048]{1,0:T(8,128)(2,1)} %convert_element_type.112), channel_id=1, source_target_pairs={{0,1},{1,0},{2,3},{3,2},{4,5},{5,4},{6,7},{7,6},{8,9},{9,8},{10,11... | collective-permute-start | bytes 196616 | tf_op jit(solution)/shard_map/ppermute | solution.py:64
  445.4 17.9 %collective-permute-start.22 = (bf16[16,2048]{1,0:T(8,128)(2,1)}, bf16[16,2048]{1,0:T(8,128)(2,1)S(1)}, u32[]{:S(2)}, u32[]{:S(2)}) collective-permute-start(bf16[16,2048]{1,0:T(8,128)(2,1)} %convert_element_type.112), channel_id=1, source_target_pairs={{0,2},{1,3},{2,0},{3,1},{4,6},{5,7},{6,4},{7,5},{8,10},{9,11},{10,... | collective-permute-start | bytes 196616 | tf_op jit(solution)/shard_map/ppermute | solution.py:64
  445.5 22.3 %collective-permute-start.23 = (bf16[16,2048]{1,0:T(8,128)(2,1)}, bf16[16,2048]{1,0:T(8,128)(2,1)}, u32[]{:S(2)}, u32[]{:S(2)}) collective-permute-start(bf16[16,2048]{1,0:T(8,128)(2,1)} %convert_element_type.112), channel_id=1, source_target_pairs={{0,3},{1,2},{2,1},{3,0},{4,7},{5,6},{6,5},{7,4},{8,11},{9,10},{10,... | collective-permute-start | bytes 196616 | tf_op jit(solution)/shard_map/ppermute | solution.py:64
  474.3 40.2 %collective-permute-start.24 = (bf16[256,2048]{1,0:T(8,128)(2,1)}, bf16[256,2048]{1,0:T(8,128)(2,1)S(1)}, u32[]{:S(2)}, u32[]{:S(2)}) collective-permute-start(bf16[256,2048]{1,0:T(8,128)(2,1)} %get-tuple-element.238), channel_id=1, source_target_pairs={{0,1},{1,0},{2,3},{3,2},{4,5},{5,4},{6,7},{7,6},{8,9},{9,8},{10,11... | collective-permute-start | bytes 3145736 | tf_op jit(solution)/shard_map/ppermute | solution.py:64
  476.8 45.8 %collective-permute-start.25 = (bf16[256,2048]{1,0:T(8,128)(2,1)}, bf16[256,2048]{1,0:T(8,128)(2,1)}, u32[]{:S(2)}, u32[]{:S(2)}) collective-permute-start(bf16[256,2048]{1,0:T(8,128)(2,1)} %add_convert_fusion), channel_id=1, source_target_pairs={{0,2},{1,3},{2,0},{3,1},{4,6},{5,7},{6,4},{7,5},{8,10},{9,11},{10,... | collective-permute-start | bytes 3145736 | tf_op jit(solution)/shard_map/ppermute | solution.py:64
  (47 other events, 436.3 us)
Sparse Core Ops, SparseCore 0:
  139.4 43.8 all-gather.10
  185.7 54.3 all-gather.6
  242.6 54.3 all-gather.8
  469.8 28.3 all-gather.12

commit v3 on v2

--- a/solution.py
+++ b/solution.py
@@ -77,28 +77,40 @@
 def project_kernel(kept, at_ref, x_ref, gain_ref, bias_ref, aq_ref, bq_ref, wq_ref, *refs):
     merged_ref, normed_ref, z_ref, w_ref, out_ref, low_ref, thin_ref, sems, loads = refs[kept:]
     count = x_ref.shape[0]
-    weights = [pltpu.make_async_copy(wq_ref.at[i], w_ref.at[i], loads.at[i]) for i in range(wq_ref.shape[0])]
-    for copy in weights:
-        copy.start()
     rows = pl.ds(pl.multiple_of(at_ref[0] * count, count), count)
-
-    def norm(part):
+    parts = wq_ref.shape[0]
+
+    def load(i):
+        return pltpu.make_async_copy(wq_ref.at[i], w_ref.at[i], loads.at[i])
+
+    def save(i):
+        return pltpu.make_async_copy(out_ref.at[i], merged_ref.at[i, rows, :], sems.at[2 + i])
+
+    for i in range(parts):
+        load(i).start()
+
+    chunk = min(64, count)
+
+    def norm(i, carry):
+        part = pl.ds(pl.multiple_of(i * chunk, chunk), chunk)
         low_ref[part, :] = layer_norm(x_ref[part, :].astype(F32), gain_ref[...], bias_ref[...]).astype(BF16)
-
-    by_rows(count, norm)
-    normed = low_ref[...]
+        return carry
+
+    lax.fori_loop(0, count // chunk, norm, 0)
     copies = [pltpu.make_async_copy(low_ref, normed_ref.at[rows, :], sems.at[0])]
     copies[0].start()
-    inner = dot_nt(normed, aq_ref[...]).astype(BF16)
-    thin_ref[...] = inner
+    thin_ref[...] = dot_nt(low_ref[...], aq_ref[...]).astype(BF16)
     copies.append(pltpu.make_async_copy(thin_ref, z_ref.at[rows, :], sems.at[1]))
     copies[1].start()
-    for i in range(wq_ref.shape[0]):
-        weights[i].wait()
-        out_ref[i] = (dot_nn(normed, w_ref[i]) + dot_nn(inner, bq_ref[i])).astype(BF16)
-        copies.append(pltpu.make_async_copy(out_ref.at[i], merged_ref.at[i, rows, :], sems.at[2 + i]))
-        copies[-1].start()
-    for copy in copies:
+
+    def one(i, carry):
+        load(i).wait()
+        out_ref[i] = (dot_nn(low_ref[...], w_ref[i]) + dot_nn(thin_ref[...], bq_ref[i])).astype(BF16)
+        save(i).start()
+        return carry
+
+    lax.fori_loop(0, parts, one, 0)
+    for copy in copies + [save(i) for i in range(parts)]:
         copy.wait()
 
 
@@ -133,18 +145,12 @@
     return (lax.broadcasted_iota(jnp.int32, (1, 2 * HD), 1) // HD) == half
 
 
-def pair_scores(keys, query, seg_col, seg_row, slope, apart):
-    rows, cols = keys.shape[0], query.shape[0]
-    raw = dot_nt(keys, query)
-    delta = (
-        lax.broadcasted_iota(jnp.int32, (rows, cols), 0)
-        - lax.broadcasted_iota(jnp.int32, (rows, cols), 1)
-        - apart
-    )
+def allowed_pairs(seg_col, seg_row, causal):
+    dims = (seg_col.shape[0], seg_row.shape[1])
     allowed = seg_col == seg_row
-    if apart == 0:
-        allowed = allowed & (delta <= 0)
-    return jnp.where(allowed, raw + slope * delta.astype(F32), MASKED)
+    if causal:
+        allowed = allowed & (lax.broadcasted_iota(jnp.int32, dims, 0) <= lax.broadcasted_iota(jnp.int32, dims, 1))
+    return allowed
 
 
 def reach_of(block):
@@ -153,40 +159,39 @@
 
 def attend_kernel(block, count, first_ref, seg_ref, slope_ref, col_ref, row_ref, q_ref, k_ref, v_ref,
                   o_ref, stat_ref, turned_ref, top_ref, total_ref, sum_ref):
-    head = pl.program_id(0)
-    half = lax.rem(head, 2)
-    slope = slope_ref[head]
-    mask = lane_mask(half)
-    heads_rows = pl.ds(pl.multiple_of(half * HD, HD), HD)
-
-    @pl.when(half == 0)
-    def _():
-        turned_ref[...] = v_ref[0].T
+    pair = pl.program_id(0)
+    turned_ref[...] = v_ref[0].T
 
     for own in range(count):
         i = first_ref[0] + own
         start = pl.multiple_of(i * block, block)
         here = pl.ds(own * block, block)
-        scaled = jnp.where(mask, q_ref[0, pl.ds(start, block), :] * HD ** -0.5, 0).astype(BF16)
-        row = row_ref[:, pl.ds(start, block)]
+        query = q_ref[0, pl.ds(start, block), :] * HD ** -0.5
+        scaled = [jnp.where(lane_mask(half), query, 0).astype(BF16) for half in range(2)]
 
         def one(back):
             at = pl.multiple_of(start - back * block, block)
             keys = pl.ds(at, block)
-            scores = pair_scores(k_ref[0, keys, :], scaled, col_ref[keys, :1], row, slope, back * block)
-            best = jnp.max(scores, 0, keepdims=True)
-            if back:
-                best = jnp.maximum(best, top_ref[...])
-            weights = jnp.exp(scores - best)
-            total = jnp.sum(weights, 0, keepdims=True)
-            result = dot_nn(turned_ref[heads_rows, keys], weights.astype(BF16))
-            if back:
-                fade = jnp.exp(top_ref[...] - best)
-                total = total + fade * total_ref[...]
-                result = result + fade * sum_ref[...]
-            top_ref[...] = best
-            total_ref[...] = total
-            sum_ref[...] = result
+            allowed = allowed_pairs(col_ref[keys, :1], row_ref[:, pl.ds(start, block)], back == 0)
+            place = lax.broadcasted_iota(jnp.int32, (block, block), 0).astype(F32)
+            for half in range(2):
+                slope = slope_ref[2 * pair + half]
+                shift = slope * at.astype(F32)
+                scores = jnp.where(allowed, dot_nt(k_ref[0, keys, :], scaled[half]) + slope * place, MASKED)
+                best = jnp.max(scores, 0, keepdims=True) + shift
+                if back:
+                    before = top_ref[half]
+                    best = jnp.maximum(best, before)
+                weights = jnp.exp(scores - (best - shift))
+                total = jnp.sum(weights, 0, keepdims=True)
+                result = dot_nn(turned_ref[half * HD:(half + 1) * HD, keys], weights.astype(BF16))
+                if back:
+                    fade = jnp.exp(before - best)
+                    total = total + fade * total_ref[half]
+                    result = result + fade * sum_ref[half]
+                top_ref[half] = best
+                total_ref[half] = total
+                sum_ref[half] = result
 
         one(0)
         for back in range(1, reach_of(block) + 1):
@@ -196,10 +201,10 @@
             def _(back=back):
                 one(back)
 
-        stat_ref[0, :, here] = top_ref[...] + jnp.log(total_ref[...])
-        done = (sum_ref[...] / total_ref[...]).T
-        both = jnp.concatenate([done, done], 1)
-        o_ref[here, :] = jnp.where(mask, both, o_ref[here, :].astype(F32)).astype(BF16)
+        for half in range(2):
+            stat_ref[half, :, here] = top_ref[half] + jnp.log(total_ref[half])
+        done = jnp.concatenate([sum_ref[half] / total_ref[half] for half in range(2)], 0)
+        o_ref[here, :] = done.T.astype(BF16)
 
 
 def attend(first, merged, seg, slopes, count):
@@ -209,28 +214,28 @@
     col = jnp.broadcast_to(seg[:, None], (rows, 128))
 
     def part(i):
-        return pl.BlockSpec((1, rows, 2 * HD), lambda h, *_: (i, 0, h // 2))
+        return pl.BlockSpec((1, rows, 2 * HD), lambda h, *_: (i, 0, h))
 
     return pl.pallas_call(
         functools.partial(attend_kernel, block, count),
         out_shape=(shape((count * block, width)), shape((heads, 1, count * block), F32)),
         grid_spec=pltpu.PrefetchScalarGridSpec(
             num_scalar_prefetch=3,
-            grid=(heads,),
+            grid=(heads // 2,),
             in_specs=[
                 pl.BlockSpec((rows, 128), lambda h, *_: (0, 0)),
                 pl.BlockSpec((1, rows), lambda h, *_: (0, 0)),
                 part(0), part(1), part(2),
             ],
             out_specs=(
-                pl.BlockSpec((count * block, 2 * HD), lambda h, *_: (0, h // 2)),
-                pl.BlockSpec((1, 1, count * block), lambda h, *_: (h, 0, 0)),
+                pl.BlockSpec((count * block, 2 * HD), lambda h, *_: (0, h)),
+                pl.BlockSpec((2, 1, count * block), lambda h, *_: (h, 0, 0)),
             ),
             scratch_shapes=[
                 pltpu.VMEM((2 * HD, rows), BF16),
-                pltpu.VMEM((1, block), F32),
-                pltpu.VMEM((1, block), F32),
-                pltpu.VMEM((HD, block), F32),
+                pltpu.VMEM((2, 1, block), F32),
+                pltpu.VMEM((2, 1, block), F32),
+                pltpu.VMEM((2, HD, block), F32),
             ],
         ),
         name="attend",
@@ -239,38 +244,40 @@
 
 def attend_back_kernel(block, seg_ref, slope_ref, col_ref, row_ref, stat_ref, m_ref, g_ref, q_ref, k_ref, v_ref,
                        d_ref, turned_ref, center_ref, qsum_ref, ksum_ref, vsum_ref):
-    head = pl.program_id(0)
-    half = lax.rem(head, 2)
-    slope = slope_ref[head]
+    pair = pl.program_id(0)
     count = g_ref.shape[0] // block
-    mask = lane_mask(half)
-    rows = pl.ds(pl.multiple_of(half * HD, HD), HD)
-
-    @pl.when(half == 0)
-    def _():
-        turned_ref[...] = k_ref[0].T
-        product = (g_ref[...].astype(F32) * m_ref[...].astype(F32)).T
-        center_ref[0:1] = jnp.sum(product[:HD], 0, keepdims=True)
-        center_ref[1:2] = jnp.sum(product[HD:], 0, keepdims=True)
-        qsum_ref[...] = jnp.zeros_like(qsum_ref)
-        ksum_ref[...] = jnp.zeros_like(ksum_ref)
-        vsum_ref[...] = jnp.zeros_like(vsum_ref)
+    turned_ref[...] = k_ref[0].T
+    product = (g_ref[...].astype(F32) * m_ref[...].astype(F32)).T
+    for half in range(2):
+        center_ref[half:half + 1] = jnp.sum(product[half * HD:(half + 1) * HD], 0, keepdims=True)
+    qsum_ref[...] = jnp.zeros_like(qsum_ref)
+    ksum_ref[...] = jnp.zeros_like(ksum_ref)
+    vsum_ref[...] = jnp.zeros_like(vsum_ref)
 
     for i in range(count):
         queries = pl.ds(i * block, block)
-        scaled = jnp.where(mask, q_ref[0, queries, :] * HD ** -0.5, 0).astype(BF16)
-        grads = jnp.where(mask, g_ref[queries, :], 0).astype(BF16)
-        row = row_ref[:, queries]
+        query = q_ref[0, queries, :] * HD ** -0.5
+        scaled = [jnp.where(lane_mask(half), query, 0).astype(BF16) for half in range(2)]
+        grads = [jnp.where(lane_mask(half), g_ref[queries, :], 0).astype(BF16) for half in range(2)]
 
         def one(j):
             keys = pl.ds(j * block, block)
-            scores = pair_scores(k_ref[0, keys, :], scaled, col_ref[keys, :1], row, slope, (i - j) * block)
-            probs = jnp.exp(scores - stat_ref[0, :, queries])
-            d_probs = dot_nt(v_ref[0, keys, :], grads)
-            d_scores = (probs * (d_probs - center_ref[pl.ds(half, 1), queries])).astype(BF16)
-            vsum_ref[keys, :] += dot_nn(probs.astype(BF16), grads)
-            ksum_ref[keys, :] += dot_nn(d_scores, scaled)
-            qsum_ref[rows, queries] += dot_nn(turned_ref[rows, keys], d_scores)
+            allowed = allowed_pairs(col_ref[keys, :1], row_ref[:, queries], i == j)
+            place = lax.broadcasted_iota(jnp.int32, (block, block), 0).astype(F32)
+            val_part, key_part = 0.0, 0.0
+            for half in range(2):
+                slope = slope_ref[2 * pair + half]
+                shift = slope * float(j * block)
+                scores = jnp.where(allowed, dot_nt(k_ref[0, keys, :], scaled[half]) + slope * place, MASKED)
+                probs = jnp.exp(scores - (stat_ref[half, :, queries] - shift))
+                d_probs = dot_nt(v_ref[0, keys, :], grads[half])
+                d_scores = (probs * (d_probs - center_ref[half:half + 1, queries])).astype(BF16)
+                val_part = val_part + dot_nn(probs.astype(BF16), grads[half])
+                key_part = key_part + dot_nn(d_scores, scaled[half])
+                rows = slice(half * HD, (half + 1) * HD)
+                qsum_ref[rows, queries] += dot_nn(turned_ref[rows, keys], d_scores)
+            vsum_ref[keys, :] += val_part
+            ksum_ref[keys, :] += key_part
 
         one(i)
         for back in range(1, min(i, reach_of(block)) + 1):
@@ -280,35 +287,33 @@
             def _(j=j):
                 one(j)
 
-    @pl.when(half == 1)
-    def _():
-        d_ref[0] = (qsum_ref[...] * HD ** -0.5).T.astype(BF16)
-        d_ref[1] = ksum_ref[...].astype(BF16)
-        d_ref[2] = vsum_ref[...].astype(BF16)
+    d_ref[0] = (qsum_ref[...] * HD ** -0.5).T.astype(BF16)
+    d_ref[1] = ksum_ref[...].astype(BF16)
+    d_ref[2] = vsum_ref[...].astype(BF16)
 
 
 def attend_back(merged, mixed, grad, stat, seg, slopes):
     parts, rows, width = merged.shape
     block = min(256, rows)
-    wide = pl.BlockSpec((rows, 2 * HD), lambda h, *_: (0, h // 2))
+    wide = pl.BlockSpec((rows, 2 * HD), lambda h, *_: (0, h))
     col = jnp.broadcast_to(seg[:, None], (rows, 128))
 
     def part(i):
-        return pl.BlockSpec((1, rows, 2 * HD), lambda h, *_: (i, 0, h // 2))
+        return pl.BlockSpec((1, rows, 2 * HD), lambda h, *_: (i, 0, h))
 
     return pl.pallas_call(
         functools.partial(attend_back_kernel, block),
         out_shape=shape(merged.shape),
         grid_spec=pltpu.PrefetchScalarGridSpec(
             num_scalar_prefetch=2,
-            grid=(width // HD,),
+            grid=(width // (2 * HD),),
             in_specs=[
                 pl.BlockSpec((rows, 128), lambda h, *_: (0, 0)),
                 pl.BlockSpec((1, rows), lambda h, *_: (0, 0)),
-                pl.BlockSpec((1, 1, rows), lambda h, *_: (h, 0, 0)),
+                pl.BlockSpec((2, 1, rows), lambda h, *_: (h, 0, 0)),
                 wide, wide, part(0), part(1), part(2),
             ],
-            out_specs=pl.BlockSpec((parts, rows, 2 * HD), lambda h, *_: (0, 0, h // 2)),
+            out_specs=pl.BlockSpec((parts, rows, 2 * HD), lambda h, *_: (0, 0, h)),
             scratch_shapes=[
                 pltpu.VMEM((2 * HD, rows), BF16),
                 pltpu.VMEM((2, rows), F32),
@@ -322,53 +327,79 @@
 
 
 def dense_kernel(at_ref, x0_ref, x1_ref, m0_ref, m1_ref, m2_ref, m3_ref, a_ref, bd_ref, gain_ref, bias_ref, au_ref,
-                 own_ref, far_ref, middle_ref, second_ref, zd_ref, zu_ref, w_ref, m_ref, loads):
+                 own_ref, far_ref, middle_ref, second_ref, zd_ref, zu_ref, w_ref, m_ref, sum_ref, loads):
     size = m0_ref.shape[1]
     count = x0_ref.shape[0]
-    width = x0_ref.shape[1]
-    pieces, _, thick, _ = far_ref.shape
-    copies = [pltpu.make_async_copy(own_ref.reshape(pieces, thick, width), w_ref.at[0], loads.at[0])]
-    copies += [pltpu.make_async_copy(far_ref.at[:, r], w_ref.at[1 + r], loads.at[1 + r]) for r in range(3)]
-    for copy in copies:
-        copy.start()
+    tiles, pieces, _, thick, tile = w_ref.shape
+    near = at_ref[0] * count
+    away = (1 - at_ref[0]) * count
+
+    def columns(t):
+        return pl.ds(pl.multiple_of(t * tile, tile), tile)
+
+    def load(t):
+        cols = columns(t)
+        own = own_ref.reshape(pieces, thick, own_ref.shape[1]).at[:, :, cols]
+        far = far_ref.at[:, pl.ds(4, 3), :, cols]
+        return (
+            pltpu.make_async_copy(own, w_ref.at[t, :, 0], loads.at[0, t]),
+            pltpu.make_async_copy(far, w_ref.at[t, :, pl.ds(1, 3)], loads.at[1, t]),
+        )
+
+    def start(t, carry):
+        for copy in load(t):
+            copy.start()
+        return carry
+
+    lax.fori_loop(0, tiles, start, 0)
     for r, m in enumerate((m0_ref, m1_ref, m2_ref, m3_ref)):
         m_ref[:, r * size:(r + 1) * size] = m[...]
-    inner = dot_nt(m_ref[...], a_ref[...]).astype(BF16)
-    zd_ref[...] = inner
-    for copy in copies:
-        copy.wait()
-    weights = w_ref[...].reshape(4 * size, width)
-    swapped = at_ref[0] == 1
-    tile = min(512, width)
-    for i in range(2):
-        rows = slice(i * count, (i + 1) * count)
-        near, away = (x0_ref, x1_ref) if i == 0 else (x1_ref, x0_ref)
-        for j in range(width // tile):
-            cols = slice(j * tile, (j + 1) * tile)
-            x = jnp.where(swapped, away[:, cols], near[:, cols]).astype(F32)
-            middle_ref[rows, cols] = x + dot_nn(m_ref[rows, :], weights[:, cols]) + dot_nn(inner[rows], bd_ref[:, cols])
-
-    def norm(part):
-        second_ref[part, :] = layer_norm(middle_ref[part, :], gain_ref[...], bias_ref[...]).astype(BF16)
-
-    by_rows(2 * count, norm)
+    zd_ref[...] = dot_nt(m_ref[...], a_ref[...]).astype(BF16)
+
+    def one(t, carry):
+        cols = columns(t)
+        for copy in load(t):
+            copy.wait()
+        total = dot_nn(zd_ref[...], bd_ref[:, cols])
+        for r in range(4):
+            weights = w_ref[t, :, r].reshape(pieces * thick, tile)
+            total = total + dot_nn(m_ref[:, r * size:(r + 1) * size], weights)
+        sum_ref[:, cols] = total
+        for x_ref, start in ((x0_ref, near), (x1_ref, away)):
+            rows = pl.ds(pl.multiple_of(start, count), count)
+            sum_ref[rows, cols] += x_ref[:, cols].astype(F32)
+        return carry
+
+    lax.fori_loop(0, tiles, one, 0)
+    chunk = min(64, count)
+
+    def norm(i, carry):
+        part = pl.ds(pl.multiple_of(i * chunk, chunk), chunk)
+        values = sum_ref[part, :]
+        middle_ref[part, :] = values.astype(BF16)
+        second_ref[part, :] = layer_norm(values, gain_ref[...], bias_ref[...]).astype(BF16)
+        return carry
+
+    lax.fori_loop(0, 2 * count // chunk, norm, 0)
     zu_ref[...] = dot_nt(second_ref[...], au_ref[...]).astype(BF16)
 
 
 def dense(low, x_own, x_far, m_parts, ad, bd, gain, bias, au, w_own, w_far):
     count, width = x_own.shape
     rank = ad.shape[0]
+    tile = min(512, width)
+    pieces, _, thick, _ = w_far.shape
     return pl.pallas_call(
         dense_kernel,
         out_shape=(
-            shape((2 * count, width), F32), shape((2 * count, width)), shape((2 * count, rank)),
+            shape((2 * count, width)), shape((2 * count, width)), shape((2 * count, rank)),
             shape((2 * count, rank)),
         ),
         in_specs=[pl.BlockSpec(memory_space=pltpu.SMEM)] + [WHOLE] * 11 + [REMOTE] * 2,
         out_specs=(WHOLE,) * 4,
         scratch_shapes=[
-            pltpu.VMEM((4, w_far.shape[0]) + w_far.shape[2:], BF16), pltpu.VMEM((2 * count, width), BF16),
-            pltpu.SemaphoreType.DMA((4,)),
+            pltpu.VMEM((width // tile, pieces, 4, thick, tile), BF16), pltpu.VMEM((2 * count, width), BF16),
+            pltpu.VMEM((2 * count, width), F32), pltpu.SemaphoreType.DMA((2, width // tile)),
         ],
         name="dense",
     )(low.reshape(1), x_own, x_far, *m_parts, ad, bd, gain, bias, au, w_own, w_far)
@@ -376,36 +407,44 @@
 
 def feed_kernel(earlier, at_ref, x_ref, g_ref, up_ref, down_ref, zu_ref, dz_ref, bu_ref, an_ref, au_ref, *refs):
     step = pl.program_id(0)
-    total_ref, inner_ref = refs[-2:]
     if earlier:
-        before_ref, active_ref, hidden_ref, dz_out_ref, out_ref = refs[:-2]
+        before_ref, active_ref, hidden_ref, dz_out_ref, out_ref, total_ref, inner_ref, held_ref, sem = refs
+        count = held_ref.shape[0]
+        rows = pl.ds(pl.multiple_of(at_ref[0] * count, count), count)
     else:
-        active_ref, hidden_ref, dz_out_ref, out_ref = refs[:-2]
+        active_ref, hidden_ref, dz_out_ref, out_ref, total_ref, inner_ref = refs
 
     @pl.when(step == 0)
     def _():
-        total_ref[...] = before_ref[...] if earlier else jnp.zeros_like(total_ref)
+        if earlier:
+            pltpu.make_async_copy(before_ref.at[rows, :], held_ref, sem).start()
+        total_ref[...] = jnp.zeros_like(total_ref)
         inner_ref[...] = jnp.zeros_like(inner_ref)
 
-    hidden = dot_nn(x_ref[...], up_ref[...]) + dot_nn(zu_ref[...], bu_ref[...])
+    up = up_ref[...].reshape(x_ref.shape[1], hidden_ref.shape[1])
+    hidden = dot_nn(x_ref[...], up) + dot_nn(zu_ref[...], bu_ref[...])
     d_active = dot_nt(g_ref[...], down_ref[...]) + dot_nn(dz_ref[...], an_ref[...])
     active, slope = gelu_pair(hidden)
     active_ref[...] = active.astype(BF16)
     d_hidden = (d_active * slope).astype(BF16)
     hidden_ref[...] = d_hidden
-    total_ref[...] += dot_nt(d_hidden, up_ref[...])
+    total_ref[...] += dot_nt(d_hidden, up)
     inner_ref[...] += dot_nt(d_hidden, bu_ref[...])
 
     @pl.when(step == pl.num_programs(0) - 1)
     def _():
         inner = inner_ref[...].astype(BF16)
         dz_out_ref[...] = inner
-        out_ref[...] = (total_ref[...] + dot_nn(inner, au_ref[...])).astype(out_ref.dtype)
+        total = total_ref[...] + dot_nn(inner, au_ref[...])
+        if earlier:
+            pltpu.make_async_copy(before_ref.at[rows, :], held_ref, sem).wait()
+            total = total + held_ref[...]
+        out_ref[...] = total.astype(out_ref.dtype)
 
 
 def feed(at, count, x, g, up, down, zu, dz, bu, an, au, before, kind):
     width = x.shape[1]
-    ff = up.shape[1]
+    ff = up.shape[3]
     tile = min(512, ff)
     rank = bu.shape[0]
     earlier = before is not None
@@ -421,15 +460,17 @@
             num_scalar_prefetch=1,
             grid=(ff // tile,),
             in_specs=[
-                rows, rows, pl.BlockSpec((width, tile), lambda t, at: (0, t)),
+                rows, rows, pl.BlockSpec((up.shape[0], 4, up.shape[2], tile), lambda t, at: (0, 0, 0, t)),
                 pl.BlockSpec((tile, width), lambda t, at: (t, 0)), thin, thin, row, row,
                 pl.BlockSpec((rank, width), lambda t, at: (0, 0)),
-            ] + [rows] * earlier,
+            ] + [REMOTE] * earlier,
             out_specs=(
                 cols, cols, pl.BlockSpec((count, rank), lambda t, at: (0, 0)),
                 pl.BlockSpec((count, width), lambda t, at: (0, 0), pipeline_mode=once),
             ),
-            scratch_shapes=[pltpu.VMEM((count, width), F32), pltpu.VMEM((count, rank), F32)],
+            scratch_shapes=[pltpu.VMEM((count, width), F32), pltpu.VMEM((count, rank), F32)] + [
+                pltpu.VMEM((count, width), F32), pltpu.SemaphoreType.DMA(()),
+            ] * earlier,
         ),
         name="feed",
     )(at.reshape(1), x, g, up, down, zu, dz, bu, an, au, *((before,) if earlier else ()))
@@ -509,35 +550,41 @@
 
 
 def dense_back_kernel(low_ref, own_ref, far_ref, cot_ref, gain_ref, bd_ref, ad_ref, middle_ref, w0_ref, w1_ref,
-                      d_ref, low_out_ref, dz_ref, mixed_ref, mid_ref, w_ref, loads):
+                      low_out_ref, dz_ref, mixed_ref, mid_ref, w_ref, loads):
     count, width = own_ref.shape
     size = mixed_ref.shape[2]
     pieces, _, thick, _ = w1_ref.shape
     rows = pl.ds(pl.multiple_of(low_ref[0] * count, count), count)
     first = pltpu.make_async_copy(middle_ref.at[rows, :], mid_ref, loads.at[4])
     first.start()
-    copies = [pltpu.make_async_copy(w0_ref.reshape(pieces, thick, width), w_ref.at[0], loads.at[0])]
-    copies += [pltpu.make_async_copy(w1_ref.at[:, r], w_ref.at[1 + r], loads.at[1 + r]) for r in range(3)]
-    order = (3, 2, 1, 0)
-    for r in order:
-        copies[r].start()
+    pltpu.make_async_copy(w0_ref.reshape(pieces, thick, width), w_ref.at[0], loads.at[0]).start()
+
+    def start(r, carry):
+        pltpu.make_async_copy(w1_ref.at[:, r + 3], w_ref.at[r], loads.at[r]).start()
+        return carry
+
+    lax.fori_loop(1, 4, start, 0)
     first.wait()
-
-    def norm(part):
-        grad = own_ref[part, :] + far_ref[part, :].astype(F32)
-        d_middle = cot_ref[part, :].astype(F32) + norm_back(grad, mid_ref[part, :], gain_ref[...])
-        d_ref[part, :] = d_middle
-        low_out_ref[part, :] = d_middle.astype(BF16)
-
-    by_rows(count, norm)
-    low = low_out_ref[...]
-    inner = dot_nt(low, bd_ref[...]).astype(BF16)
-    dz_ref[...] = inner
-    for r in order:
-        copies[r].wait()
-        cols = slice(r * size, (r + 1) * size)
+    chunk = min(64, count)
+
+    def norm(i, carry):
+        part = pl.ds(pl.multiple_of(i * chunk, chunk), chunk)
+        grad = own_ref[part, :].astype(F32) + far_ref[part, :].astype(F32)
+        change = norm_back(grad, mid_ref[part, :].astype(F32), gain_ref[...])
+        low_out_ref[part, :] = (cot_ref[part, :].astype(F32) + change).astype(BF16)
+        return carry
+
+    lax.fori_loop(0, count // chunk, norm, 0)
+    dz_ref[...] = dot_nt(low_out_ref[...], bd_ref[...]).astype(BF16)
+
+    def one(r, carry):
+        pltpu.make_async_copy(w1_ref.at[:, 0], w_ref.at[r], loads.at[r]).wait()
         weights = w_ref[r].reshape(size, width)
-        mixed_ref[r] = (dot_nt(low, weights) + dot_nn(inner, ad_ref[:, cols])).astype(BF16)
+        cols = pl.ds(pl.multiple_of(r * size, size), size)
+        mixed_ref[r] = (dot_nt(low_out_ref[...], weights) + dot_nn(dz_ref[...], ad_ref[:, cols])).astype(BF16)
+        return carry
+
+    lax.fori_loop(0, 4, one, 0)
 
 
 def dense_back(low, own, far, middle, cot, gain, bd, ad, w_own, w_far):
@@ -545,11 +592,11 @@
     rank = bd.shape[0]
     return pl.pallas_call(
         dense_back_kernel,
-        out_shape=(shape((count, width), F32), shape((count, width)), shape((count, rank)), shape((4, count, width // 4))),
+        out_shape=(shape((count, width)), shape((count, rank)), shape((4, count, width // 4))),
         in_specs=[pl.BlockSpec(memory_space=pltpu.SMEM)] + [WHOLE] * 6 + [REMOTE] * 3,
-        out_specs=(WHOLE,) * 4,
+        out_specs=(WHOLE,) * 3,
         scratch_shapes=[
-            pltpu.VMEM((count, width), F32), pltpu.VMEM((4, w_far.shape[0]) + w_far.shape[2:], BF16),
+            pltpu.VMEM((count, width), BF16), pltpu.VMEM((4, w_far.shape[0]) + w_far.shape[2:], BF16),
             pltpu.SemaphoreType.DMA((5,)),
         ],
         name="dense_back",
@@ -557,42 +604,62 @@
 
 
 def project_back_kernel(order, at_ref, aq_ref, bq_ref, d_ref, wq_ref, *refs):
-    outs, part_ref, w_ref, sems, loads = refs[:-4], *refs[-4:]
+    outs = refs[:len(order)]
+    part_ref, w_ref, inner_ref, sems, loads = refs[len(order):]
     count = outs[0].shape[0]
+    tiles, _, tile, _ = w_ref.shape
+
+    def columns(t):
+        return pl.ds(pl.multiple_of(t * tile, tile), tile)
 
     def fetch(place):
         rows = pl.ds(pl.multiple_of((at_ref[0] ^ order[place]) * count, count), count)
-        return pltpu.make_async_copy(d_ref.at[:, rows, :], part_ref.at[place], sems.at[place])
+        here = pl.ds(place * count, count)
+        return pltpu.make_async_copy(d_ref.at[:, rows, :], part_ref.at[:, here, :], sems.at[place])
+
+    def load(t):
+        return pltpu.make_async_copy(wq_ref.at[:, columns(t), :], w_ref.at[t], loads.at[t])
+
+    def start(t, carry):
+        load(t).start()
+        return carry
 
     blocks = [fetch(place) for place in range(len(order))]
-    weights = [pltpu.make_async_copy(wq_ref.at[i], w_ref.at[i], loads.at[i]) for i in range(3)]
-    blocks[0].start()
-    for copy in weights + blocks[1:]:
+    for copy in blocks:
         copy.start()
-    for place, out in enumerate(outs):
-        blocks[place].wait()
-        parts = [part_ref[place, i] for i in range(3)]
-        inner = sum(dot_nt(d, bq_ref[i]) for i, d in enumerate(parts)).astype(BF16)
-        total = dot_nn(inner, aq_ref[...])
+    lax.fori_loop(0, tiles, start, 0)
+    for copy in blocks:
+        copy.wait()
+    inner_ref[...] = sum(dot_nt(part_ref[i], bq_ref[i]) for i in range(3)).astype(BF16)
+
+    def one(t, carry):
+        load(t).wait()
+        cols = columns(t)
+        total = dot_nn(inner_ref[...], aq_ref[:, cols])
         for i in range(3):
-            if place == 0:
-                weights[i].wait()
-            total = total + dot_nt(parts[i], w_ref[i])
-        out[...] = total.astype(out.dtype)
-
-
-def project_back(at, d_merged, wq, aq, bq, order, kinds):
+            total = total + dot_nt(part_ref[i], w_ref[t, i])
+        for place, out in enumerate(outs):
+            out[:, cols] = total[place * count:(place + 1) * count].astype(BF16)
+        return carry
+
+    lax.fori_loop(0, tiles, one, 0)
+
+
+def project_back(at, d_merged, wq, aq, bq, order):
     parts, total, local_width = d_merged.shape
     width = wq.shape[1]
     count = total // 4
+    tile = min(512, width)
+    rows = len(order) * count
     return pl.pallas_call(
         functools.partial(project_back_kernel, order),
-        out_shape=tuple(shape((count, width), k) for k in kinds),
+        out_shape=(shape((count, width)),) * len(order),
         in_specs=[pl.BlockSpec(memory_space=pltpu.SMEM)] + [WHOLE] * 2 + [REMOTE] * 2,
         out_specs=(WHOLE,) * len(order),
         scratch_shapes=[
-            pltpu.VMEM((len(order), parts, count, local_width), BF16), pltpu.VMEM(wq.shape, BF16),
-            pltpu.SemaphoreType.DMA((len(order),)), pltpu.SemaphoreType.DMA((3,)),
+            pltpu.VMEM((parts, rows, local_width), BF16), pltpu.VMEM((width // tile, parts, tile, local_width), BF16),
+            pltpu.VMEM((rows, aq.shape[0]), BF16),
+            pltpu.SemaphoreType.DMA((len(order),)), pltpu.SemaphoreType.DMA((width // tile,)),
         ],
         name="project_back",
     )(at.reshape(1), aq, bq, d_merged, wq)
@@ -678,6 +745,26 @@
         ),
         name="spread",
     )(ids, first, second)
+
+
+def last_kernel(kept_ref, one_ref, two_ref, x_ref, d_ref, gain_ref, out_ref):
+    grad = kept_ref[...].astype(F32) + one_ref[...].astype(F32) + two_ref[...].astype(F32)
+    change = norm_back(grad, x_ref[...].astype(F32), gain_ref[...])
+    out_ref[...] = (d_ref[...].astype(F32) + change).astype(BF16)
+
+
+def last_norm(kept, one, two, x, d, gain):
+    count, width = x.shape
+    chunk = min(64, count)
+    rows = pl.BlockSpec((chunk, width), lambda i: (i, 0))
+    return pl.pallas_call(
+        last_kernel,
+        out_shape=shape((count, width)),
+        grid=(count // chunk,),
+        in_specs=[rows] * 5 + [pl.BlockSpec((1, width), lambda i: (0, 0))],
+        out_specs=rows,
+        name="last_norm",
+    )(kept, one, two, x, d, gain)
 
 
 def turned(factor, which):
@@ -750,11 +837,9 @@
     m_two = swap(other, "mp", 2)
     bu_far, an_far = pack_two[last:last + rank], pack_two[last + rank:]
     packs = (pack_one[:last], pack_two, pack_one[last:])
-    wd_slices = jnp.concatenate([p[:size] for p in packs], 0)
-    wd_far = lax.all_gather(wd_slices, "dp", axis=0).reshape(copies, 3, size, width)
+    slices = jnp.concatenate([wu_first, wu_second, *(p[:size] for p in packs)], 0)
+    shared = lax.all_gather(slices, "dp", axis=0).reshape(copies, 7, size, width)
     ad = jnp.concatenate([ad] + [p[size:last].reshape(rank, local_width) for p in packs], 1)
-    wu_slice = after(jnp.concatenate([wu_first, wu_second], 0), wd_slices)
-    wu_far = lax.all_gather(wu_slice, "dp", axis=0, tiled=True)
     mine, stat_mine = attend(2 * high, merged, seg, slopes, 2)
     m_two, mine = lax.optimization_barrier((m_two, mine))
 
@@ -772,7 +857,7 @@
         return jnp.where(low == 0, jnp.concatenate([own, far], 0), jnp.concatenate([far, own], 0))
 
     middle, second, z_dense, z_up = dense(
-        low, layer_in, x_one, m_parts, ad, bd, second_gain, second_bias, au, w_dense, wd_far
+        low, layer_in, x_one, m_parts, ad, bd, second_gain, second_bias, au, w_dense, shared
     )
     wn_second, second, cot_far = lax.optimization_barrier((wn_second, second, cot_far))
     wn_far = lax.all_gather(jnp.concatenate([wn_first, wn_second], 0), "dp", axis=0, tiled=True)
@@ -781,16 +866,16 @@
     dz_down = dot_nt(cot_pair, bn).astype(BF16)
     zero = jnp.zeros((), jnp.int32)
     act, dh, dzu, so_far = feed(
-        zero, 2 * own_rows, second, cot_pair, w_up, w_down, z_up, dz_down, bu, an, au, None, F32
+        zero, 2 * own_rows, second, cot_pair, w_up.reshape(copies, 4, size, width), w_down, z_up, dz_down, bu, an, au, None, F32
     )
     gn_own, gu_own, zn, out_so_far = emit(zero, (act,), (dh,), w_down, an, bn, z_up, dz_down, None)
     out_so_far, so_far = lax.optimization_barrier((out_so_far, so_far))
-    far_args = (second, cot_pair, wu_far, wn_far, z_up, dz_down, bu_far, an_far, au, so_far)
+    far_args = (second, cot_pair, shared, wn_far, z_up, dz_down, bu_far, an_far, au, so_far)
     act_a, dh_a, dzu_a, d_send = feed(1 - low, own_rows, *far_args, BF16)
     low_late, d_send = lax.optimization_barrier((low, d_send))
 
     d_near = swap(d_send, "mp", 1)
-    act_b, dh_b, dzu_b, d_own = feed(low_late, own_rows, *far_args, F32)
+    act_b, dh_b, dzu_b, d_own = feed(low_late, own_rows, *far_args, BF16)
     gn_far, gu_far, zn_far, out_send, out_own = emit(
         low, (act_a, act_b), (dh_a, dh_b), wn_far, an_far, bn, z_up, dz_down, out_so_far
     )
@@ -808,8 +893,8 @@
     stat = halves(stat_mine, stat_other, 2)
     d_near, out_send, mixed, stat = lax.optimization_barrier((d_near, out_send, mixed, stat))
 
-    d_middle, d_low, dz_dense, d_mixed = dense_back(
-        low, d_own, d_near, middle, cotangent, second_gain, bd, ad, w_dense, wd_far
+    d_low, dz_dense, d_mixed = dense_back(
+        low, d_own, d_near, middle, cotangent, second_gain, bd, ad, w_dense, shared
     )
     d_mixed, d_low, dz_dense = lax.optimization_barrier((d_mixed, d_low, dz_dense))
     g_blocks = [d_mixed[0]] + [swap(d_mixed[r], "mp", r) for r in (1, 2, 3)]
@@ -818,40 +903,37 @@
     gb_dense = dot_tn(own(z_dense), d_low)
     gd = [dot_tn(dz_dense, own(m)) for m in m_parts]
     sums = jnp.concatenate([ga_up, gb_down, gb_dense], 1)
-    near_in = jnp.concatenate([sums, gd[1], gd[3]], 1).astype(BF16)
-    *g_blocks, near_in = lax.optimization_barrier((*g_blocks, near_in))
-
-    near = swap(near_in, "mp", 1)
-    out_near = swap(after(out_send, near_in), "mp", 1)
+    near = swap(jnp.concatenate([sums, gd[1], gd[3]], 1).astype(BF16), "mp", 1)
+    *g_blocks, near = lax.optimization_barrier((*g_blocks, near))
+
+    near = near.astype(F32)
+    sums = sums + near[:, :3 * width]
+    gd_own = gd[0] + near[:, 3 * width:3 * width + local_width]
+    gd_far = gd[2] + near[:, 3 * width + local_width:]
+    mate = swap(jnp.concatenate([sums.astype(BF16), gu_far, gn_far, gd_far.astype(BF16)], 1), "mp", 2)
+    out_near = swap(after(out_send, near), "mp", 1)
     grad = jnp.zeros((total_rows, local_width), BF16)
     for r, block in enumerate(g_blocks):
         grad = lax.dynamic_update_slice_in_dim(grad, block, (index ^ r) * own_rows, 0)
     d_merged = attend_back(merged, mixed, grad, stat, seg, slopes)
-    (send,) = project_back(index, d_merged, wq, aq, bq, (3,), (BF16,))
-    send, d_merged, near, out_near = lax.optimization_barrier((send, d_merged, near, out_near))
+    (send,) = project_back(index, d_merged, wq, aq, bq, (3,))
+    send, d_merged, mate, out_near = lax.optimization_barrier((send, d_merged, mate, out_near))
 
     relay = swap(send, "mp", 1)
-    ga_qkv, gb_qkv = inner_grads(d_merged, z_qkv, normed, bq)
-    ga_low = ga_qkv.astype(BF16)
-    near = near.astype(F32)
-    sums = sums + near[:, :3 * width]
-    gd_own = gd[0] + near[:, 3 * width:3 * width + local_width]
-    gd_far = gd[2] + near[:, 3 * width + local_width:]
-    mate_in = jnp.concatenate([sums.astype(BF16), gu_far, gn_far, gd_far.astype(BF16)], 1)
-    ga_low, mate_in, d_merged = lax.optimization_barrier((ga_low, mate_in, d_merged))
-    ga_others = [swap(ga_low, "mp", r) for r in (1, 2, 3)]
-    mate = swap(mate_in, "mp", 2)
-    send_two, send_one, kept = project_back(index, d_merged, wq, aq, bq, (2, 1, 0), (F32, BF16, F32))
-    relay, kept, send_one, send_two, mate, *ga_others = lax.optimization_barrier(
-        (relay, kept, send_one, send_two, mate, *ga_others)
-    )
-
-    d_two = swap((send_two + relay.astype(F32)).astype(BF16), "mp", 2)
-    d_one = swap(send_one, "mp", 1)
-    layer_out = (own(middle) + out_own + out_near.astype(F32)).astype(BF16)
     first_pack = jnp.concatenate([sums, gu_own, gn_own, gd_own], 1) + mate.astype(F32)
     first_pack = jnp.concatenate([first_pack.astype(BF16), jnp.full((rank, 128), which, BF16)], 1)
     first_pack = lax.all_gather(first_pack, "dp", axis=0)
+    ga_qkv, gb_qkv = inner_grads(d_merged, z_qkv, normed, bq)
+    ga_low, d_merged = lax.optimization_barrier((ga_qkv.astype(BF16), d_merged))
+    ga_others = [swap(ga_low, "mp", r) for r in (1, 2, 3)]
+    send_two, send_one, kept = project_back(index, d_merged, wq, aq, bq, (2, 1, 0))
+    relay, send_one, send_two, kept, *ga_others = lax.optimization_barrier(
+        (relay, send_one, send_two, kept, *ga_others)
+    )
+
+    d_two = swap((send_two.astype(F32) + relay.astype(F32)).astype(BF16), "mp", 2)
+    d_one = swap(send_one, "mp", 1)
+    layer_out = (own(middle).astype(F32) + out_own + out_near.astype(F32)).astype(BF16)
     ga_qkv = ga_qkv + sum(g.astype(F32) for g in ga_others)
     second_pack = jnp.concatenate([ga_qkv, gb_qkv], 1).astype(BF16)
     second_pack = lax.all_gather(second_pack, "dp", axis=0)
@@ -860,8 +942,7 @@
         ids, first_pack, second_pack, kinds, width, local_width, local_ff
     )
     d_one, d_two = lax.optimization_barrier((d_one, d_two, gb_qkv))[:2]
-    d_first = kept + d_one.astype(F32) + d_two.astype(F32)
-    input_grad = (d_middle + norm_back(d_first, layer_in.astype(F32), first_gain)).astype(BF16)
+    input_grad = last_norm(kept, d_one, d_two, layer_in, d_low, first_gain)
     return (
         layer_out,
         input_grad,

time: 545 us -> 509 us (0.934)
  the two profiles are of different devices: /device:TPU:0 before, /device:TPU:2 now
where the time goes in v3:
time: 509 us; the launch traced here: 501 us
  Pallas kernels  217 us (43%)
  waiting for transfers between devices  162 us (32%)
  starting transfers between devices  34.1 us (7%)
  local copies, waits for them, and re-layouts  30.9 us (6%)
  other arithmetic  22.8 us (4%)
  between operations  15.8 us (3%)
  blocking collectives  10.8 us (2%)
  matrix products  7.3 us (1%)
    ppermute x26, waiting for transfers between devices, swap(): return lax.ppermute(value, axis, pairs)  135 us
    pallas_call x3, Pallas kernels, feed(): pl.pallas_call(functools.partial(feed_kernel, earlier), out_shape=(shape(...  51.2 us
    ppermute x26, starting transfers between devices, swap(): return lax.ppermute(value, axis, pairs)  33.8 us
    pallas_call x2, Pallas kernels, attend(): pl.pallas_call(functools.partial(attend_kernel, block, count), out_shape=...  29.5 us
    pallas_call x2, Pallas kernels, emit(): pl.pallas_call(functools.partial(emit_kernel, earlier), out_shape=(shape(...  25.5 us
    pallas_call x4, Pallas kernels, project(): pl.pallas_call(functools.partial(project_kernel, kept), out_shape=(shape(...  24.3 us
    pallas_call x1, Pallas kernels, attend_back(): pl.pallas_call(functools.partial(attend_back_kernel, block), out_shape=sh...  24 us
    pallas_call x2, Pallas kernels, project_back(): pl.pallas_call(functools.partial(project_back_kernel, order), out_shape=(...  17.6 us
  transfers between devices with their start and end apart: 29, of which 10 were waited for; matrix products, arithmetic and copies ran while one was open for 10% of the time, Pallas kernels for 38%

profile of v3, /device:TPU:2, one launch (start us, length us, event | category | flops | bytes accessed | tf_op | source)
XLA Modules:
  0.0 500.5 jit_solution(11891760530374065319)
XLA Ops:
  17.5 6.1 %project.4 = (bf16[3,1024,512]{2,1,0:T(8,128)(2,1)}, bf16[1024,2048]{1,0:T(8,128)(2,1)}, bf16[1024,16]{1,0:T(8,128)(2,1)}) custom-call(s32[1]{0:T(128)} %bitcast.1.at_ref, bf16[256,2048]{1,0:T(8,128)(2,1)} %x_ref.3, bf16[1,2048]{1,0:T(2,128)(2,1)} %broadcast_in_dim.12.gain_ref, bf16[1,2048]{1,0:T(2,128)(2,1)} %broadcast_in_dim.13.bias_ref, ...), custom_call_target="tpu_custom_call" | custom-call | tf_op jit(solution)/shard_map/project/pallas_call | solution.py:122
  25.4 29.3 %collective-permute-done.x_ref.x1_ref = bf16[256,2048]{1,0:T(8,128)(2,1)S(1)} collective-permute-done((bf16[256,2048]{1,0:T(8,128)(2,1)}, bf16[256,2048]{1,0:T(8,128)(2,1)S(1)}, u32[]{:S(2)}, u32[]{:S(2)}) %collective-permute-start) | collective-permute-done | bytes 1048608 | tf_op jit(solution)/shard_map/ppermute | solution.py:64
  64.6 6.1 %project.5 = (bf16[3,1024,512]{2,1,0:T(8,128)(2,1)}, bf16[1024,2048]{1,0:T(8,128)(2,1)}, bf16[1024,16]{1,0:T(8,128)(2,1)}) custom-call(s32[1]{0:T(128)} %bitcast.18.at_ref, bf16[256,2048]{1,0:T(8,128)(2,1)} %copy-done.9, bf16[1,2048]{1,0:T(2,128)(2,1)} %broadcast_in_dim.12.gain_ref, ...), custom_call_target="tpu_custom_call", output_to_operand_aliasing={{0}: (7, {}), {1}: (8, {}), {2}: (9, {})} | custom-call | tf_op jit(solution)/shard_map/project/pallas_call | solution.py:122
  70.6 6.1 %project.6 = (bf16[3,1024,512]{2,1,0:T(8,128)(2,1)}, bf16[1024,2048]{1,0:T(8,128)(2,1)}, bf16[1024,16]{1,0:T(8,128)(2,1)}) custom-call(s32[1]{0:T(128)} %bitcast.15.at_ref, bf16[256,2048]{1,0:T(8,128)(2,1)} %collective-permute-done.1.x_ref, bf16[1,2048]{1,0:T(2,128)(2,1)} %broadcast_in_dim.12.gain_ref, ...), custom_call_target="tpu_custom_call", output_to_operand_aliasing={{0}: (7, {}), {1}: (8, {}), {2}: (9, {})} | custom-call | tf_op jit(solution)/shard_map/project/pallas_call | solution.py:122
  76.8 28.1 %collective-permute-done.3 = bf16[100,2048]{1,0:T(8,128)(2,1)S(1)} collective-permute-done((bf16[100,2048]{1,0:T(8,128)(2,1)}, bf16[100,2048]{1,0:T(8,128)(2,1)S(1)}, u32[]{:S(2)}, u32[]{:S(2)}) %collective-permute-start.3) | collective-permute-done | bytes 409632 | tf_op jit(solution)/shard_map/ppermute | solution.py:64
  106.7 6.1 %project.7 = (bf16[3,1024,512]{2,1,0:T(8,128)(2,1)}, bf16[1024,2048]{1,0:T(8,128)(2,1)}, bf16[1024,16]{1,0:T(8,128)(2,1)}) custom-call(s32[1]{0:T(128)} %bitcast.10.at_ref, bf16[256,2048]{1,0:T(8,128)(2,1)} %collective-permute-done.2.x_ref, bf16[1,2048]{1,0:T(2,128)(2,1)} %broadcast_in_dim.12.gain_ref, ...), custom_call_target="tpu_custom_call", output_to_operand_aliasing={{0}: (7, {}), {1}: (8, {}), {2}: (9, {})} | custom-call | tf_op jit(solution)/shard_map/project/pallas_call | solution.py:122
  113.8 17.7 %attend.2 = (bf16[512,512]{1,0:T(8,128)(2,1)}, f32[8,1,512]{2,1,0:T(1,128)}) custom-call(s32[1]{0:T(128)} %bitcast.8.first_ref, s32[1024]{0:T(1024)} %bitcast.85, f32[8]{0:T(128)} %multiply_exponential_fusion.slope_ref, s32[1024,128]{1,0:T(8,128)} %broadcast_in_dim.14.col_ref, s32[1,1024]{1,0:T(1,128)} %row_ref.5, ...), custom_call_target="tpu_custom_call" | custom-call | tf_op jit(solution)/shard_map/attend/pallas_call | solution.py:219
  135.9 11.8 %attend.3 = (bf16[512,512]{1,0:T(8,128)(2,1)}, f32[8,1,512]{2,1,0:T(1,128)}) custom-call(s32[1]{0:T(128)} %bitcast.19.first_ref, s32[1024]{0:T(1024)} %bitcast.86, f32[8]{0:T(128)} %multiply_exponential_fusion.slope_ref, s32[1024,128]{1,0:T(8,128)} %broadcast_in_dim.14.col_ref, s32[1,1024]{1,0:T(1,128)} %row_ref.5, ...), custom_call_target="tpu_custom_call" | custom-call | tf_op jit(solution)/shard_map/attend/pallas_call | solution.py:219
  147.7 8.0 %collective-permute-done.7.m2_ref = bf16[512,512]{1,0:T(8,128)(2,1)S(1)} collective-permute-done((bf16[512,512]{1,0:T(8,128)(2,1)}, bf16[512,512]{1,0:T(8,128)(2,1)S(1)}, u32[]{:S(2)}, u32[]{:S(2)}) %collective-permute-start.7) | collective-permute-done | bytes 524320 | tf_op jit(solution)/shard_map/ppermute | solution.py:64
  160.8 30.1 %collective-permute-done.8.m1_ref = bf16[512,512]{1,0:T(8,128)(2,1)S(1)} collective-permute-done((bf16[512,512]{1,0:T(8,128)(2,1)S(1)}, bf16[512,512]{1,0:T(8,128)(2,1)S(1)}, u32[]{:S(2)}, u32[]{:S(2)}) %collective-permute-start.8) | collective-permute-done | bytes 524320 | tf_op jit(solution)/shard_map/ppermute | solution.py:64
  198.3 15.7 %all-gather.8.cloned.1.call-done = bf16[3584,2048]{1,0:T(8,128)(2,1)} async-done(((bf16[448,2048]{1,0:T(8,128)(2,1)}), bf16[3584,2048]{1,0:T(8,128)(2,1)}) %all-gather.8.cloned.1.call-update) | async-done | bytes 14680080 | tf_op jit(solution)/shard_map/all_gather | solution.py:841
  214.1 14.0 %dense.1 = (bf16[512,2048]{1,0:T(8,128)(2,1)}, bf16[512,2048]{1,0:T(8,128)(2,1)}, bf16[512,16]{1,0:T(8,128)(2,1)}, bf16[512,16]{1,0:T(8,128)(2,1)}) custom-call(s32[1]{0:T(128)} %bitcast.at_ref.low_ref, bf16[256,2048]{1,0:T(8,128)(2,1)} %x_ref.3, bf16[256,2048]{1,0:T(8,128)(2,1)} %copy-done.9, bf16[512,512]{1,0:T(8,128)(2,1)} %get-tuple-element.158.m0_ref, ...), custom_call_target="tpu_custom_call" | custom-call | tf_op jit(solution)/shard_map/dense/pallas_call | solution.py:392
  232.5 3.2 maximum_select_fusion.g_ref
  237.2 24.0 %feed.3 = (bf16[512,2048]{1,0:T(8,128)(2,1)}, bf16[512,2048]{1,0:T(8,128)(2,1)}, bf16[512,16]{1,0:T(8,128)(2,1)}, f32[512,2048]{1,0:T(8,128)}) custom-call(s32[1]{0:T(128)} %constant.61.clone.1.at_ref, bf16[512,2048]{1,0:T(8,128)(2,1)} %get-tuple-element.171.x_ref, bf16[512,2048]{1,0:T(8,128)(2,1)} %copy-done.2, bf16[8,4,64,2048]{3,2,1,0:T(8,128)(2,1)} %bitcast.82, ...), custom_call_target="tpu_custom_call" | custom-call | tf_op jit(solution)/shard_map/feed/pallas_call | solution.py:456
  261.1 11.8 %emit.2 = (bf16[16,2048]{1,0:T(8,128)(2,1)}, bf16[16,2048]{1,0:T(8,128)(2,1)}, bf16[512,16]{1,0:T(8,128)(2,1)}, f32[512,2048]{1,0:T(8,128)}) custom-call(s32[1]{0:T(128)} %constant.61.clone.1.at_ref, bf16[512,2048]{1,0:T(8,128)(2,1)} %get-tuple-element.176.refs_0_, bf16[512,2048]{1,0:T(8,128)(2,1)} %get-tuple-element.177.refs_1_, ...), custom_call_target="tpu_custom_call" | custom-call | tf_op jit(solution)/shard_map/emit/pallas_call | solution.py:531
  273.0 11.9 %all-gather.6.cloned.1.call-done.down_ref.refs_8_ = bf16[2048,2048]{1,0:T(8,128)(2,1)} async-done(((bf16[256,2048]{1,0:T(8,128)(2,1)}), bf16[2048,2048]{1,0:T(8,128)(2,1)}) %all-gather.6.cloned.1.call-update) | async-done | bytes 8388624 | tf_op jit(solution)/shard_map/all_gather | solution.py:863
  284.9 13.7 %feed.4 = (bf16[256,2048]{1,0:T(8,128)(2,1)}, bf16[256,2048]{1,0:T(8,128)(2,1)}, bf16[256,16]{1,0:T(8,128)(2,1)}, bf16[256,2048]{1,0:T(8,128)(2,1)}) custom-call(s32[1]{0:T(128)} %bitcast.25.at_ref, bf16[512,2048]{1,0:T(8,128)(2,1)} %get-tuple-element.171.x_ref, bf16[512,2048]{1,0:T(8,128)(2,1)} %copy-done.2, bf16[8,7,64,2048]{3,2,1,0:T(8,128)(2,1)} %bitcast.73, ...), custom_call_target="tpu_custom_call" | custom-call | tf_op jit(solution)/shard_map/feed/pallas_call | solution.py:456
  302.7 13.6 %feed.5 = (bf16[256,2048]{1,0:T(8,128)(2,1)}, bf16[256,2048]{1,0:T(8,128)(2,1)}, bf16[256,16]{1,0:T(8,128)(2,1)}, bf16[256,2048]{1,0:T(8,128)(2,1)}) custom-call(s32[1]{0:T(128)} %bitcast.30.at_ref, bf16[512,2048]{1,0:T(8,128)(2,1)} %get-tuple-element.171.x_ref, bf16[512,2048]{1,0:T(8,128)(2,1)} %copy-done.2, bf16[8,7,64,2048]{3,2,1,0:T(8,128)(2,1)} %bitcast.74, ...), custom_call_target="tpu_custom_call" | custom-call | tf_op jit(solution)/shard_map/feed/pallas_call | solution.py:456
  317.6 13.7 %emit.3 = (bf16[16,2048]{1,0:T(8,128)(2,1)}, bf16[16,2048]{1,0:T(8,128)(2,1)}, bf16[512,16]{1,0:T(8,128)(2,1)}, bf16[256,2048]{1,0:T(8,128)(2,1)}, f32[256,2048]{1,0:T(8,128)}) custom-call(s32[1]{0:T(128)} %bitcast.at_ref.low_ref, bf16[256,2048]{1,0:T(8,128)(2,1)} %get-tuple-element.181.refs_0_, bf16[256,2048]{1,0:T(8,128)(2,1)} %get-tuple-element.184.refs_1_, ...), custom_call_target="tpu_custom_call" | custom-call | tf_op jit(solution)/shard_map/emit/pallas_call | solution.py:531
  334.5 9.3 %dense_back.1 = (bf16[256,2048]{1,0:T(8,128)(2,1)}, bf16[256,16]{1,0:T(8,128)(2,1)}, bf16[4,256,512]{2,1,0:T(8,128)(2,1)}) custom-call(s32[1]{0:T(128)} %bitcast.at_ref.low_ref, bf16[256,2048]{1,0:T(8,128)(2,1)} %get-tuple-element.195.own_ref, bf16[256,2048]{1,0:T(8,128)(2,1)} %collective-permute-done.13.far_ref, bf16[256,2048]{1,0:T(8,128)(2,1)} %cot_ref.1, ...), custom_call_target="tpu_custom_call" | custom-call | tf_op jit(solution)/shard_map/dense_back/pallas_call | solution.py:593
  355.3 15.1 %collective-permute-done.17 = bf16[16,7168]{1,0:T(8,128)(2,1)S(1)} collective-permute-done((bf16[16,7168]{1,0:T(8,128)(2,1)}, bf16[16,7168]{1,0:T(8,128)(2,1)S(1)}, u32[]{:S(2)}, u32[]{:S(2)}) %collective-permute-start.17) | collective-permute-done | bytes 229408 | tf_op jit(solution)/shard_map/ppermute | solution.py:64
  378.7 24.0 %attend_back.1.d_ref = bf16[3,1024,512]{2,1,0:T(8,128)(2,1)} custom-call(s32[1024]{0:T(1024)} %bitcast.87, f32[8]{0:T(128)} %multiply_exponential_fusion.slope_ref, s32[1024,128]{1,0:T(8,128)} %broadcast_in_dim.14.col_ref, s32[1,1024]{1,0:T(1,128)} %row_ref.5, f32[8,1,1024]{2,1,0:T(1,128)} %broadcast_select_fusion.stat_ref, ...), custom_call_target="tpu_custom_call" | custom-call | tf_op jit(solution)/shard_map/attend_back/pallas_call | solution.py:304
  402.7 6.2 %project_back.2 = bf16[256,2048]{1,0:T(8,128)(2,1)} custom-call(s32[1]{0:T(128)} %bitcast.1.at_ref, bf16[16,2048]{1,0:T(8,128)(2,1)} %dynamic-slice_bitcast_fusion.5.aq_ref, bf16[3,16,512]{2,1,0:T(8,128)(2,1)} %dynamic-slice_bitcast_fusion.6.bq_ref, bf16[3,1024,512]{2,1,0:T(8,128)(2,1)} %attend_back.1.d_ref, bf16[3,2048,512]{2,1,0:T(8,128)(2,1)} %bitcast.80), custom_call_target="tpu_custom_call" | custom-call | tf_op jit(solution)/shard_map/project_back/pallas_call | solution.py:654
  413.3 7.0 %inner_grads.1 = (f32[16,2048]{1,0:T(8,128)}, f32[16,1536]{1,0:T(8,128)}) custom-call(bf16[3,1024,512]{2,1,0:T(8,128)(2,1)} %attend_back.1.d_ref, bf16[1024,16]{1,0:T(8,128)(2,1)} %get-tuple-element.221.z_ref, bf16[1024,2048]{1,0:T(8,128)(2,1)} %get-tuple-element.222.n_ref, bf16[3,16,512]{2,1,0:T(8,128)(2,1)} %dynamic-slice_bitcast_fusion.6.bq_ref), custom_call_target="tpu_custom_call" | custom-call | tf_op jit(solution)/shard_map/inner_grads/pallas_call | solution.py:688
  422.3 3.3 collective-permute-start.23
  425.6 3.4 add_convert_fusion.1
  429.0 11.4 %project_back.3 = (bf16[256,2048]{1,0:T(8,128)(2,1)}, bf16[256,2048]{1,0:T(8,128)(2,1)}, bf16[256,2048]{1,0:T(8,128)(2,1)}) custom-call(s32[1]{0:T(128)} %bitcast.1.at_ref, bf16[16,2048]{1,0:T(8,128)(2,1)} %dynamic-slice_bitcast_fusion.5.aq_ref, bf16[3,16,512]{2,1,0:T(8,128)(2,1)} %dynamic-slice_bitcast_fusion.6.bq_ref, ...), custom_call_target="tpu_custom_call" | custom-call | tf_op jit(solution)/shard_map/project_back/pallas_call | solution.py:654
  445.7 10.8 %all_gather.24.second_ref = bf16[8,16,3584]{2,1,0:T(8,128)(2,1)} all-gather(bf16[1,16,3584]{2,1,0:T(8,128)(2,1)S(1)} %pad_maximum_fusion.4), channel_id=1, replica_groups=mesh['dp'=8,'mp'=4] {'dp'}, dimensions={0}, use_global_device_ids=true | all-gather | bytes 1032192 | tf_op jit(solution)/shard_map/all_gather | solution.py:939
  458.0 8.9 %spread.1 = (f32[8,16,2048]{2,1,0:T(8,128)}, f32[8,16,2048]{2,1,0:T(8,128)}, f32[8,16,2048]{2,1,0:T(8,128)}, f32[8,16,2048]{2,1,0:T(8,128)}, f32[8,16,2048]{2,1,...) custom-call(s32[8]{0:T(128)} %fusion.23.ids_ref, ...), custom_call_target="tpu_custom_call" | custom-call | tf_op jit(solution)/shard_map/spread/pallas_call | solution.py:732
  466.9 16.4 %collective-permute-done.24.one_ref = bf16[256,2048]{1,0:T(8,128)(2,1)S(1)} collective-permute-done((bf16[256,2048]{1,0:T(8,128)(2,1)}, bf16[256,2048]{1,0:T(8,128)(2,1)S(1)}, u32[]{:S(2)}, u32[]{:S(2)}) %collective-permute-start.24) | collective-permute-done | bytes 1048608 | tf_op jit(solution)/shard_map/ppermute | solution.py:64
  483.3 5.0 %collective-permute-done.25.two_ref = bf16[256,2048]{1,0:T(8,128)(2,1)} collective-permute-done((bf16[256,2048]{1,0:T(8,128)(2,1)S(1)}, bf16[256,2048]{1,0:T(8,128)(2,1)}, u32[]{:S(2)}, u32[]{:S(2)}) %collective-permute-start.25) | collective-permute-done | bytes 1048608 | tf_op jit(solution)/shard_map/ppermute | solution.py:64
  488.3 5.1 %last_norm.1 = bf16[256,2048]{1,0:T(8,128)(2,1)} custom-call(bf16[256,2048]{1,0:T(8,128)(2,1)} %get-tuple-element.229.kept_ref, bf16[256,2048]{1,0:T(8,128)(2,1)} %copy-done.21, bf16[256,2048]{1,0:T(8,128)(2,1)} %collective-permute-done.25.two_ref, bf16[256,2048]{1,0:T(8,128)(2,1)} %x_ref.3, bf16[256,2048]{1,0:T(8,128)(2,1)} %get-tuple-element.207.d_ref, ...), custom_call_target="tpu_custom_call" | custom-call | tf_op jit(solution)/shard_map/last_norm/pallas_call | solution.py:760
  (226 shorter events, 87.8 us)
Async XLA Ops:
  7.2 206.9 %all-gather.8.cloned.1.call-start = ((), (), s32[]{:S(2)}) async-start(), calls=%async_computation.1 | async-start | bytes 16515072 | tf_op jit(solution)/shard_map/all_gather | solution.py:841
  7.2 47.5 %collective-permute-start = (bf16[256,2048]{1,0:T(8,128)(2,1)}, bf16[256,2048]{1,0:T(8,128)(2,1)S(1)}, u32[]{:S(2)}, u32[]{:S(2)}) collective-permute-start(bf16[256,2048]{1,0:T(8,128)(2,1)} %x_ref.3), channel_id=1, source_target_pairs={{0,1},{1,0},{2,3},{3,2},{4,5},{5,4},{6,7},{7,6},{8,9},{9,8},{10,11... | collective-permute-start | bytes 3145736 | tf_op jit(solution)/shard_map/ppermute | solution.py:64
  8.9 48.4 %collective-permute-start.1 = (bf16[256,2048]{1,0:T(8,128)(2,1)}, bf16[256,2048]{1,0:T(8,128)(2,1)}, u32[]{:S(2)}, u32[]{:S(2)}) collective-permute-start(bf16[256,2048]{1,0:T(8,128)(2,1)} %x_ref.3), channel_id=1, source_target_pairs={{0,2},{1,3},{2,0},{3,1},{4,6},{5,7},{6,4},{7,5},{8,10},{9,11},{10,... | collective-permute-start | bytes 3145736 | tf_op jit(solution)/shard_map/ppermute | solution.py:64
  24.4 46.2 %copy-start.19 = (bf16[16,2048]{1,0:T(8,128)(2,1)}, bf16[16,2048]{1,0:T(8,128)(2,1)S(1)}, u32[]{:S(2)}) copy-start(bf16[16,2048]{1,0:T(8,128)(2,1)S(1)} %dynamic-slice_bitcast_fusion.3.an_ref.refs_5_) | copy-start | bytes 196612
  57.3 47.7 %collective-permute-start.2 = (bf16[256,2048]{1,0:T(8,128)(2,1)}, bf16[256,2048]{1,0:T(8,128)(2,1)}, u32[]{:S(2)}, u32[]{:S(2)}) collective-permute-start(bf16[256,2048]{1,0:T(8,128)(2,1)} %collective-permute-done.1.x_ref), channel_id=1, source_target_pairs={{0,1},{1,0},{2,3},{3,2},{4,5},{5,4},{6,7},{7,6},{8,9},{9,8},{10,11... | collective-permute-start | bytes 3145736 | tf_op jit(solution)/shard_map/ppermute | solution.py:64
  60.8 44.1 %collective-permute-start.4 = (bf16[128,2048]{1,0:T(8,128)(2,1)}, bf16[128,2048]{1,0:T(8,128)(2,1)S(1)}, u32[]{:S(2)}, u32[]{:S(2)}) collective-permute-start(bf16[128,2048]{1,0:T(8,128)(2,1)} %get-tuple-element.136), channel_id=1, source_target_pairs={{0,2},{1,3},{2,0},{3,1},{4,6},{5,7},{6,4},{7,5},{8,10},{9,11},{10,... | collective-permute-start | bytes 1572872 | tf_op jit(solution)/shard_map/ppermute | solution.py:64
  64.3 40.6 %collective-permute-start.3 = (bf16[100,2048]{1,0:T(8,128)(2,1)}, bf16[100,2048]{1,0:T(8,128)(2,1)S(1)}, u32[]{:S(2)}, u32[]{:S(2)}) collective-permute-start(bf16[100,2048]{1,0:T(8,128)(2,1)} %pad_maximum_fusion.2), channel_id=1, source_target_pairs={{0,2},{1,3},{2,0},{3,1},{4,6},{5,7},{6,4},{7,5},{8,10},{9,11},{10,... | collective-permute-start | bytes 1228808 | tf_op jit(solution)/shard_map/ppermute | solution.py:64
  105.0 26.5 %collective-permute-start.5 = (bf16[136,2048]{1,0:T(8,128)(2,1)S(1)}, bf16[136,2048]{1,0:T(8,128)(2,1)S(1)}, u32[]{:S(2)}, u32[]{:S(2)}) collective-permute-start(bf16[136,2048]{1,0:T(8,128)(2,1)S(1)} %pad_maximum_fusion.1), channel_id=1, source_target_pairs={{0,1},{1,0},{2,3},{3,2},{4,5},{5,4},{6,7},{7,6},{8,9},{9,8},{10,11... | collective-permute-start | bytes 1671176 | tf_op jit(solution)/shard_map/ppermute | solution.py:64
  105.1 26.4 %collective-permute-start.6 = (bf16[128,2048]{1,0:T(8,128)(2,1)}, bf16[128,2048]{1,0:T(8,128)(2,1)}, u32[]{:S(2)}, u32[]{:S(2)}) collective-permute-start(bf16[128,2048]{1,0:T(8,128)(2,1)} %get-tuple-element.154), channel_id=1, source_target_pairs={{0,2},{1,3},{2,0},{3,1},{4,6},{5,7},{6,4},{7,5},{8,10},{9,11},{10,... | collective-permute-start | bytes 1572872 | tf_op jit(solution)/shard_map/ppermute | solution.py:64
  134.3 150.6 %all-gather.6.cloned.1.call-start = ((), (), s32[]{:S(2)}) async-start(), calls=%async_computation | async-start | bytes 9437184 | tf_op jit(solution)/shard_map/all_gather | solution.py:863
  134.5 21.2 %collective-permute-start.7 = (bf16[512,512]{1,0:T(8,128)(2,1)}, bf16[512,512]{1,0:T(8,128)(2,1)S(1)}, u32[]{:S(2)}, u32[]{:S(2)}) collective-permute-start(bf16[512,512]{1,0:T(8,128)(2,1)} %get-tuple-element.155), channel_id=1, source_target_pairs={{0,2},{1,3},{2,0},{3,1},{4,6},{5,7},{6,4},{7,5},{8,10},{9,11},{10,... | collective-permute-start | bytes 1572872 | tf_op jit(solution)/shard_map/ppermute | solution.py:64
  147.7 49.9 %slice-start = ((bf16[100,2048]{1,0:T(8,128)(2,1)}), bf16[4,2048]{1,0:T(4,128)(2,1)S(1)}, s32[]{:S(2)}) async-start(bf16[100,2048]{1,0:T(8,128)(2,1)} %copy-done.17), calls=%async_computation.3 | async-start | bytes 32768 | tf_op jit(solution)/shard_map/slice | solution.py:842
  155.7 58.3 %copy-start.13 = (bf16[512,512]{1,0:T(8,128)(2,1)}, bf16[512,512]{1,0:T(8,128)(2,1)S(1)}, u32[]{:S(2)}) copy-start(bf16[512,512]{1,0:T(8,128)(2,1)S(1)} %collective-permute-done.7.m2_ref) | copy-start | bytes 1572868
  155.7 35.1 %collective-permute-start.9 = (bf16[512,512]{1,0:T(8,128)(2,1)S(1)}, bf16[512,512]{1,0:T(8,128)(2,1)}, u32[]{:S(2)}, u32[]{:S(2)}) collective-permute-start(bf16[512,512]{1,0:T(8,128)(2,1)S(1)} %collective-permute-done.7.m2_ref), channel_id=1, source_target_pairs={{0,1},{1,0},{2,3},{3,2},{4,5},{5,4},{6,7},{7,6},{8,9},{9,8},{10,11... | collective-permute-start | bytes 1572872 | tf_op jit(solution)/shard_map/ppermute | solution.py:64
  156.8 34.0 %collective-permute-start.8 = (bf16[512,512]{1,0:T(8,128)(2,1)S(1)}, bf16[512,512]{1,0:T(8,128)(2,1)S(1)}, u32[]{:S(2)}, u32[]{:S(2)}) collective-permute-start(bf16[512,512]{1,0:T(8,128)(2,1)S(1)} %copy-done.10), channel_id=1, source_target_pairs={{0,1},{1,0},{2,3},{3,2},{4,5},{5,4},{6,7},{7,6},{8,9},{9,8},{10,11... | collective-permute-start | bytes 1572872 | tf_op jit(solution)/shard_map/ppermute | solution.py:64
  158.8 32.0 %collective-permute-start.10 = (bf16[128,2048]{1,0:T(8,128)(2,1)}, bf16[128,2048]{1,0:T(8,128)(2,1)S(1)}, u32[]{:S(2)}, u32[]{:S(2)}) collective-permute-start(bf16[128,2048]{1,0:T(8,128)(2,1)} %get-tuple-element.258), channel_id=1, source_target_pairs={{0,2},{1,3},{2,0},{3,1},{4,6},{5,7},{6,4},{7,5},{8,10},{9,11},{10,... | collective-permute-start | bytes 1572872 | tf_op jit(solution)/shard_map/ppermute | solution.py:64
  190.8 37.3 %collective-permute-start.12 = (bf16[256,2048]{1,0:T(8,128)(2,1)S(1)}, bf16[256,2048]{1,0:T(8,128)(2,1)}, u32[]{:S(2)}, u32[]{:S(2)}) collective-permute-start(bf16[256,2048]{1,0:T(8,128)(2,1)S(1)} %copy-done.6), channel_id=1, source_target_pairs={{0,1},{1,0},{2,3},{3,2},{4,5},{5,4},{6,7},{7,6},{8,9},{9,8},{10,11... | collective-permute-start | bytes 3145736 | tf_op jit(solution)/shard_map/ppermute | solution.py:64
  195.0 33.1 %collective-permute-start.11 = (bf16[128,2048]{1,0:T(8,128)(2,1)}, bf16[128,2048]{1,0:T(8,128)(2,1)}, u32[]{:S(2)}, u32[]{:S(2)}) collective-permute-start(bf16[128,2048]{1,0:T(8,128)(2,1)} %get-tuple-element.168), channel_id=1, source_target_pairs={{0,2},{1,3},{2,0},{3,1},{4,6},{5,7},{6,4},{7,5},{8,10},{9,11},{10,... | collective-permute-start | bytes 1572872 | tf_op jit(solution)/shard_map/ppermute | solution.py:64
  230.3 226.2 %all-gather.10.cloned.1.call-start = ((), (), s32[]{:S(2)}) async-start(), calls=%async_computation.2 | async-start | bytes 3133440 | tf_op jit(solution)/shard_map/all_gather | solution.py:925
  298.5 36.0 %collective-permute-start.13 = (bf16[256,2048]{1,0:T(8,128)(2,1)}, bf16[256,2048]{1,0:T(8,128)(2,1)}, u32[]{:S(2)}, u32[]{:S(2)}) collective-permute-start(bf16[256,2048]{1,0:T(8,128)(2,1)} %get-tuple-element.189), channel_id=1, source_target_pairs={{0,1},{1,0},{2,3},{3,2},{4,5},{5,4},{6,7},{7,6},{8,9},{9,8},{10,11... | collective-permute-start | bytes 3145736 | tf_op jit(solution)/shard_map/ppermute | solution.py:64
  346.1 24.3 %collective-permute-start.14 = (bf16[256,512]{1,0:T(8,128)(2,1)S(1)}, bf16[256,512]{1,0:T(8,128)(2,1)S(1)}, u32[]{:S(2)}, u32[]{:S(2)}) collective-permute-start(bf16[256,512]{1,0:T(8,128)(2,1)S(1)} %get-tuple-element.256), channel_id=1, source_target_pairs={{0,1},{1,0},{2,3},{3,2},{4,5},{5,4},{6,7},{7,6},{8,9},{9,8},{10,11... | collective-permute-start | bytes 786440 | tf_op jit(solution)/shard_map/ppermute | solution.py:64
  346.6 23.8 %collective-permute-start.15 = (bf16[256,512]{1,0:T(8,128)(2,1)S(1)}, bf16[256,512]{1,0:T(8,128)(2,1)S(1)}, u32[]{:S(2)}, u32[]{:S(2)}) collective-permute-start(bf16[256,512]{1,0:T(8,128)(2,1)S(1)} %get-tuple-element.255), channel_id=1, source_target_pairs={{0,2},{1,3},{2,0},{3,1},{4,6},{5,7},{6,4},{7,5},{8,10},{9,11},{10,... | collective-permute-start | bytes 786440 | tf_op jit(solution)/shard_map/ppermute | solution.py:64
  349.0 21.4 %collective-permute-start.16 = (bf16[256,512]{1,0:T(8,128)(2,1)S(1)}, bf16[256,512]{1,0:T(8,128)(2,1)S(1)}, u32[]{:S(2)}, u32[]{:S(2)}) collective-permute-start(bf16[256,512]{1,0:T(8,128)(2,1)S(1)} %get-tuple-element.254), channel_id=1, source_target_pairs={{0,3},{1,2},{2,1},{3,0},{4,7},{5,6},{6,5},{7,4},{8,11},{9,10},{10,... | collective-permute-start | bytes 786440 | tf_op jit(solution)/shard_map/ppermute | solution.py:64
  353.9 16.5 %collective-permute-start.17 = (bf16[16,7168]{1,0:T(8,128)(2,1)}, bf16[16,7168]{1,0:T(8,128)(2,1)S(1)}, u32[]{:S(2)}, u32[]{:S(2)}) collective-permute-start(bf16[16,7168]{1,0:T(8,128)(2,1)} %fusion.1), channel_id=1, source_target_pairs={{0,1},{1,0},{2,3},{3,2},{4,5},{5,4},{6,7},{7,6},{8,9},{9,8},{10,11... | collective-permute-start | bytes 688136 | tf_op jit(solution)/shard_map/ppermute | solution.py:64
  372.1 37.0 %collective-permute-start.19 = (bf16[256,2048]{1,0:T(8,128)(2,1)}, bf16[256,2048]{1,0:T(8,128)(2,1)S(1)}, u32[]{:S(2)}, u32[]{:S(2)}) collective-permute-start(bf16[256,2048]{1,0:T(8,128)(2,1)} %get-tuple-element.217), channel_id=1, source_target_pairs={{0,1},{1,0},{2,3},{3,2},{4,5},{5,4},{6,7},{7,6},{8,9},{9,8},{10,11... | collective-permute-start | bytes 3145736 | tf_op jit(solution)/shard_map/ppermute | solution.py:64
  375.6 33.5 %collective-permute-start.18 = (bf16[16,10752]{1,0:T(8,128)(2,1)}, bf16[16,10752]{1,0:T(8,128)(2,1)}, u32[]{:S(2)}, u32[]{:S(2)}) collective-permute-start(bf16[16,10752]{1,0:T(8,128)(2,1)} %pad_maximum_fusion.3), channel_id=1, source_target_pairs={{0,2},{1,3},{2,0},{3,1},{4,6},{5,7},{6,4},{7,5},{8,10},{9,11},{10,... | collective-permute-start | bytes 1032200 | tf_op jit(solution)/shard_map/ppermute | solution.py:64
  411.2 29.2 %collective-permute-start.20 = (bf16[256,2048]{1,0:T(8,128)(2,1)}, bf16[256,2048]{1,0:T(8,128)(2,1)}, u32[]{:S(2)}, u32[]{:S(2)}) collective-permute-start(bf16[256,2048]{1,0:T(8,128)(2,1)} %project_back.2), channel_id=1, source_target_pairs={{0,1},{1,0},{2,3},{3,2},{4,5},{5,4},{6,7},{7,6},{8,9},{9,8},{10,11... | collective-permute-start | bytes 3145736 | tf_op jit(solution)/shard_map/ppermute | solution.py:64
  421.3 19.2 %collective-permute-start.21 = (bf16[16,2048]{1,0:T(8,128)(2,1)S(1)}, bf16[16,2048]{1,0:T(8,128)(2,1)S(1)}, u32[]{:S(2)}, u32[]{:S(2)}) collective-permute-start(bf16[16,2048]{1,0:T(8,128)(2,1)S(1)} %convert_element_type.106), channel_id=1, source_target_pairs={{0,1},{1,0},{2,3},{3,2},{4,5},{5,4},{6,7},{7,6},{8,9},{9,8},{10,11... | collective-permute-start | bytes 196616 | tf_op jit(solution)/shard_map/ppermute | solution.py:64
  421.3 19.1 %collective-permute-start.22 = (bf16[16,2048]{1,0:T(8,128)(2,1)S(1)}, bf16[16,2048]{1,0:T(8,128)(2,1)S(1)}, u32[]{:S(2)}, u32[]{:S(2)}) collective-permute-start(bf16[16,2048]{1,0:T(8,128)(2,1)S(1)} %convert_element_type.106), channel_id=1, source_target_pairs={{0,2},{1,3},{2,0},{3,1},{4,6},{5,7},{6,4},{7,5},{8,10},{9,11},{10,... | collective-permute-start | bytes 196616 | tf_op jit(solution)/shard_map/ppermute | solution.py:64
  422.3 18.1 %collective-permute-start.23 = (bf16[16,2048]{1,0:T(8,128)(2,1)S(1)}, bf16[16,2048]{1,0:T(8,128)(2,1)S(1)}, u32[]{:S(2)}, u32[]{:S(2)}) collective-permute-start(bf16[16,2048]{1,0:T(8,128)(2,1)S(1)} %convert_element_type.106), channel_id=1, source_target_pairs={{0,3},{1,2},{2,1},{3,0},{4,7},{5,6},{6,5},{7,4},{8,11},{9,10},{10,... | collective-permute-start | bytes 196616 | tf_op jit(solution)/shard_map/ppermute | solution.py:64
  440.5 42.8 %collective-permute-start.24 = (bf16[256,2048]{1,0:T(8,128)(2,1)}, bf16[256,2048]{1,0:T(8,128)(2,1)S(1)}, u32[]{:S(2)}, u32[]{:S(2)}) collective-permute-start(bf16[256,2048]{1,0:T(8,128)(2,1)} %get-tuple-element.230), channel_id=1, source_target_pairs={{0,1},{1,0},{2,3},{3,2},{4,5},{5,4},{6,7},{7,6},{8,9},{9,8},{10,11... | collective-permute-start | bytes 3145736 | tf_op jit(solution)/shard_map/ppermute | solution.py:64
  442.5 45.9 %collective-permute-start.25 = (bf16[256,2048]{1,0:T(8,128)(2,1)S(1)}, bf16[256,2048]{1,0:T(8,128)(2,1)}, u32[]{:S(2)}, u32[]{:S(2)}) collective-permute-start(bf16[256,2048]{1,0:T(8,128)(2,1)S(1)} %add_convert_fusion), channel_id=1, source_target_pairs={{0,2},{1,3},{2,0},{3,1},{4,6},{5,7},{6,4},{7,5},{8,10},{9,11},{10,... | collective-permute-start | bytes 3145736 | tf_op jit(solution)/shard_map/ppermute | solution.py:64
  (50 other events, 470.3 us)
Sparse Core Ops, SparseCore 0:
  134.4 79.6 all-gather.7
  230.4 54.4 all-gather.5
  411.4 29.4 all-gather.9

commit v4 on v3

--- a/solution.py
+++ b/solution.py
@@ -163,7 +163,7 @@
     turned_ref[...] = v_ref[0].T
 
     for own in range(count):
-        i = first_ref[0] + own
+        i = first_ref[0] ^ own
         start = pl.multiple_of(i * block, block)
         here = pl.ds(own * block, block)
         query = q_ref[0, pl.ds(start, block), :] * HD ** -0.5
@@ -242,10 +242,18 @@
     )(first.reshape(1), seg, slopes, col, seg[None, :], merged, merged, merged)
 
 
-def attend_back_kernel(block, seg_ref, slope_ref, col_ref, row_ref, stat_ref, m_ref, g_ref, q_ref, k_ref, v_ref,
-                       d_ref, turned_ref, center_ref, qsum_ref, ksum_ref, vsum_ref):
+def attend_back_kernel(block, at_ref, seg_ref, slope_ref, col_ref, row_ref, *refs):
+    stats, mixed, grads_in = refs[:2], refs[2:4], refs[4:8]
+    q_ref, k_ref, v_ref, d_ref, stat_ref, m_ref, g_ref, turned_ref, center_ref, qsum_ref, ksum_ref, vsum_ref = refs[8:]
     pair = pl.program_id(0)
     count = g_ref.shape[0] // block
+    size = grads_in[0].shape[0]
+    for r, ref in enumerate(grads_in):
+        rows = pl.ds(pl.multiple_of((at_ref[0] ^ r) * size, size), size)
+        part = slice((r % 2) * size, (r % 2 + 1) * size)
+        g_ref[rows, :] = ref[...]
+        m_ref[rows, :] = mixed[r // 2][part, :]
+        stat_ref[:, :, rows] = stats[r // 2][:, :, part]
     turned_ref[...] = k_ref[0].T
     product = (g_ref[...].astype(F32) * m_ref[...].astype(F32)).T
     for half in range(2):
@@ -292,11 +300,14 @@
     d_ref[2] = vsum_ref[...].astype(BF16)
 
 
-def attend_back(merged, mixed, grad, stat, seg, slopes):
+def attend_back(at, merged, mixed, grads, stats, seg, slopes):
     parts, rows, width = merged.shape
     block = min(256, rows)
-    wide = pl.BlockSpec((rows, 2 * HD), lambda h, *_: (0, h))
+    half = rows // 2
     col = jnp.broadcast_to(seg[:, None], (rows, 128))
+
+    def wide(count):
+        return pl.BlockSpec((count, 2 * HD), lambda h, *_: (0, h))
 
     def part(i):
         return pl.BlockSpec((1, rows, 2 * HD), lambda h, *_: (i, 0, h))
@@ -305,16 +316,19 @@
         functools.partial(attend_back_kernel, block),
         out_shape=shape(merged.shape),
         grid_spec=pltpu.PrefetchScalarGridSpec(
-            num_scalar_prefetch=2,
+            num_scalar_prefetch=3,
             grid=(width // (2 * HD),),
             in_specs=[
                 pl.BlockSpec((rows, 128), lambda h, *_: (0, 0)),
                 pl.BlockSpec((1, rows), lambda h, *_: (0, 0)),
-                pl.BlockSpec((2, 1, rows), lambda h, *_: (h, 0, 0)),
-                wide, wide, part(0), part(1), part(2),
+            ] + [pl.BlockSpec((2, 1, half), lambda h, *_: (h, 0, 0))] * 2 + [wide(half)] * 2 + [wide(rows // 4)] * 4 + [
+                part(0), part(1), part(2),
             ],
             out_specs=pl.BlockSpec((parts, rows, 2 * HD), lambda h, *_: (0, 0, h)),
             scratch_shapes=[
+                pltpu.VMEM((2, 1, rows), F32),
+                pltpu.VMEM((rows, 2 * HD), BF16),
+                pltpu.VMEM((rows, 2 * HD), BF16),
                 pltpu.VMEM((2 * HD, rows), BF16),
                 pltpu.VMEM((2, rows), F32),
                 pltpu.VMEM((2 * HD, rows), F32),
@@ -323,16 +337,14 @@
             ],
         ),
         name="attend_back",
-    )(seg, slopes, col, seg[None, :], stat, mixed, grad, merged, merged, merged)
-
-
-def dense_kernel(at_ref, x0_ref, x1_ref, m0_ref, m1_ref, m2_ref, m3_ref, a_ref, bd_ref, gain_ref, bias_ref, au_ref,
+    )(at.reshape(1), seg, slopes, col, seg[None, :], *stats, *mixed, *grads, merged, merged, merged)
+
+
+def dense_kernel(x0_ref, x1_ref, m0_ref, m1_ref, m2_ref, m3_ref, a_ref, bd_ref, gain_ref, bias_ref, au_ref,
                  own_ref, far_ref, middle_ref, second_ref, zd_ref, zu_ref, w_ref, m_ref, sum_ref, loads):
     size = m0_ref.shape[1]
     count = x0_ref.shape[0]
     tiles, pieces, _, thick, tile = w_ref.shape
-    near = at_ref[0] * count
-    away = (1 - at_ref[0]) * count
 
     def columns(t):
         return pl.ds(pl.multiple_of(t * tile, tile), tile)
@@ -353,7 +365,9 @@
 
     lax.fori_loop(0, tiles, start, 0)
     for r, m in enumerate((m0_ref, m1_ref, m2_ref, m3_ref)):
-        m_ref[:, r * size:(r + 1) * size] = m[...]
+        cols = slice(r * size, (r + 1) * size)
+        m_ref[:count, cols] = m[(r % 2) * count:(r % 2 + 1) * count, :]
+        m_ref[count:, cols] = m[(1 - r % 2) * count:(2 - r % 2) * count, :]
     zd_ref[...] = dot_nt(m_ref[...], a_ref[...]).astype(BF16)
 
     def one(t, carry):
@@ -364,10 +378,8 @@
         for r in range(4):
             weights = w_ref[t, :, r].reshape(pieces * thick, tile)
             total = total + dot_nn(m_ref[:, r * size:(r + 1) * size], weights)
-        sum_ref[:, cols] = total
-        for x_ref, start in ((x0_ref, near), (x1_ref, away)):
-            rows = pl.ds(pl.multiple_of(start, count), count)
-            sum_ref[rows, cols] += x_ref[:, cols].astype(F32)
+        sum_ref[:count, cols] = total[:count] + x0_ref[:, cols].astype(F32)
+        sum_ref[count:, cols] = total[count:] + x1_ref[:, cols].astype(F32)
         return carry
 
     lax.fori_loop(0, tiles, one, 0)
@@ -384,7 +396,7 @@
     zu_ref[...] = dot_nt(second_ref[...], au_ref[...]).astype(BF16)
 
 
-def dense(low, x_own, x_far, m_parts, ad, bd, gain, bias, au, w_own, w_far):
+def dense(x_own, x_far, m_parts, ad, bd, gain, bias, au, w_own, w_far):
     count, width = x_own.shape
     rank = ad.shape[0]
     tile = min(512, width)
@@ -395,17 +407,19 @@
             shape((2 * count, width)), shape((2 * count, width)), shape((2 * count, rank)),
             shape((2 * count, rank)),
         ),
-        in_specs=[pl.BlockSpec(memory_space=pltpu.SMEM)] + [WHOLE] * 11 + [REMOTE] * 2,
+        in_specs=[WHOLE] * 11 + [REMOTE] * 2,
         out_specs=(WHOLE,) * 4,
         scratch_shapes=[
             pltpu.VMEM((width // tile, pieces, 4, thick, tile), BF16), pltpu.VMEM((2 * count, width), BF16),
             pltpu.VMEM((2 * count, width), F32), pltpu.SemaphoreType.DMA((2, width // tile)),
         ],
         name="dense",
-    )(low.reshape(1), x_own, x_far, *m_parts, ad, bd, gain, bias, au, w_own, w_far)
-
-
-def feed_kernel(earlier, at_ref, x_ref, g_ref, up_ref, down_ref, zu_ref, dz_ref, bu_ref, an_ref, au_ref, *refs):
+    )(x_own, x_far, *m_parts, ad, bd, gain, bias, au, w_own, w_far)
+
+
+def feed_kernel(earlier, at_ref, x_ref, up_ref, down_ref, zu_ref, dz_ref, bu_ref, an_ref, au_ref, *refs):
+    blocks = 1 if earlier else 2
+    g_refs, refs = refs[:blocks], refs[blocks:]
     step = pl.program_id(0)
     if earlier:
         before_ref, active_ref, hidden_ref, dz_out_ref, out_ref, total_ref, inner_ref, held_ref, sem = refs
@@ -423,7 +437,7 @@
 
     up = up_ref[...].reshape(x_ref.shape[1], hidden_ref.shape[1])
     hidden = dot_nn(x_ref[...], up) + dot_nn(zu_ref[...], bu_ref[...])
-    d_active = dot_nt(g_ref[...], down_ref[...]) + dot_nn(dz_ref[...], an_ref[...])
+    d_active = jnp.concatenate([dot_nt(g[...], down_ref[...]) for g in g_refs], 0) + dot_nn(dz_ref[...], an_ref[...])
     active, slope = gelu_pair(hidden)
     active_ref[...] = active.astype(BF16)
     d_hidden = (d_active * slope).astype(BF16)
@@ -460,10 +474,10 @@
             num_scalar_prefetch=1,
             grid=(ff // tile,),
             in_specs=[
-                rows, rows, pl.BlockSpec((up.shape[0], 4, up.shape[2], tile), lambda t, at: (0, 0, 0, t)),
+                rows, pl.BlockSpec((up.shape[0], 4, up.shape[2], tile), lambda t, at: (0, 0, 0, t)),
                 pl.BlockSpec((tile, width), lambda t, at: (t, 0)), thin, thin, row, row,
                 pl.BlockSpec((rank, width), lambda t, at: (0, 0)),
-            ] + [REMOTE] * earlier,
+            ] + [pl.BlockSpec(b.shape, lambda t, at: (0, 0), pipeline_mode=once) for b in g] + [REMOTE] * earlier,
             out_specs=(
                 cols, cols, pl.BlockSpec((count, rank), lambda t, at: (0, 0)),
                 pl.BlockSpec((count, width), lambda t, at: (0, 0), pipeline_mode=once),
@@ -473,89 +487,81 @@
             ] * earlier,
         ),
         name="feed",
-    )(at.reshape(1), x, g, up, down, zu, dz, bu, an, au, *((before,) if earlier else ()))
-
-
-def emit_kernel(earlier, at_ref, *refs):
-    parts = 2 if earlier else 1
+    )(jnp.full((1,), at, jnp.int32), x, up, down, zu, dz, bu, an, au, *g, *((before,) if earlier else ()))
+
+
+def emit_kernel(earlier, at_ref, active_ref, hidden_ref, down_ref, an_ref, bn_ref, z_in_ref, d_in_ref, *refs):
     step = pl.program_id(0)
-    total_ref, inner_ref = refs[-2:]
-    actives, hiddens, zs, ds = (refs[i * parts:(i + 1) * parts] for i in range(4))
-    down_ref, an_ref, bn_ref = refs[4 * parts:4 * parts + 3]
-    outs = refs[4 * parts + 3:-2]
     if earlier:
-        befores, outs = outs[:2], outs[2:]
-    gn_ref, gu_ref, z_ref = outs[:3]
-    count = actives[0].shape[0]
-    gn, gu = 0.0, 0.0
-    for i in range(parts):
-        rows = slice(i * count, (i + 1) * count)
-
-        @pl.when(step == 0)
-        def _():
-            total_ref[rows] = befores[i][...] if earlier else jnp.zeros((count, total_ref.shape[1]), F32)
-            inner_ref[rows] = jnp.zeros((count, inner_ref.shape[1]), F32)
-
-        active = actives[i][...]
-        total_ref[rows] += dot_nn(active, down_ref[...])
-        inner_ref[rows] += dot_nt(active, an_ref[...])
-        gn = gn + dot_tn(ds[i][...], active)
-        gu = gu + dot_tn(zs[i][...], hiddens[i][...])
-    gn_ref[...] = gn.astype(BF16)
-    gu_ref[...] = gu.astype(BF16)
+        before_ref, gn_ref, gu_ref, z_ref, out_ref, total_ref, inner_ref, held_ref, sem = refs
+        count = held_ref.shape[0]
+        copy = pltpu.make_async_copy(before_ref.at[pl.ds(at_ref[0] * count, count), :], held_ref, sem)
+    else:
+        gn_ref, gu_ref, z_ref, out_ref, total_ref, inner_ref = refs
+
+    @pl.when(step == 0)
+    def _():
+        if earlier:
+            copy.start()
+        total_ref[...] = jnp.zeros_like(total_ref)
+        inner_ref[...] = jnp.zeros_like(inner_ref)
+
+    active = active_ref[...]
+    total_ref[...] += dot_nn(active, down_ref[...])
+    inner_ref[...] += dot_nt(active, an_ref[...])
+    gn_ref[...] = dot_tn(d_in_ref[...], active).astype(BF16)
+    gu_ref[...] = dot_tn(z_in_ref[...], hidden_ref[...]).astype(BF16)
 
     @pl.when(step == pl.num_programs(0) - 1)
     def _():
         inner = inner_ref[...].astype(BF16)
         z_ref[...] = inner
-        for i in range(parts):
-            rows = slice(i * count, (i + 1) * count)
-            out = outs[3 + i]
-            out[...] = (total_ref[rows] + dot_nn(inner[rows], bn_ref[...])).astype(out.dtype)
-
-
-def emit(low, actives, hiddens, down, an, bn, zu, dz, before):
-    parts = len(actives)
-    count, ff = actives[0].shape
+        total = total_ref[...] + dot_nn(inner, bn_ref[...])
+        if earlier:
+            copy.wait()
+            total = total + held_ref[...]
+        out_ref[...] = total.astype(out_ref.dtype)
+
+
+def emit(at, active, hidden, down, an, bn, zu, dz, before, kind):
+    count, ff = active.shape
     width = down.shape[1]
     tile = min(512, ff)
     rank = an.shape[0]
     earlier = before is not None
-    once = pl.Buffered(1)
-    places = (lambda at: 1 - at[0], lambda at: at[0]) if earlier else (lambda at: 0,)
     cols = pl.BlockSpec((count, tile), lambda t, at: (0, t))
     row = pl.BlockSpec((rank, tile), lambda t, at: (0, t))
-    thin = [pl.BlockSpec((count, rank), lambda t, at, p=p: (p(at), 0)) for p in places]
-    wide = [pl.BlockSpec((count, width), lambda t, at, p=p: (p(at), 0), pipeline_mode=once) for p in places]
-    kinds = (BF16, F32) if earlier else (F32,)
+    thin = pl.BlockSpec((count, rank), lambda t, at: (at[0], 0))
     return pl.pallas_call(
         functools.partial(emit_kernel, earlier),
-        out_shape=(
-            shape((rank, ff)), shape((rank, ff)), shape((parts * count, rank)),
-        ) + tuple(shape((count, width), k) for k in kinds),
+        out_shape=(shape((rank, ff)), shape((rank, ff)), shape((count, rank)), shape((count, width), kind)),
         grid_spec=pltpu.PrefetchScalarGridSpec(
             num_scalar_prefetch=1,
             grid=(ff // tile,),
-            in_specs=[cols] * (2 * parts) + thin * 2 + [
-                pl.BlockSpec((tile, width), lambda t, at: (t, 0)), row,
-                pl.BlockSpec((rank, width), lambda t, at: (0, 0)),
-            ] + wide * earlier,
+            in_specs=[
+                cols, cols, pl.BlockSpec((tile, width), lambda t, at: (t, 0)), row,
+                pl.BlockSpec((rank, width), lambda t, at: (0, 0)), thin, thin,
+            ] + [REMOTE] * earlier,
             out_specs=(
-                row, row, pl.BlockSpec((parts * count, rank), lambda t, at: (0, 0)),
-            ) + (pl.BlockSpec((count, width), lambda t, at: (0, 0), pipeline_mode=once),) * parts,
-            scratch_shapes=[pltpu.VMEM((parts * count, width), F32), pltpu.VMEM((parts * count, rank), F32)],
+                row, row, pl.BlockSpec((count, rank), lambda t, at: (0, 0)),
+                pl.BlockSpec((count, width), lambda t, at: (0, 0), pipeline_mode=pl.Buffered(1)),
+            ),
+            scratch_shapes=[pltpu.VMEM((count, width), F32), pltpu.VMEM((count, rank), F32)] + [
+                pltpu.VMEM((count, width), F32), pltpu.SemaphoreType.DMA(()),
+            ] * earlier,
         ),
         name="emit",
-    )(low.reshape(1), *actives, *hiddens, *([zu] * parts), *([dz] * parts), down, an, bn, *([before] * parts * earlier))
-
-
-def dense_back_kernel(low_ref, own_ref, far_ref, cot_ref, gain_ref, bd_ref, ad_ref, middle_ref, w0_ref, w1_ref,
-                      low_out_ref, dz_ref, mixed_ref, mid_ref, w_ref, loads):
+    )(jnp.full((1,), at, jnp.int32), active, hidden, down, an, bn, zu, dz, *((before,) if earlier else ()))
+
+
+def dense_back_kernel(own_ref, far_ref, cot_ref, gain_ref, bd_ref, ad_ref, middle_ref, w0_ref, w1_ref,
+                      low_out_ref, dz_ref, *refs):
+    outs = refs[:4]
+    mid_ref, w_ref, loads = refs[4:]
     count, width = own_ref.shape
-    size = mixed_ref.shape[2]
+    size = outs[0].shape[1]
     pieces, _, thick, _ = w1_ref.shape
-    rows = pl.ds(pl.multiple_of(low_ref[0] * count, count), count)
-    first = pltpu.make_async_copy(middle_ref.at[rows, :], mid_ref, loads.at[4])
+    first = pltpu.make_async_copy(middle_ref.at[pl.ds(0, count), :], mid_ref, loads.at[4])
     first.start()
     pltpu.make_async_copy(w0_ref.reshape(pieces, thick, width), w_ref.at[0], loads.at[0]).start()
 
@@ -581,26 +587,32 @@
         pltpu.make_async_copy(w1_ref.at[:, 0], w_ref.at[r], loads.at[r]).wait()
         weights = w_ref[r].reshape(size, width)
         cols = pl.ds(pl.multiple_of(r * size, size), size)
-        mixed_ref[r] = (dot_nt(low_out_ref[...], weights) + dot_nn(dz_ref[...], ad_ref[:, cols])).astype(BF16)
+        value = (dot_nt(low_out_ref[...], weights) + dot_nn(dz_ref[...], ad_ref[:, cols])).astype(BF16)
+        for n, out in enumerate(outs):
+
+            @pl.when(r == n)
+            def _(out=out):
+                out[...] = value
+
         return carry
 
     lax.fori_loop(0, 4, one, 0)
 
 
-def dense_back(low, own, far, middle, cot, gain, bd, ad, w_own, w_far):
+def dense_back(own, far, middle, cot, gain, bd, ad, w_own, w_far):
     count, width = own.shape
     rank = bd.shape[0]
     return pl.pallas_call(
         dense_back_kernel,
-        out_shape=(shape((count, width)), shape((count, rank)), shape((4, count, width // 4))),
-        in_specs=[pl.BlockSpec(memory_space=pltpu.SMEM)] + [WHOLE] * 6 + [REMOTE] * 3,
-        out_specs=(WHOLE,) * 3,
+        out_shape=(shape((count, width)), shape((count, rank))) + (shape((count, width // 4)),) * 4,
+        in_specs=[WHOLE] * 6 + [REMOTE] * 3,
+        out_specs=(WHOLE,) * 6,
         scratch_shapes=[
             pltpu.VMEM((count, width), BF16), pltpu.VMEM((4, w_far.shape[0]) + w_far.shape[2:], BF16),
             pltpu.SemaphoreType.DMA((5,)),
         ],
         name="dense_back",
-    )(low.reshape(1), own, far, cot, gain, bd, ad, middle, w_own, w_far)
+    )(own, far, cot, gain, bd, ad, middle, w_own, w_far)
 
 
 def project_back_kernel(order, at_ref, aq_ref, bq_ref, d_ref, wq_ref, *refs):
@@ -829,7 +841,7 @@
     wu_second = swap(after(wu_halves[1], x_three), "mp", 2)
     held = step_in(3, x_three, held)
     merged, normed, z_qkv = held
-    other, stat_other = attend(2 * (1 - high), merged, seg, slopes, 2)
+    other, stat_other = attend(index ^ 2, merged, seg, slopes, 2)
     other, pack_one, pack_two, wu_first, wu_second, merged = lax.optimization_barrier(
         (other, pack_one, pack_two, wu_first, wu_second, merged)
     )
@@ -840,7 +852,7 @@
     slices = jnp.concatenate([wu_first, wu_second, *(p[:size] for p in packs)], 0)
     shared = lax.all_gather(slices, "dp", axis=0).reshape(copies, 7, size, width)
     ad = jnp.concatenate([ad] + [p[size:last].reshape(rank, local_width) for p in packs], 1)
-    mine, stat_mine = attend(2 * high, merged, seg, slopes, 2)
+    mine, stat_mine = attend(index, merged, seg, slopes, 2)
     m_two, mine = lax.optimization_barrier((m_two, mine))
 
     m_one = swap(mine, "mp", 1)
@@ -853,55 +865,45 @@
     cot_far = swap(after(cotangent, m_one), "mp", 1)
     wn_second = swap(after(wn_halves[1], m_one), "mp", 2)
 
-    def pair(own, far):
-        return jnp.where(low == 0, jnp.concatenate([own, far], 0), jnp.concatenate([far, own], 0))
-
     middle, second, z_dense, z_up = dense(
-        low, layer_in, x_one, m_parts, ad, bd, second_gain, second_bias, au, w_dense, shared
+        layer_in, x_one, m_parts, ad, bd, second_gain, second_bias, au, w_dense, shared
     )
     wn_second, second, cot_far = lax.optimization_barrier((wn_second, second, cot_far))
     wn_far = lax.all_gather(jnp.concatenate([wn_first, wn_second], 0), "dp", axis=0, tiled=True)
 
-    cot_pair = pair(cotangent, cot_far)
-    dz_down = dot_nt(cot_pair, bn).astype(BF16)
-    zero = jnp.zeros((), jnp.int32)
+    cots = (cotangent, cot_far)
+    dz_down = jnp.concatenate([dot_nt(c, bn).astype(BF16) for c in cots], 0)
     act, dh, dzu, so_far = feed(
-        zero, 2 * own_rows, second, cot_pair, w_up.reshape(copies, 4, size, width), w_down, z_up, dz_down, bu, an, au, None, F32
+        0, 2 * own_rows, second, cots, w_up.reshape(copies, 4, size, width), w_down, z_up, dz_down, bu, an, au, None, F32
     )
-    gn_own, gu_own, zn, out_so_far = emit(zero, (act,), (dh,), w_down, an, bn, z_up, dz_down, None)
+    gn_own, gu_own, zn, out_so_far = emit(0, act, dh, w_down, an, bn, z_up, dz_down, None, F32)
     out_so_far, so_far = lax.optimization_barrier((out_so_far, so_far))
-    far_args = (second, cot_pair, shared, wn_far, z_up, dz_down, bu_far, an_far, au, so_far)
-    act_a, dh_a, dzu_a, d_send = feed(1 - low, own_rows, *far_args, BF16)
-    low_late, d_send = lax.optimization_barrier((low, d_send))
+    far_args = (shared, wn_far, z_up, dz_down, bu_far, an_far, au, so_far)
+    act_a, dh_a, dzu_a, d_send = feed(1, own_rows, second, (cot_far,), *far_args, BF16)
+    second, d_send = lax.optimization_barrier((second, d_send))
 
     d_near = swap(d_send, "mp", 1)
-    act_b, dh_b, dzu_b, d_own = feed(low_late, own_rows, *far_args, BF16)
-    gn_far, gu_far, zn_far, out_send, out_own = emit(
-        low, (act_a, act_b), (dh_a, dh_b), wn_far, an_far, bn, z_up, dz_down, out_so_far
+    act_b, dh_b, dzu_b, d_own = feed(0, own_rows, second, (cotangent,), *far_args, BF16)
+    act_a, d_own = lax.optimization_barrier((act_a, d_own))
+    gn_a, gu_a, zn_a, out_send = emit(1, act_a, dh_a, wn_far, an_far, bn, z_up, dz_down, out_so_far, BF16)
+    d_near, d_own, out_send = lax.optimization_barrier((d_near, d_own, out_send))
+
+    d_low, dz_dense, *d_mixed = dense_back(
+        d_own, d_near, middle, cotangent, second_gain, bd, ad, w_dense, shared
     )
-
-    def halves(own, far, axis):
-        return jnp.where(high == 0, jnp.concatenate([own, far], axis), jnp.concatenate([far, own], axis))
-
-    def own(value):
-        return lax.dynamic_slice_in_dim(value, low * own_rows, own_rows, 0)
-
-    def join(value, first, second):
-        return (value.astype(F32) + pair(second, first).astype(F32)).astype(BF16)
-
-    mixed = halves(mine, other, 0)
-    stat = halves(stat_mine, stat_other, 2)
-    d_near, out_send, mixed, stat = lax.optimization_barrier((d_near, out_send, mixed, stat))
-
-    d_low, dz_dense, d_mixed = dense_back(
-        low, d_own, d_near, middle, cotangent, second_gain, bd, ad, w_dense, shared
-    )
-    d_mixed, d_low, dz_dense = lax.optimization_barrier((d_mixed, d_low, dz_dense))
+    d_low, dz_dense, act_b, *d_mixed = lax.optimization_barrier((d_low, dz_dense, act_b, *d_mixed))
     g_blocks = [d_mixed[0]] + [swap(d_mixed[r], "mp", r) for r in (1, 2, 3)]
-    ga_up = dot_tn(join(dzu, dzu_a, dzu_b), second)
-    gb_down = dot_tn(join(zn, zn_far[:own_rows], zn_far[own_rows:]), cot_pair)
-    gb_dense = dot_tn(own(z_dense), d_low)
-    gd = [dot_tn(dz_dense, own(m)) for m in m_parts]
+    gn_b, gu_b, zn_b, out_own = emit(0, act_b, dh_b, wn_far, an_far, bn, z_up, dz_down, out_so_far, F32)
+
+    def join(value, own, far):
+        return (value.astype(F32) + jnp.concatenate([own, far], 0).astype(F32)).astype(BF16)
+
+    ga_up = dot_tn(join(dzu, dzu_b, dzu_a), second)
+    zn = join(zn, zn_b, zn_a)
+    gb_down = dot_tn(zn[:own_rows], cotangent) + dot_tn(zn[own_rows:], cot_far)
+    gb_dense = dot_tn(z_dense[:own_rows], d_low)
+    gd = [dot_tn(dz_dense, m[(r % 2) * own_rows:(r % 2 + 1) * own_rows]) for r, m in enumerate(m_parts)]
+    gu_far, gn_far = ((a.astype(F32) + b.astype(F32)).astype(BF16) for a, b in ((gu_a, gu_b), (gn_a, gn_b)))
     sums = jnp.concatenate([ga_up, gb_down, gb_dense], 1)
     near = swap(jnp.concatenate([sums, gd[1], gd[3]], 1).astype(BF16), "mp", 1)
     *g_blocks, near = lax.optimization_barrier((*g_blocks, near))
@@ -912,10 +914,7 @@
     gd_far = gd[2] + near[:, 3 * width + local_width:]
     mate = swap(jnp.concatenate([sums.astype(BF16), gu_far, gn_far, gd_far.astype(BF16)], 1), "mp", 2)
     out_near = swap(after(out_send, near), "mp", 1)
-    grad = jnp.zeros((total_rows, local_width), BF16)
-    for r, block in enumerate(g_blocks):
-        grad = lax.dynamic_update_slice_in_dim(grad, block, (index ^ r) * own_rows, 0)
-    d_merged = attend_back(merged, mixed, grad, stat, seg, slopes)
+    d_merged = attend_back(index, merged, (mine, other), g_blocks, (stat_mine, stat_other), seg, slopes)
     (send,) = project_back(index, d_merged, wq, aq, bq, (3,))
     send, d_merged, mate, out_near = lax.optimization_barrier((send, d_merged, mate, out_near))
 
@@ -926,18 +925,17 @@
     ga_qkv, gb_qkv = inner_grads(d_merged, z_qkv, normed, bq)
     ga_low, d_merged = lax.optimization_barrier((ga_qkv.astype(BF16), d_merged))
     ga_others = [swap(ga_low, "mp", r) for r in (1, 2, 3)]
-    send_two, send_one, kept = project_back(index, d_merged, wq, aq, bq, (2, 1, 0))
-    relay, send_one, send_two, kept, *ga_others = lax.optimization_barrier(
-        (relay, send_one, send_two, kept, *ga_others)
-    )
+    send_two, send_one = project_back(index, d_merged, wq, aq, bq, (2, 1))
+    relay, send_one, send_two, *ga_others = lax.optimization_barrier((relay, send_one, send_two, *ga_others))
 
     d_two = swap((send_two.astype(F32) + relay.astype(F32)).astype(BF16), "mp", 2)
     d_one = swap(send_one, "mp", 1)
-    layer_out = (own(middle).astype(F32) + out_own + out_near.astype(F32)).astype(BF16)
+    layer_out = (middle[:own_rows].astype(F32) + out_own + out_near.astype(F32)).astype(BF16)
     ga_qkv = ga_qkv + sum(g.astype(F32) for g in ga_others)
     second_pack = jnp.concatenate([ga_qkv, gb_qkv], 1).astype(BF16)
     second_pack = lax.all_gather(second_pack, "dp", axis=0)
     ids = first_pack[:, 0, -1].astype(jnp.int32)
+    (kept,) = project_back(after(index, ids), d_merged, wq, aq, bq, (0,))
     ga_up, gb_down, gb_dense, gb_up, ga_down, ga_dense, ga_qkv, gb_qkv = spread(
         ids, first_pack, second_pack, kinds, width, local_width, local_ff
     )

time: 509 us -> 496 us (0.974)
  the two profiles are of different devices: /device:TPU:2 before, /device:TPU:4 now
where the time goes in v4:
time: 496 us; the launch traced here: 487 us
  Pallas kernels  224 us (45%)
  waiting for transfers between devices  144 us (29%)
  starting transfers between devices  32.7 us (7%)
  local copies, waits for them, and re-layouts  30.4 us (6%)
  blocking collectives  20.3 us (4%)
  between operations  15.4 us (3%)
  other arithmetic  14.5 us (3%)
  matrix products  6.97 us (1%)
    ppermute x26, waiting for transfers between devices, swap(): return lax.ppermute(value, axis, pairs)  114 us
    pallas_call x3, Pallas kernels, feed(): pl.pallas_call(functools.partial(feed_kernel, earlier), out_shape=(shape(...  51 us
    ppermute x26, starting transfers between devices, swap(): return lax.ppermute(value, axis, pairs)  32.4 us
    pallas_call x2, Pallas kernels, attend(): pl.pallas_call(functools.partial(attend_kernel, block, count), out_shape=...  29.5 us
    pallas_call x3, Pallas kernels, emit(): pl.pallas_call(functools.partial(emit_kernel, earlier), out_shape=(shape(...  28.6 us
    pallas_call x1, Pallas kernels, attend_back(): pl.pallas_call(functools.partial(attend_back_kernel, block), out_shape=sh...  24.3 us
    pallas_call x4, Pallas kernels, project(): pl.pallas_call(functools.partial(project_kernel, kept), out_shape=(shape(...  24.3 us
    pallas_call x3, Pallas kernels, project_back(): pl.pallas_call(functools.partial(project_back_kernel, order), out_shape=(...  21.7 us
  transfers between devices with their start and end apart: 29, of which 11 were waited for; matrix products, arithmetic and copies ran while one was open for 9% of the time, Pallas kernels for 40%

profile of v4, /device:TPU:4, one launch (start us, length us, event | category | flops | bytes accessed | tf_op | source)
XLA Modules:
  0.0 487.4 jit_solution(18148320639912807443)
XLA Ops:
  17.5 6.1 %project.4 = (bf16[3,1024,512]{2,1,0:T(8,128)(2,1)}, bf16[1024,2048]{1,0:T(8,128)(2,1)}, bf16[1024,16]{1,0:T(8,128)(2,1)}) custom-call(s32[1]{0:T(128)} %bitcast.at_ref.first_ref, bf16[256,2048]{1,0:T(8,128)(2,1)} %x_ref.3, bf16[1,2048]{1,0:T(2,128)(2,1)} %broadcast_in_dim.10.gain_ref, bf16[1,2048]{1,0:T(2,128)(2,1)} %broadcast_in_dim.11.bias_ref, ...), custom_call_target="tpu_custom_call" | custom-call | tf_op jit(solution)/shard_map/project/pallas_call | solution.py:122
  25.4 29.3 %collective-permute-done.x_ref.x1_ref = bf16[256,2048]{1,0:T(8,128)(2,1)S(1)} collective-permute-done((bf16[256,2048]{1,0:T(8,128)(2,1)}, bf16[256,2048]{1,0:T(8,128)(2,1)S(1)}, u32[]{:S(2)}, u32[]{:S(2)}) %collective-permute-start) | collective-permute-done | bytes 1048608 | tf_op jit(solution)/shard_map/ppermute | solution.py:64
  64.6 6.1 %project.5 = (bf16[3,1024,512]{2,1,0:T(8,128)(2,1)}, bf16[1024,2048]{1,0:T(8,128)(2,1)}, bf16[1024,16]{1,0:T(8,128)(2,1)}) custom-call(s32[1]{0:T(128)} %bitcast.16.at_ref, bf16[256,2048]{1,0:T(8,128)(2,1)} %copy-done.8, bf16[1,2048]{1,0:T(2,128)(2,1)} %broadcast_in_dim.10.gain_ref, ...), custom_call_target="tpu_custom_call", output_to_operand_aliasing={{0}: (7, {}), {1}: (8, {}), {2}: (9, {})} | custom-call | tf_op jit(solution)/shard_map/project/pallas_call | solution.py:122
  70.6 6.1 %project.6 = (bf16[3,1024,512]{2,1,0:T(8,128)(2,1)}, bf16[1024,2048]{1,0:T(8,128)(2,1)}, bf16[1024,16]{1,0:T(8,128)(2,1)}) custom-call(s32[1]{0:T(128)} %bitcast.7.at_ref.first_ref, bf16[256,2048]{1,0:T(8,128)(2,1)} %collective-permute-done.1.x_ref, ...), custom_call_target="tpu_custom_call", output_to_operand_aliasing={{0}: (7, {}), {1}: (8, {}), {2}: (9, {})} | custom-call | tf_op jit(solution)/shard_map/project/pallas_call | solution.py:122
  76.7 28.2 %collective-permute-done.3 = bf16[100,2048]{1,0:T(8,128)(2,1)S(1)} collective-permute-done((bf16[100,2048]{1,0:T(8,128)(2,1)}, bf16[100,2048]{1,0:T(8,128)(2,1)S(1)}, u32[]{:S(2)}, u32[]{:S(2)}) %collective-permute-start.3) | collective-permute-done | bytes 409632 | tf_op jit(solution)/shard_map/ppermute | solution.py:64
  106.6 6.1 %project.7 = (bf16[3,1024,512]{2,1,0:T(8,128)(2,1)}, bf16[1024,2048]{1,0:T(8,128)(2,1)}, bf16[1024,16]{1,0:T(8,128)(2,1)}) custom-call(s32[1]{0:T(128)} %bitcast.9.at_ref, bf16[256,2048]{1,0:T(8,128)(2,1)} %collective-permute-done.2.x_ref, bf16[1,2048]{1,0:T(2,128)(2,1)} %broadcast_in_dim.10.gain_ref, ...), custom_call_target="tpu_custom_call", output_to_operand_aliasing={{0}: (7, {}), {1}: (8, {}), {2}: (9, {})} | custom-call | tf_op jit(solution)/shard_map/project/pallas_call | solution.py:122
  113.8 17.7 %attend.2 = (bf16[512,512]{1,0:T(8,128)(2,1)}, f32[8,1,512]{2,1,0:T(1,128)}) custom-call(s32[1]{0:T(128)} %bitcast.7.at_ref.first_ref, s32[1024]{0:T(1024)} %bitcast.79, f32[8]{0:T(128)} %multiply_exponential_fusion.slope_ref, s32[1024,128]{1,0:T(8,128)} %broadcast_in_dim.12.col_ref, s32[1,1024]{1,0:T(1,128)} %row_ref.5, ...), custom_call_target="tpu_custom_call" | custom-call | tf_op jit(solution)/shard_map/attend/pallas_call | solution.py:219
  135.8 11.8 %attend.3 = (bf16[512,512]{1,0:T(8,128)(2,1)}, f32[8,1,512]{2,1,0:T(1,128)}) custom-call(s32[1]{0:T(128)} %bitcast.at_ref.first_ref, s32[1024]{0:T(1024)} %bitcast.80, f32[8]{0:T(128)} %multiply_exponential_fusion.slope_ref, s32[1024,128]{1,0:T(8,128)} %broadcast_in_dim.12.col_ref, s32[1,1024]{1,0:T(1,128)} %row_ref.5, ...), custom_call_target="tpu_custom_call" | custom-call | tf_op jit(solution)/shard_map/attend/pallas_call | solution.py:219
  147.7 8.0 %collective-permute-done.7.m2_ref = bf16[512,512]{1,0:T(8,128)(2,1)S(1)} collective-permute-done((bf16[512,512]{1,0:T(8,128)(2,1)}, bf16[512,512]{1,0:T(8,128)(2,1)S(1)}, u32[]{:S(2)}, u32[]{:S(2)}) %collective-permute-start.7) | collective-permute-done | bytes 524320 | tf_op jit(solution)/shard_map/ppermute | solution.py:64
  160.6 30.3 %collective-permute-done.8.m1_ref = bf16[512,512]{1,0:T(8,128)(2,1)S(1)} collective-permute-done((bf16[512,512]{1,0:T(8,128)(2,1)S(1)}, bf16[512,512]{1,0:T(8,128)(2,1)S(1)}, u32[]{:S(2)}, u32[]{:S(2)}) %collective-permute-start.8) | collective-permute-done | bytes 524320 | tf_op jit(solution)/shard_map/ppermute | solution.py:64
  199.9 13.4 %all-gather.8.cloned.1.call-done = bf16[3584,2048]{1,0:T(8,128)(2,1)} async-done(((bf16[448,2048]{1,0:T(8,128)(2,1)}), bf16[3584,2048]{1,0:T(8,128)(2,1)}) %all-gather.8.cloned.1.call-update) | async-done | bytes 14680080 | tf_op jit(solution)/shard_map/all_gather | solution.py:853
  213.3 13.6 %dense.1 = (bf16[512,2048]{1,0:T(8,128)(2,1)}, bf16[512,2048]{1,0:T(8,128)(2,1)}, bf16[512,16]{1,0:T(8,128)(2,1)}, bf16[512,16]{1,0:T(8,128)(2,1)}) custom-call(bf16[256,2048]{1,0:T(8,128)(2,1)} %x_ref.3, bf16[256,2048]{1,0:T(8,128)(2,1)} %copy-done.8, bf16[512,512]{1,0:T(8,128)(2,1)} %get-tuple-element.168.m0_ref.refs_2_, bf16[512,512]{1,0:T(8,128)(2,1)} %copy-done.17, ...), custom_call_target="tpu_custom_call" | custom-call | tf_op jit(solution)/shard_map/dense/pallas_call | solution.py:404
  233.6 23.7 %feed.3 = (bf16[512,2048]{1,0:T(8,128)(2,1)}, bf16[512,2048]{1,0:T(8,128)(2,1)}, bf16[512,16]{1,0:T(8,128)(2,1)}, f32[512,2048]{1,0:T(8,128)}) custom-call(s32[1]{0:T(128)} %constant.60.clone.1.at_ref, bf16[512,2048]{1,0:T(8,128)(2,1)} %get-tuple-element.194.x_ref, bf16[8,4,64,2048]{3,2,1,0:T(8,128)(2,1)} %bitcast.76, bf16[2048,2048]{1,0:T(8,128)(2,1)} %down_ref.3, ...), custom_call_target="tpu_custom_call" | custom-call | tf_op jit(solution)/shard_map/feed/pallas_call | solution.py:470
  257.3 11.8 %emit.3 = (bf16[16,2048]{1,0:T(8,128)(2,1)}, bf16[16,2048]{1,0:T(8,128)(2,1)}, bf16[512,16]{1,0:T(8,128)(2,1)}, f32[512,2048]{1,0:T(8,128)}) custom-call(s32[1]{0:T(128)} %constant.60.clone.1.at_ref, bf16[512,2048]{1,0:T(8,128)(2,1)} %get-tuple-element.186.active_ref, bf16[512,2048]{1,0:T(8,128)(2,1)} %get-tuple-element.187.hidden_ref, ...), custom_call_target="tpu_custom_call" | custom-call | tf_op jit(solution)/shard_map/emit/pallas_call | solution.py:535
  269.0 16.2 %all-gather.6.cloned.1.call-done.down_ref = bf16[2048,2048]{1,0:T(8,128)(2,1)} async-done(((bf16[256,2048]{1,0:T(8,128)(2,1)}), bf16[2048,2048]{1,0:T(8,128)(2,1)}) %all-gather.6.cloned.1.call-update) | async-done | bytes 8388624 | tf_op jit(solution)/shard_map/all_gather | solution.py:872
  285.3 13.6 %feed.4 = (bf16[256,2048]{1,0:T(8,128)(2,1)}, bf16[256,2048]{1,0:T(8,128)(2,1)}, bf16[256,16]{1,0:T(8,128)(2,1)}, bf16[256,2048]{1,0:T(8,128)(2,1)}) custom-call(s32[1]{0:T(128)} %constant.61.clone.1.at_ref, bf16[512,2048]{1,0:T(8,128)(2,1)} %get-tuple-element.194.x_ref, bf16[8,7,64,2048]{3,2,1,0:T(8,128)(2,1)} %bitcast.73, ...), custom_call_target="tpu_custom_call" | custom-call | tf_op jit(solution)/shard_map/feed/pallas_call | solution.py:470
  300.5 13.7 %feed.5 = (bf16[256,2048]{1,0:T(8,128)(2,1)}, bf16[256,2048]{1,0:T(8,128)(2,1)}, bf16[256,16]{1,0:T(8,128)(2,1)}, bf16[256,2048]{1,0:T(8,128)(2,1)}) custom-call(s32[1]{0:T(128)} %constant.60.clone.1.at_ref, bf16[512,2048]{1,0:T(8,128)(2,1)} %get-tuple-element.194.x_ref, bf16[8,7,64,2048]{3,2,1,0:T(8,128)(2,1)} %bitcast.74, ...), custom_call_target="tpu_custom_call" | custom-call | tf_op jit(solution)/shard_map/feed/pallas_call | solution.py:470
  315.3 8.4 %emit.4 = (bf16[16,2048]{1,0:T(8,128)(2,1)}, bf16[16,2048]{1,0:T(8,128)(2,1)}, bf16[256,16]{1,0:T(8,128)(2,1)}, bf16[256,2048]{1,0:T(8,128)(2,1)}) custom-call(s32[1]{0:T(128)} %constant.61.clone.1.at_ref, bf16[256,2048]{1,0:T(8,128)(2,1)} %get-tuple-element.197.active_ref, bf16[256,2048]{1,0:T(8,128)(2,1)} %get-tuple-element.198.hidden_ref, ...), custom_call_target="tpu_custom_call" | custom-call | tf_op jit(solution)/shard_map/emit/pallas_call | solution.py:535
  325.7 9.8 %dense_back.1 = (bf16[256,2048]{1,0:T(8,128)(2,1)}, bf16[256,16]{1,0:T(8,128)(2,1)}, bf16[256,512]{1,0:T(8,128)(2,1)}, bf16[256,512]{1,0:T(8,128)(2,1)}, bf16[25...) custom-call(bf16[256,2048]{1,0:T(8,128)(2,1)} %get-tuple-element.201.own_ref, ...), custom_call_target="tpu_custom_call" | custom-call | tf_op jit(solution)/shard_map/dense_back/pallas_call | solution.py:605
  339.9 8.5 %emit.5 = (bf16[16,2048]{1,0:T(8,128)(2,1)}, bf16[16,2048]{1,0:T(8,128)(2,1)}, bf16[256,16]{1,0:T(8,128)(2,1)}, f32[256,2048]{1,0:T(8,128)}) custom-call(s32[1]{0:T(128)} %constant.60.clone.1.at_ref, bf16[256,2048]{1,0:T(8,128)(2,1)} %get-tuple-element.210.active_ref, bf16[256,2048]{1,0:T(8,128)(2,1)} %get-tuple-element.211.hidden_ref, ...), custom_call_target="tpu_custom_call" | custom-call | tf_op jit(solution)/shard_map/emit/pallas_call | solution.py:535
  354.7 7.6 %collective-permute-done.17 = bf16[16,7168]{1,0:T(8,128)(2,1)S(1)} collective-permute-done((bf16[16,7168]{1,0:T(8,128)(2,1)}, bf16[16,7168]{1,0:T(8,128)(2,1)S(1)}, u32[]{:S(2)}, u32[]{:S(2)}) %collective-permute-start.17) | collective-permute-done | bytes 229408 | tf_op jit(solution)/shard_map/ppermute | solution.py:64
  367.6 24.3 %attend_back.1.d_ref = bf16[3,1024,512]{2,1,0:T(8,128)(2,1)} custom-call(s32[1]{0:T(128)} %bitcast.at_ref.first_ref, s32[1024]{0:T(1024)} %bitcast.81, f32[8]{0:T(128)} %multiply_exponential_fusion.slope_ref, s32[1024,128]{1,0:T(8,128)} %broadcast_in_dim.12.col_ref, s32[1,1024]{1,0:T(1,128)} %row_ref.5, f32[8,1,512]{2,1,0:T(1,128)} %get-tuple-element.213.refs_0_, ...), custom_call_target="tpu_custom_call" | custom-call | tf_op jit(solution)/shard_map/attend_back/pallas_call | solution.py:315
  391.9 6.3 %project_back.3 = bf16[256,2048]{1,0:T(8,128)(2,1)} custom-call(s32[1]{0:T(128)} %bitcast.at_ref.first_ref, bf16[16,2048]{1,0:T(8,128)(2,1)} %dynamic-slice_bitcast_fusion.5.aq_ref, bf16[3,16,512]{2,1,0:T(8,128)(2,1)} %dynamic-slice_bitcast_fusion.6.bq_ref, bf16[3,1024,512]{2,1,0:T(8,128)(2,1)} %attend_back.1.d_ref, bf16[3,2048,512]{2,1,0:T(8,128)(2,1)} %bitcast.69), custom_call_target="tpu_custom_call" | custom-call | tf_op jit(solution)/shard_map/project_back/pallas_call | solution.py:666
  400.5 6.7 %inner_grads.1 = (f32[16,2048]{1,0:T(8,128)}, f32[16,1536]{1,0:T(8,128)}) custom-call(bf16[3,1024,512]{2,1,0:T(8,128)(2,1)} %attend_back.1.d_ref, bf16[1024,16]{1,0:T(8,128)(2,1)} %get-tuple-element.245.z_ref, bf16[1024,2048]{1,0:T(8,128)(2,1)} %get-tuple-element.246.n_ref, bf16[3,16,512]{2,1,0:T(8,128)(2,1)} %dynamic-slice_bitcast_fusion.6.bq_ref), custom_call_target="tpu_custom_call" | custom-call | tf_op jit(solution)/shard_map/inner_grads/pallas_call | solution.py:700
  412.5 3.4 add_convert_fusion.1
  415.9 9.1 %project_back.5 = (bf16[256,2048]{1,0:T(8,128)(2,1)}, bf16[256,2048]{1,0:T(8,128)(2,1)}) custom-call(s32[1]{0:T(128)} %bitcast.at_ref.first_ref, bf16[16,2048]{1,0:T(8,128)(2,1)} %dynamic-slice_bitcast_fusion.5.aq_ref, bf16[3,16,512]{2,1,0:T(8,128)(2,1)} %dynamic-slice_bitcast_fusion.6.bq_ref, bf16[3,1024,512]{2,1,0:T(8,128)(2,1)} %attend_back.1.d_ref, ...), custom_call_target="tpu_custom_call" | custom-call | tf_op jit(solution)/shard_map/project_back/pallas_call | solution.py:666
  429.4 3.4 collective-permute-start.25
  432.9 20.3 %all_gather.24.second_ref = bf16[8,16,3584]{2,1,0:T(8,128)(2,1)} all-gather(bf16[1,16,3584]{2,1,0:T(8,128)(2,1)S(1)} %pad_maximum_fusion.4), channel_id=1, replica_groups=mesh['dp'=8,'mp'=4] {'dp'}, dimensions={0}, use_global_device_ids=true | all-gather | bytes 1032192 | tf_op jit(solution)/shard_map/all_gather | solution.py:936
  454.7 6.3 %project_back.4.kept_ref = bf16[256,2048]{1,0:T(8,128)(2,1)} custom-call(s32[1]{0:T(128)} %bitcast.28.at_ref, bf16[16,2048]{1,0:T(8,128)(2,1)} %dynamic-slice_bitcast_fusion.5.aq_ref, bf16[3,16,512]{2,1,0:T(8,128)(2,1)} %dynamic-slice_bitcast_fusion.6.bq_ref, bf16[3,1024,512]{2,1,0:T(8,128)(2,1)} %attend_back.1.d_ref, bf16[3,2048,512]{2,1,0:T(8,128)(2,1)} %bitcast.71), custom_call_target="tpu_custom_call" | custom-call | tf_op jit(solution)/shard_map/project_back/pallas_call | solution.py:666
  461.0 8.9 %spread.1 = (f32[8,16,2048]{2,1,0:T(8,128)}, f32[8,16,2048]{2,1,0:T(8,128)}, f32[8,16,2048]{2,1,0:T(8,128)}, f32[8,16,2048]{2,1,0:T(8,128)}, f32[8,16,2048]{2,1,...) custom-call(s32[8]{0:T(128)} %fusion.16.ids_ref, ...), custom_call_target="tpu_custom_call" | custom-call | tf_op jit(solution)/shard_map/spread/pallas_call | solution.py:744
  470.4 5.0 %collective-permute-done.25.two_ref = bf16[256,2048]{1,0:T(8,128)(2,1)} collective-permute-done((bf16[256,2048]{1,0:T(8,128)(2,1)S(1)}, bf16[256,2048]{1,0:T(8,128)(2,1)}, u32[]{:S(2)}, u32[]{:S(2)}) %collective-permute-start.25) | collective-permute-done | bytes 1048608 | tf_op jit(solution)/shard_map/ppermute | solution.py:64
  475.5 5.2 %last_norm.1 = bf16[256,2048]{1,0:T(8,128)(2,1)} custom-call(bf16[256,2048]{1,0:T(8,128)(2,1)} %project_back.4.kept_ref, bf16[256,2048]{1,0:T(8,128)(2,1)} %copy-done.23, bf16[256,2048]{1,0:T(8,128)(2,1)} %collective-permute-done.25.two_ref, bf16[256,2048]{1,0:T(8,128)(2,1)} %x_ref.3, bf16[256,2048]{1,0:T(8,128)(2,1)} %get-tuple-element.226.d_ref, ...), custom_call_target="tpu_custom_call" | custom-call | tf_op jit(solution)/shard_map/last_norm/pallas_call | solution.py:772
  (213 shorter events, 83.3 us)
Async XLA Ops:
  7.2 206.1 %all-gather.8.cloned.1.call-start = ((), (), s32[]{:S(2)}) async-start(), calls=%async_computation.1 | async-start | bytes 16515072 | tf_op jit(solution)/shard_map/all_gather | solution.py:853
  7.2 47.5 %collective-permute-start = (bf16[256,2048]{1,0:T(8,128)(2,1)}, bf16[256,2048]{1,0:T(8,128)(2,1)S(1)}, u32[]{:S(2)}, u32[]{:S(2)}) collective-permute-start(bf16[256,2048]{1,0:T(8,128)(2,1)} %x_ref.3), channel_id=1, source_target_pairs={{0,1},{1,0},{2,3},{3,2},{4,5},{5,4},{6,7},{7,6},{8,9},{9,8},{10,11... | collective-permute-start | bytes 3145736 | tf_op jit(solution)/shard_map/ppermute | solution.py:64
  8.9 48.4 %collective-permute-start.1 = (bf16[256,2048]{1,0:T(8,128)(2,1)}, bf16[256,2048]{1,0:T(8,128)(2,1)}, u32[]{:S(2)}, u32[]{:S(2)}) collective-permute-start(bf16[256,2048]{1,0:T(8,128)(2,1)} %x_ref.3), channel_id=1, source_target_pairs={{0,2},{1,3},{2,0},{3,1},{4,6},{5,7},{6,4},{7,5},{8,10},{9,11},{10,... | collective-permute-start | bytes 3145736 | tf_op jit(solution)/shard_map/ppermute | solution.py:64
  24.4 46.2 %copy-start.21 = (bf16[16,2048]{1,0:T(8,128)(2,1)}, bf16[16,2048]{1,0:T(8,128)(2,1)S(1)}, u32[]{:S(2)}) copy-start(bf16[16,2048]{1,0:T(8,128)(2,1)S(1)} %dynamic-slice_bitcast_fusion.3.an_ref) | copy-start | bytes 196612
  57.3 47.7 %collective-permute-start.2 = (bf16[256,2048]{1,0:T(8,128)(2,1)}, bf16[256,2048]{1,0:T(8,128)(2,1)}, u32[]{:S(2)}, u32[]{:S(2)}) collective-permute-start(bf16[256,2048]{1,0:T(8,128)(2,1)} %collective-permute-done.1.x_ref), channel_id=1, source_target_pairs={{0,1},{1,0},{2,3},{3,2},{4,5},{5,4},{6,7},{7,6},{8,9},{9,8},{10,11... | collective-permute-start | bytes 3145736 | tf_op jit(solution)/shard_map/ppermute | solution.py:64
  60.8 44.1 %collective-permute-start.4 = (bf16[128,2048]{1,0:T(8,128)(2,1)}, bf16[128,2048]{1,0:T(8,128)(2,1)S(1)}, u32[]{:S(2)}, u32[]{:S(2)}) collective-permute-start(bf16[128,2048]{1,0:T(8,128)(2,1)} %get-tuple-element.146), channel_id=1, source_target_pairs={{0,2},{1,3},{2,0},{3,1},{4,6},{5,7},{6,4},{7,5},{8,10},{9,11},{10,... | collective-permute-start | bytes 1572872 | tf_op jit(solution)/shard_map/ppermute | solution.py:64
  64.3 40.6 %collective-permute-start.3 = (bf16[100,2048]{1,0:T(8,128)(2,1)}, bf16[100,2048]{1,0:T(8,128)(2,1)S(1)}, u32[]{:S(2)}, u32[]{:S(2)}) collective-permute-start(bf16[100,2048]{1,0:T(8,128)(2,1)} %pad_maximum_fusion.2), channel_id=1, source_target_pairs={{0,2},{1,3},{2,0},{3,1},{4,6},{5,7},{6,4},{7,5},{8,10},{9,11},{10,... | collective-permute-start | bytes 1228808 | tf_op jit(solution)/shard_map/ppermute | solution.py:64
  105.0 26.4 %collective-permute-start.5 = (bf16[136,2048]{1,0:T(8,128)(2,1)S(1)}, bf16[136,2048]{1,0:T(8,128)(2,1)S(1)}, u32[]{:S(2)}, u32[]{:S(2)}) collective-permute-start(bf16[136,2048]{1,0:T(8,128)(2,1)S(1)} %pad_maximum_fusion.1), channel_id=1, source_target_pairs={{0,1},{1,0},{2,3},{3,2},{4,5},{5,4},{6,7},{7,6},{8,9},{9,8},{10,11... | collective-permute-start | bytes 1671176 | tf_op jit(solution)/shard_map/ppermute | solution.py:64
  105.1 26.3 %collective-permute-start.6 = (bf16[128,2048]{1,0:T(8,128)(2,1)}, bf16[128,2048]{1,0:T(8,128)(2,1)}, u32[]{:S(2)}, u32[]{:S(2)}) collective-permute-start(bf16[128,2048]{1,0:T(8,128)(2,1)} %get-tuple-element.164), channel_id=1, source_target_pairs={{0,2},{1,3},{2,0},{3,1},{4,6},{5,7},{6,4},{7,5},{8,10},{9,11},{10,... | collective-permute-start | bytes 1572872 | tf_op jit(solution)/shard_map/ppermute | solution.py:64
  134.2 151.1 %all-gather.6.cloned.1.call-start = ((), (), s32[]{:S(2)}) async-start(), calls=%async_computation | async-start | bytes 9437184 | tf_op jit(solution)/shard_map/all_gather | solution.py:872
  134.5 21.3 %collective-permute-start.7 = (bf16[512,512]{1,0:T(8,128)(2,1)}, bf16[512,512]{1,0:T(8,128)(2,1)S(1)}, u32[]{:S(2)}, u32[]{:S(2)}) collective-permute-start(bf16[512,512]{1,0:T(8,128)(2,1)} %get-tuple-element.165.refs_3_), channel_id=1, source_target_pairs={{0,2},{1,3},{2,0},{3,1},{4,6},{5,7},{6,4},{7,5},{8,10},{9,11},{10,... | collective-permute-start | bytes 1572872 | tf_op jit(solution)/shard_map/ppermute | solution.py:64
  147.7 51.5 %slice-start = ((bf16[100,2048]{1,0:T(8,128)(2,1)}), bf16[4,2048]{1,0:T(4,128)(2,1)S(1)}, s32[]{:S(2)}) async-start(bf16[100,2048]{1,0:T(8,128)(2,1)} %copy-done.19), calls=%async_computation.3 | async-start | bytes 32768 | tf_op jit(solution)/shard_map/slice | solution.py:854
  155.7 57.6 %copy-start.13 = (bf16[512,512]{1,0:T(8,128)(2,1)}, bf16[512,512]{1,0:T(8,128)(2,1)S(1)}, u32[]{:S(2)}) copy-start(bf16[512,512]{1,0:T(8,128)(2,1)S(1)} %collective-permute-done.7.m2_ref) | copy-start | bytes 1572868
  155.7 35.2 %collective-permute-start.9 = (bf16[512,512]{1,0:T(8,128)(2,1)S(1)}, bf16[512,512]{1,0:T(8,128)(2,1)S(1)}, u32[]{:S(2)}, u32[]{:S(2)}) collective-permute-start(bf16[512,512]{1,0:T(8,128)(2,1)S(1)} %collective-permute-done.7.m2_ref), channel_id=1, source_target_pairs={{0,1},{1,0},{2,3},{3,2},{4,5},{5,4},{6,7},{7,6},{8,9},{9,8},{10,11... | collective-permute-start | bytes 1572872 | tf_op jit(solution)/shard_map/ppermute | solution.py:64
  156.7 34.2 %collective-permute-start.8 = (bf16[512,512]{1,0:T(8,128)(2,1)S(1)}, bf16[512,512]{1,0:T(8,128)(2,1)S(1)}, u32[]{:S(2)}, u32[]{:S(2)}) collective-permute-start(bf16[512,512]{1,0:T(8,128)(2,1)S(1)} %copy-done.9), channel_id=1, source_target_pairs={{0,1},{1,0},{2,3},{3,2},{4,5},{5,4},{6,7},{7,6},{8,9},{9,8},{10,11... | collective-permute-start | bytes 1572872 | tf_op jit(solution)/shard_map/ppermute | solution.py:64
  158.6 33.9 %collective-permute-start.10 = (bf16[128,2048]{1,0:T(8,128)(2,1)S(1)}, bf16[128,2048]{1,0:T(8,128)(2,1)}, u32[]{:S(2)}, u32[]{:S(2)}) collective-permute-start(bf16[128,2048]{1,0:T(8,128)(2,1)S(1)} %get-tuple-element.274), channel_id=1, source_target_pairs={{0,2},{1,3},{2,0},{3,1},{4,6},{5,7},{6,4},{7,5},{8,10},{9,11},{10,... | collective-permute-start | bytes 1572872 | tf_op jit(solution)/shard_map/ppermute | solution.py:64
  192.6 34.4 %collective-permute-start.12 = (bf16[256,2048]{1,0:T(8,128)(2,1)S(1)}, bf16[256,2048]{1,0:T(8,128)(2,1)S(1)}, u32[]{:S(2)}, u32[]{:S(2)}) collective-permute-start(bf16[256,2048]{1,0:T(8,128)(2,1)S(1)} %copy-done.3), channel_id=1, source_target_pairs={{0,1},{1,0},{2,3},{3,2},{4,5},{5,4},{6,7},{7,6},{8,9},{9,8},{10,11... | collective-permute-start | bytes 3145736 | tf_op jit(solution)/shard_map/ppermute | solution.py:64
  195.5 31.4 %collective-permute-start.11 = (bf16[128,2048]{1,0:T(8,128)(2,1)}, bf16[128,2048]{1,0:T(8,128)(2,1)S(1)}, u32[]{:S(2)}, u32[]{:S(2)}) collective-permute-start(bf16[128,2048]{1,0:T(8,128)(2,1)} %get-tuple-element.178), channel_id=1, source_target_pairs={{0,2},{1,3},{2,0},{3,1},{4,6},{5,7},{6,4},{7,5},{8,10},{9,11},{10,... | collective-permute-start | bytes 1572872 | tf_op jit(solution)/shard_map/ppermute | solution.py:64
  230.4 222.7 %all-gather.10.cloned.1.call-start = ((), (), s32[]{:S(2)}) async-start(), calls=%async_computation.2 | async-start | bytes 3133440 | tf_op jit(solution)/shard_map/all_gather | solution.py:924
  298.9 26.8 %collective-permute-start.13 = (bf16[256,2048]{1,0:T(8,128)(2,1)}, bf16[256,2048]{1,0:T(8,128)(2,1)}, u32[]{:S(2)}, u32[]{:S(2)}) collective-permute-start(bf16[256,2048]{1,0:T(8,128)(2,1)} %get-tuple-element.192), channel_id=1, source_target_pairs={{0,1},{1,0},{2,3},{3,2},{4,5},{5,4},{6,7},{7,6},{8,9},{9,8},{10,11... | collective-permute-start | bytes 3145736 | tf_op jit(solution)/shard_map/ppermute | solution.py:64
  335.5 26.8 %collective-permute-start.14 = (bf16[256,512]{1,0:T(8,128)(2,1)}, bf16[256,512]{1,0:T(8,128)(2,1)S(1)}, u32[]{:S(2)}, u32[]{:S(2)}) collective-permute-start(bf16[256,512]{1,0:T(8,128)(2,1)} %get-tuple-element.216), channel_id=1, source_target_pairs={{0,1},{1,0},{2,3},{3,2},{4,5},{5,4},{6,7},{7,6},{8,9},{9,8},{10,11... | collective-permute-start | bytes 786440 | tf_op jit(solution)/shard_map/ppermute | solution.py:64
  336.1 26.2 %collective-permute-start.15 = (bf16[256,512]{1,0:T(8,128)(2,1)}, bf16[256,512]{1,0:T(8,128)(2,1)S(1)}, u32[]{:S(2)}, u32[]{:S(2)}) collective-permute-start(bf16[256,512]{1,0:T(8,128)(2,1)} %get-tuple-element.217), channel_id=1, source_target_pairs={{0,2},{1,3},{2,0},{3,1},{4,6},{5,7},{6,4},{7,5},{8,10},{9,11},{10,... | collective-permute-start | bytes 786440 | tf_op jit(solution)/shard_map/ppermute | solution.py:64
  338.5 23.8 %collective-permute-start.16 = (bf16[256,512]{1,0:T(8,128)(2,1)}, bf16[256,512]{1,0:T(8,128)(2,1)}, u32[]{:S(2)}, u32[]{:S(2)}) collective-permute-start(bf16[256,512]{1,0:T(8,128)(2,1)} %get-tuple-element.218), channel_id=1, source_target_pairs={{0,3},{1,2},{2,1},{3,0},{4,7},{5,6},{6,5},{7,4},{8,11},{9,10},{10,... | collective-permute-start | bytes 786440 | tf_op jit(solution)/shard_map/ppermute | solution.py:64
  354.6 7.7 %collective-permute-start.17 = (bf16[16,7168]{1,0:T(8,128)(2,1)}, bf16[16,7168]{1,0:T(8,128)(2,1)S(1)}, u32[]{:S(2)}, u32[]{:S(2)}) collective-permute-start(bf16[16,7168]{1,0:T(8,128)(2,1)} %fusion.1), channel_id=1, source_target_pairs={{0,1},{1,0},{2,3},{3,2},{4,5},{5,4},{6,7},{7,6},{8,9},{9,8},{10,11... | collective-permute-start | bytes 688136 | tf_op jit(solution)/shard_map/ppermute | solution.py:64
  362.5 35.8 %collective-permute-start.19 = (bf16[256,2048]{1,0:T(8,128)(2,1)}, bf16[256,2048]{1,0:T(8,128)(2,1)S(1)}, u32[]{:S(2)}, u32[]{:S(2)}) collective-permute-start(bf16[256,2048]{1,0:T(8,128)(2,1)} %get-tuple-element.238), channel_id=1, source_target_pairs={{0,1},{1,0},{2,3},{3,2},{4,5},{5,4},{6,7},{7,6},{8,9},{9,8},{10,11... | collective-permute-start | bytes 3145736 | tf_op jit(solution)/shard_map/ppermute | solution.py:64
  363.1 35.3 %collective-permute-start.18 = (bf16[16,10752]{1,0:T(8,128)(2,1)S(1)}, bf16[16,10752]{1,0:T(8,128)(2,1)S(1)}, u32[]{:S(2)}, u32[]{:S(2)}) collective-permute-start(bf16[16,10752]{1,0:T(8,128)(2,1)S(1)} %pad_maximum_fusion.3), channel_id=1, source_target_pairs={{0,2},{1,3},{2,0},{3,1},{4,6},{5,7},{6,4},{7,5},{8,10},{9,11},{10,... | collective-permute-start | bytes 1032200 | tf_op jit(solution)/shard_map/ppermute | solution.py:64
  399.3 28.1 %collective-permute-start.20 = (bf16[256,2048]{1,0:T(8,128)(2,1)}, bf16[256,2048]{1,0:T(8,128)(2,1)}, u32[]{:S(2)}, u32[]{:S(2)}) collective-permute-start(bf16[256,2048]{1,0:T(8,128)(2,1)} %project_back.3), channel_id=1, source_target_pairs={{0,1},{1,0},{2,3},{3,2},{4,5},{5,4},{6,7},{7,6},{8,9},{9,8},{10,11... | collective-permute-start | bytes 3145736 | tf_op jit(solution)/shard_map/ppermute | solution.py:64
  408.1 19.3 %collective-permute-start.21 = (bf16[16,2048]{1,0:T(8,128)(2,1)S(1)}, bf16[16,2048]{1,0:T(8,128)(2,1)S(1)}, u32[]{:S(2)}, u32[]{:S(2)}) collective-permute-start(bf16[16,2048]{1,0:T(8,128)(2,1)S(1)} %convert_element_type.145), channel_id=1, source_target_pairs={{0,1},{1,0},{2,3},{3,2},{4,5},{5,4},{6,7},{7,6},{8,9},{9,8},{10,11... | collective-permute-start | bytes 196616 | tf_op jit(solution)/shard_map/ppermute | solution.py:64
  409.1 18.3 %collective-permute-start.22 = (bf16[16,2048]{1,0:T(8,128)(2,1)S(1)}, bf16[16,2048]{1,0:T(8,128)(2,1)S(1)}, u32[]{:S(2)}, u32[]{:S(2)}) collective-permute-start(bf16[16,2048]{1,0:T(8,128)(2,1)S(1)} %convert_element_type.145), channel_id=1, source_target_pairs={{0,2},{1,3},{2,0},{3,1},{4,6},{5,7},{6,4},{7,5},{8,10},{9,11},{10,... | collective-permute-start | bytes 196616 | tf_op jit(solution)/shard_map/ppermute | solution.py:64
  409.3 18.1 %collective-permute-start.23 = (bf16[16,2048]{1,0:T(8,128)(2,1)S(1)}, bf16[16,2048]{1,0:T(8,128)(2,1)S(1)}, u32[]{:S(2)}, u32[]{:S(2)}) collective-permute-start(bf16[16,2048]{1,0:T(8,128)(2,1)S(1)} %convert_element_type.145), channel_id=1, source_target_pairs={{0,3},{1,2},{2,1},{3,0},{4,7},{5,6},{6,5},{7,4},{8,11},{9,10},{10,... | collective-permute-start | bytes 196616 | tf_op jit(solution)/shard_map/ppermute | solution.py:64
  427.4 43.0 %collective-permute-start.24 = (bf16[256,2048]{1,0:T(8,128)(2,1)}, bf16[256,2048]{1,0:T(8,128)(2,1)S(1)}, u32[]{:S(2)}, u32[]{:S(2)}) collective-permute-start(bf16[256,2048]{1,0:T(8,128)(2,1)} %get-tuple-element.253), channel_id=1, source_target_pairs={{0,1},{1,0},{2,3},{3,2},{4,5},{5,4},{6,7},{7,6},{8,9},{9,8},{10,11... | collective-permute-start | bytes 3145736 | tf_op jit(solution)/shard_map/ppermute | solution.py:64
  429.4 46.0 %collective-permute-start.25 = (bf16[256,2048]{1,0:T(8,128)(2,1)S(1)}, bf16[256,2048]{1,0:T(8,128)(2,1)}, u32[]{:S(2)}, u32[]{:S(2)}) collective-permute-start(bf16[256,2048]{1,0:T(8,128)(2,1)S(1)} %add_convert_fusion), channel_id=1, source_target_pairs={{0,2},{1,3},{2,0},{3,1},{4,6},{5,7},{6,4},{7,5},{8,10},{9,11},{10,... | collective-permute-start | bytes 3145736 | tf_op jit(solution)/shard_map/ppermute | solution.py:64
  (43 other events, 353.9 us)
Sparse Core Ops, SparseCore 0:
  134.3 78.9 all-gather.7
  230.6 54.6 all-gather.5
  399.5 28.9 all-gather.9
